TPU v7x, 32 devices: a whole 2x2x4 slice. The times are simulated.
32 devices in a mesh: seq: 8 (over z, y), head: 4 (over x, core).
Axes of the slice: x: 2, y: 2, z: 4, core: 2. Of those that a mesh axis runs over, the one named last changes fastest.
Arguments:
- tokens: bfloat16 [1024, 1024], P('seq'), may hold values from -6 to 6
- cotangent: bfloat16 [1024, 1024], P('seq'), may hold values from -6 to 6
- gate_code: int32 [2, 1024, 8], P(None, 'seq', 'head'), may hold values from 0 to 723000
- beta_code: int32 [2, 1024, 8], P(None, 'seq', 'head'), may hold values from 256 to 1024
- norm1_gain: float32 [2, 1024], replicated, may hold values from 0.5 to 1.5
- weight_in: bfloat16 [2, 1024, 6144], P(None, None, 'head'), may hold values from -0.1875 to 0.1875
- conv_weight: bfloat16 [2, 4, 4096], P(None, None, 'head'), may hold values from -3 to 3
- out_gain: float32 [2, 256], replicated, may hold values from 0.5 to 1.5
- weight_out: bfloat16 [2, 2048, 1024], P(None, 'head'), may hold values from -0.25 to 0.25
- norm2_gain: float32 [2, 1024], replicated, may hold values from 0.5 to 1.5
- weight_gate: bfloat16 [2, 1024, 2816], P(None, None, 'head'), may hold values from -0.1875 to 0.1875
- weight_up: bfloat16 [2, 1024, 2816], P(None, None, 'head'), may hold values from -0.1875 to 0.1875
- weight_down: bfloat16 [2, 2816, 1024], P(None, 'head'), may hold values from -0.21875 to 0.21875
Outputs:
- activations: bfloat16 [1024, 1024], P('seq')
- input_grad: float32 [1024, 1024], P('seq')
- grad_norm1_gain: float32 [2, 1024], replicated
- grad_weight_in: float32 [2, 1024, 6144], P(None, 'seq', 'head')
- grad_conv_weight: float32 [2, 4, 4096], P(None, None, 'head')
- grad_out_gain: float32 [2, 256], replicated
- grad_weight_out: float32 [2, 2048, 1024], P(None, 'head', 'seq')
- grad_norm2_gain: float32 [2, 1024], replicated
- grad_weight_gate: float32 [2, 1024, 2816], P(None, 'seq', 'head')
- grad_weight_up: float32 [2, 1024, 2816], P(None, 'seq', 'head')
- grad_weight_down: float32 [2, 2816, 1024], P(None, 'head', 'seq')
All inputs are finite; a program needn't handle non-finite values.
Results may differ from a plain program's by a relative error of at most 0.02.
Values sent between devices are 32-bit elements; how exact they have to be, the bound alone decides.
No kernel may reach another device: no remote copies, remote signals or barrier semaphores. Data moves between devices by JAX's collectives and lax.ppermute only.
A program may use at most 256 MiB of HBM per device.

v0:
```python
import jax
import jax.numpy as jnp
from jax import lax
from jax.sharding import PartitionSpec as P

DK = 128
DV = 256
CONV = 4
SPAN = 64
STACK_LEVELS = 2


highest = lax.Precision.HIGHEST
norm_eps = 1e-06
gate_unit = 1.0 / 1048576.0
beta_unit = 1.0 / 1024.0


def from_behind(array, axis, by):
    length = lax.axis_size(axis)
    pairs = [(i, i + by) for i in range(length) if 0 <= i + by < length]
    return lax.ppermute(array, axis, pairs)


def rms_norm(stream, gain):
    return stream * lax.rsqrt(jnp.mean(stream * stream, axis=-1, keepdims=True) + norm_eps) * gain


def unit_rows(vectors):
    return vectors * lax.rsqrt(jnp.sum(vectors * vectors, axis=-1, keepdims=True) + norm_eps)


def swiglu(gate_pre, up_pre):
    return jax.nn.silu(gate_pre) * up_pre


def post_mix(outputs, gate_z, gain):
    return rms_norm(outputs, gain) * jax.nn.silu(gate_z)


def mixer_inputs(windowed, conv_taps):
    length_total = windowed.shape[0] - (CONV - 1)
    conv_out = conv_taps[0] * windowed[CONV - 1 :]
    for tap_index in range(1, CONV):
        conv_out = (
            conv_out
            + conv_taps[tap_index]
            * windowed[CONV - 1 - tap_index : CONV - 1 - tap_index + length_total]
        )
    active = jax.nn.silu(conv_out).reshape(length_total, -1, 2 * DK + DV)
    queries = unit_rows(active[:, :, :DK]) * DK ** (-0.5)
    keys_unit = unit_rows(active[:, :, DK : 2 * DK])
    return (queries, keys_unit, active[:, :, 2 * DK :])


def span_step(carry_state, pieces):
    queries, keys_unit, values_in, logdecay, beta_rate = pieces
    block_len = queries.shape[0]
    cumulated = jnp.cumsum(logdecay, axis=0)
    cum_heads = jnp.transpose(cumulated)
    row_index = lax.broadcasted_iota(jnp.int32, (1, block_len, block_len), 1)
    col_index = lax.broadcasted_iota(jnp.int32, (1, block_len, block_len), 2)
    inclusive = row_index >= col_index
    log_ratio = jnp.where(inclusive, cum_heads[:, :, None] - cum_heads[:, None, :], 0.0)
    decay_ratio = jnp.where(inclusive, jnp.exp(log_ratio), 0.0)
    beta_heads = jnp.transpose(beta_rate)
    key_key = jnp.einsum("thd,shd->hts", keys_unit, keys_unit, precision=highest)
    strict_lower = jnp.where(
        row_index > col_index, beta_heads[:, :, None] * decay_ratio * key_key, 0.0
    )
    system = strict_lower + jnp.eye(block_len, dtype=strict_lower.dtype)[None]
    decay_all = jnp.exp(cumulated)
    right_side = jnp.concatenate(
        [beta_rate[:, :, None] * values_in, (beta_rate * decay_all)[:, :, None] * keys_unit], axis=2
    )
    right_side = jnp.transpose(right_side, (1, 0, 2))
    solved_system = lax.linalg.triangular_solve(system, right_side, left_side=True, lower=True)
    val_width = values_in.shape[2]
    new_values = solved_system[:, :, :val_width] - jnp.einsum(
        "htd,hvd->htv", solved_system[:, :, val_width:], carry_state, precision=highest
    )
    query_key = jnp.einsum("thd,shd->hts", queries, keys_unit, precision=highest)
    mixing = decay_ratio * query_key
    outputs = jnp.transpose(decay_all)[:, :, None] * jnp.einsum(
        "thd,hvd->htv", queries, carry_state, precision=highest
    )
    outputs = outputs + jnp.einsum("hts,hsv->htv", mixing, new_values, precision=highest)
    to_end = jnp.exp(cumulated[-1][None, :] - cumulated)
    new_state = jnp.exp(cumulated[-1])[:, None, None] * carry_state
    new_state = new_state + jnp.einsum(
        "hsv,shd->hvd", new_values, to_end[:, :, None] * keys_unit, precision=highest
    )
    return (new_state, jnp.transpose(outputs, (1, 0, 2)))


def delta_rule(queries, keys_unit, values_in, logdecay, beta_rate, carry_state):
    length_total = queries.shape[0]
    block_count = length_total // SPAN

    def blocks(tensor):
        return tensor.reshape((block_count, SPAN) + tensor.shape[1:])

    final_state, outputs = lax.scan(
        span_step,
        carry_state,
        (
            blocks(queries),
            blocks(keys_unit),
            blocks(values_in),
            blocks(logdecay),
            blocks(beta_rate),
        ),
    )
    return (outputs.reshape((length_total,) + outputs.shape[2:]), final_state)


def state_prefix(transfer, offset):
    all_transfer, all_offset = (
        lax.all_gather(transfer, "seq", axis=0, tiled=True),
        lax.all_gather(offset, "seq", axis=0, tiled=True),
    )
    devices = lax.axis_size("seq")
    position = lax.axis_index("seq")
    transfer_kept = all_transfer.reshape((devices,) + transfer.shape)
    offsets_all = all_offset.reshape((devices,) + offset.shape)

    def advance(index_now, carry_state):
        moved = (
            jnp.einsum("hvj,hjk->hvk", carry_state, transfer_kept[index_now], precision=highest)
            + offsets_all[index_now]
        )
        return jnp.where(index_now < position, moved, carry_state)

    incoming = lax.fori_loop(0, devices, advance, jnp.zeros_like(offset))
    return (incoming, transfer_kept)


def state_back(transfer_kept, local_grad):
    all_grad = lax.all_gather(local_grad, "seq", axis=0, tiled=True)
    devices = lax.axis_size("seq")
    position = lax.axis_index("seq")
    grads_all = all_grad.reshape((devices,) + local_grad.shape)

    def retreat(step_index, carry_state):
        index_now = devices - 1 - step_index
        moved = (
            jnp.einsum("hvj,hkj->hvk", carry_state, transfer_kept[index_now], precision=highest)
            + grads_all[index_now]
        )
        return jnp.where(index_now > position, moved, carry_state)

    outgoing = lax.fori_loop(0, devices, retreat, jnp.zeros_like(local_grad))
    return outgoing


def head_total(partial_sum):
    share = lax.psum_scatter(partial_sum, "head", scatter_dimension=1, tiled=True)
    return lax.all_gather(share, "head", axis=1, tiled=True)


def layer_forward(stream, logdecay, beta_rate, weights):
    (
        gain_one,
        weight_in,
        conv_weight,
        out_gain,
        weight_out,
        gain_two,
        weight_gate,
        weight_up,
        weight_down,
    ) = weights
    length_total = stream.shape[0]
    normed = rms_norm(stream, gain_one).astype(jnp.bfloat16)
    projected = jnp.dot(normed, weight_in, preferred_element_type=jnp.float32).reshape(
        length_total, -1, 2 * DK + 2 * DV
    )
    head_count = projected.shape[1]
    conv_input = projected[:, :, : 2 * DK + DV].reshape(length_total, -1)
    gate_z = projected[:, :, 2 * DK + DV :]
    before = from_behind(conv_input[length_total - (CONV - 1) :], "seq", 1)
    windowed = jnp.concatenate([before, conv_input], axis=0)
    conv_taps = conv_weight.astype(jnp.float32)
    queries, keys_unit, values_in = mixer_inputs(windowed, conv_taps)
    wide_values = jnp.concatenate(
        [values_in, jnp.zeros((length_total, head_count, DK), jnp.float32)], axis=2
    )
    start_state = jnp.concatenate(
        [
            jnp.zeros((head_count, DV, DK), jnp.float32),
            jnp.broadcast_to(jnp.eye(DK, dtype=jnp.float32), (head_count, DK, DK)),
        ],
        axis=1,
    )
    wide_out, wide_end = delta_rule(
        queries, keys_unit, wide_values, logdecay, beta_rate, start_state
    )
    carried = wide_out[:, :, DV:]
    incoming, transfer_kept = state_prefix(wide_end[:, DV:], wide_end[:, :DV])
    outputs = wide_out[:, :, :DV] + jnp.einsum("thd,hvd->thv", carried, incoming, precision=highest)
    gated_out = post_mix(outputs, gate_z, out_gain).reshape(length_total, -1).astype(jnp.bfloat16)
    stream_mid = stream + head_total(
        jnp.dot(gated_out, weight_out, preferred_element_type=jnp.float32)
    )
    second_normed = rms_norm(stream_mid, gain_two).astype(jnp.bfloat16)
    gate_pre = jnp.dot(second_normed, weight_gate, preferred_element_type=jnp.float32)
    up_pre = jnp.dot(second_normed, weight_up, preferred_element_type=jnp.float32)
    hidden = swiglu(gate_pre, up_pre).astype(jnp.bfloat16)
    stream_next = stream_mid + head_total(
        jnp.dot(hidden, weight_down, preferred_element_type=jnp.float32)
    )
    stored = (
        stream,
        normed,
        windowed,
        conv_taps,
        gate_z,
        queries,
        keys_unit,
        values_in,
        outputs,
        carried,
        incoming,
        transfer_kept,
        gated_out,
        stream_mid,
        second_normed,
        gate_pre,
        up_pre,
        hidden,
    )
    return (stream_next, stored)


def layer_backward(grad_stream, logdecay, beta_rate, weights, stored):
    (
        gain_one,
        weight_in,
        conv_weight,
        out_gain,
        weight_out,
        gain_two,
        weight_gate,
        weight_up,
        weight_down,
    ) = weights
    (
        stream,
        normed,
        windowed,
        conv_taps,
        gate_z,
        queries,
        keys_unit,
        values_in,
        outputs,
        carried,
        incoming,
        transfer_kept,
        gated_out,
        stream_mid,
        second_normed,
        gate_pre,
        up_pre,
        hidden,
    ) = stored
    length_total = grad_stream.shape[0]
    back_bf = grad_stream.astype(jnp.bfloat16)
    grad_down = jnp.dot(hidden.T, back_bf, preferred_element_type=jnp.float32)
    grad_hidden = jnp.dot(back_bf, weight_down.T, preferred_element_type=jnp.float32)
    _, act_pull = jax.vjp(swiglu, gate_pre, up_pre)
    grad_gate_pre, grad_up_pre = act_pull(grad_hidden)
    grad_gate_pre = grad_gate_pre.astype(jnp.bfloat16)
    grad_up_pre = grad_up_pre.astype(jnp.bfloat16)
    grad_gate = jnp.dot(second_normed.T, grad_gate_pre, preferred_element_type=jnp.float32)
    grad_up = jnp.dot(second_normed.T, grad_up_pre, preferred_element_type=jnp.float32)
    ffn_partial = jnp.dot(
        grad_gate_pre, weight_gate.T, preferred_element_type=jnp.float32
    ) + jnp.dot(grad_up_pre, weight_up.T, preferred_element_type=jnp.float32)
    grad_normed_two = lax.psum(ffn_partial, "head")
    _, norm_pull = jax.vjp(rms_norm, stream_mid, gain_two)
    grad_mid, grad_gain_two = norm_pull(grad_normed_two)
    grad_stream = grad_stream + grad_mid
    back_bf = grad_stream.astype(jnp.bfloat16)
    grad_out = jnp.dot(gated_out.T, back_bf, preferred_element_type=jnp.float32)
    grad_gated = jnp.dot(back_bf, weight_out.T, preferred_element_type=jnp.float32).reshape(
        length_total, -1, DV
    )
    _, post_pull = jax.vjp(post_mix, outputs, gate_z, out_gain)
    grad_outputs, grad_gate_z, gain_mid_part = post_pull(grad_gated)
    local_grad = jnp.einsum("thv,thd->hvd", grad_outputs, carried, precision=highest)
    outgoing = state_back(transfer_kept, local_grad)

    def core_rule(queries, keys_unit, values_in):
        return delta_rule(queries, keys_unit, values_in, logdecay, beta_rate, incoming)

    _, rule_pull = jax.vjp(core_rule, queries, keys_unit, values_in)
    grad_queries, grad_keys, grad_values = rule_pull((grad_outputs, outgoing))
    _, mix_pull = jax.vjp(mixer_inputs, windowed, conv_taps)
    grad_window, grad_conv = mix_pull((grad_queries, grad_keys, grad_values))
    from_next = from_behind(grad_window[: CONV - 1], "seq", -1)
    grad_conv_in = grad_window[CONV - 1 :] + jnp.pad(
        from_next, ((length_total - (CONV - 1), 0), (0, 0))
    )
    grad_proj = (
        jnp.concatenate([grad_conv_in.reshape(length_total, -1, 2 * DK + DV), grad_gate_z], axis=2)
        .reshape(length_total, -1)
        .astype(jnp.bfloat16)
    )
    grad_in = jnp.dot(normed.T, grad_proj, preferred_element_type=jnp.float32)
    mixer_partial = jnp.dot(grad_proj, weight_in.T, preferred_element_type=jnp.float32)
    grad_normed, grad_out_gain = lax.psum((mixer_partial, gain_mid_part), "head")
    _, norm_pull = jax.vjp(rms_norm, stream, gain_one)
    grad_prev, grad_gain_one = norm_pull(grad_normed)
    return (
        grad_stream + grad_prev,
        (
            grad_gain_one,
            grad_in,
            grad_conv,
            grad_out_gain,
            grad_out,
            grad_gain_two,
            grad_gate,
            grad_up,
            grad_down,
        ),
    )


def body(
    tokens,
    cotangent,
    gate_code,
    beta_code,
    norm1_gain,
    weight_in,
    conv_weight,
    out_gain,
    weight_out,
    norm2_gain,
    weight_gate,
    weight_up,
    weight_down,
):
    logdecay = -gate_code.astype(jnp.float32) * gate_unit
    beta_rate = beta_code.astype(jnp.float32) * beta_unit
    everything = (
        norm1_gain,
        weight_in,
        conv_weight,
        out_gain,
        weight_out,
        norm2_gain,
        weight_gate,
        weight_up,
        weight_down,
    )
    stream = tokens.astype(jnp.float32)
    kept_layers = []
    for layer_idx in range(STACK_LEVELS):
        weights = tuple((tensor[layer_idx] for tensor in everything))
        stream, stored = layer_forward(stream, logdecay[layer_idx], beta_rate[layer_idx], weights)
        kept_layers.append((weights, stored))
    activations = stream.astype(jnp.bfloat16)
    grad_stream = cotangent.astype(jnp.float32)
    large_grads = []
    small_grads = []
    for layer_idx in reversed(range(STACK_LEVELS)):
        weights, stored = kept_layers[layer_idx]
        grad_stream, layer_part = layer_backward(
            grad_stream, logdecay[layer_idx], beta_rate[layer_idx], weights, stored
        )
        large_part = (layer_part[1], layer_part[4], layer_part[6], layer_part[7], layer_part[8])
        large_grads.insert(0, large_part)
        small_grads.insert(0, (layer_part[2], layer_part[0], layer_part[3], layer_part[5]))
    large_stack = tuple(
        (
            jnp.stack([grad_group[slot_index] for grad_group in large_grads])
            for slot_index in range(5)
        )
    )
    large_stack = (
        lax.psum_scatter(large_stack[0], "seq", scatter_dimension=1, tiled=True),
        lax.psum_scatter(large_stack[1], "seq", scatter_dimension=2, tiled=True),
        lax.psum_scatter(large_stack[2], "seq", scatter_dimension=1, tiled=True),
        lax.psum_scatter(large_stack[3], "seq", scatter_dimension=1, tiled=True),
        lax.psum_scatter(large_stack[4], "seq", scatter_dimension=2, tiled=True),
    )
    small_stack = tuple(
        (
            jnp.stack([grad_group[slot_index] for grad_group in small_grads])
            for slot_index in range(4)
        )
    )
    conv_grad, gain_one_grad, out_gain_grad, gain_two_grad = lax.psum(
        (small_stack[0], small_stack[1], small_stack[2], small_stack[3]), "seq"
    )
    return (
        activations,
        grad_stream,
        gain_one_grad,
        large_stack[0],
        conv_grad,
        out_gain_grad,
        large_stack[1],
        gain_two_grad,
        large_stack[2],
        large_stack[3],
        large_stack[4],
    )


def solution(mesh):
    in_specs = (
        P("seq", None),
        P("seq", None),
        P(None, "seq", "head"),
        P(None, "seq", "head"),
        P(),
        P(None, None, "head"),
        P(None, None, "head"),
        P(),
        P(None, "head", None),
        P(),
        P(None, None, "head"),
        P(None, None, "head"),
        P(None, "head", None),
    )
    out_specs = (
        P("seq", None),
        P("seq", None),
        P(),
        P(None, "seq", "head"),
        P(None, None, "head"),
        P(),
        P(None, "head", "seq"),
        P(),
        P(None, "seq", "head"),
        P(None, "seq", "head"),
        P(None, "head", "seq"),
    )
    return jax.shard_map(body, mesh=mesh, in_specs=in_specs, out_specs=out_specs, check_vma=False)
```

profile of v0, /device:TPU:0, one launch (start us, length us, event | category | flops | bytes accessed | tf_op | source)
XLA Modules:
  0.0 1594.9 jit_solution(10691709195272504350)
XLA Ops:
  41.2 28.4 %while.210 = (s32[]{:T(128)}, f32[2,384,128]{2,1,0:T(8,128)S(1)}, f32[2,64,2,384]{3,1,0,2:T(8,128)S(1)}, f32[2,64,2]{1,2,0:T(2,128)S(1)}, f32[2,64,2]{1,2,0:T(2,...) while((s32[]{:T(128)}, f32[2,384,128]{2,1,0:T(8,128)S(1)}, ...), condition=%wide.region_5.7_spmd, body=%wide.region_3.6_spmd.sunk | while | flops 340353152 | bytes 4627117 | solution.py:103
  71.3 41.7 %all-gather.7.cloned.1.call-done = f32[16,128,128]{2,1,0:T(8,128)} async-done(((f32[2,128,128]{2,1,0:T(8,128)}), f32[16,128,128]{2,1,0:T(8,128)}) %all-gather.7.cloned.1.call-update) | async-done | bytes 1048592 | tf_op jit(solution)/shard_map/all_gather | solution.py:119
  113.0 50.5 %all-gather.9.cloned.1.call-done = f32[16,256,128]{2,1,0:T(8,128)} async-done(((f32[2,256,128]{2,1,0:T(8,128)}), f32[16,256,128]{2,1,0:T(8,128)}) %all-gather.9.cloned.1.call-update) | async-done | bytes 2097168 | tf_op jit(solution)/shard_map/all_gather | solution.py:120
  163.5 20.1 %while.216 = (s32[]{:T(128)}, f32[2,256,128]{1,2,0:T(8,128)S(1)}, s32[]{:T(128)}, f32[8,2,128,128]{3,2,1,0:T(8,128)}, f32[8,2,256,128]{3,2,1,0:T(8,128)}, /*index=5*/s32[]{:T(128)}, s32[]{:T(128)}) while((s32[]{:T(128)}, f32[2,256,128]{1,2,0:T(8,128)S(1)}, s32[]{:T(128)}, f32[8,2,128,128]{3,2,1,0:T(8,128)}, ...), condition=%wide.region_7.9_spmd.clone, body=%wide.region_6.8_spmd.clone.sunk | while | flops 100925440 | bytes 2754667 | solution.py:134
  187.0 20.2 %reduce-scatter.10.cloned.1.call-done = f32[128,256]{1,0:T(8,128)} async-done(((f32[128,1024]{1,0:T(8,128)}), f32[128,256]{1,0:T(8,128)}) %reduce-scatter.10.cloned.1.call-update) | async-done | bytes 131088 | tf_op jit(solution)/shard_map/reduce_scatter | solution.py:157
  275.9 30.3 %while.211 = (s32[]{:T(128)}, f32[2,384,128]{2,1,0:T(8,128)S(1)}, f32[2,64,2,384]{3,1,0,2:T(8,128)S(1)}, f32[2,64,2]{1,2,0:T(2,128)S(1)}, f32[2,64,2]{1,2,0:T(2,...) while((s32[]{:T(128)}, f32[2,384,128]{2,1,0:T(8,128)S(1)}, ...), condition=%wide.region_17.19_spmd, body=%wide.region_15.18_spmd.sunk | while | flops 340353152 | bytes 4627117 | solution.py:103
  307.8 41.1 %all-gather.11.cloned.1.call-done = f32[16,128,128]{2,1,0:T(8,128)} async-done(((f32[2,128,128]{2,1,0:T(8,128)}), f32[16,128,128]{2,1,0:T(8,128)}) %all-gather.11.cloned.1.call-update) | async-done | bytes 1048592 | tf_op jit(solution)/shard_map/all_gather | solution.py:119
  348.9 50.4 %all-gather.13.cloned.1.call-done = f32[16,256,128]{2,1,0:T(8,128)} async-done(((f32[2,256,128]{2,1,0:T(8,128)}), f32[16,256,128]{2,1,0:T(8,128)}) %all-gather.13.cloned.1.call-update) | async-done | bytes 2097168 | tf_op jit(solution)/shard_map/all_gather | solution.py:120
  399.3 20.0 %while.217 = (s32[]{:T(128)}, f32[2,256,128]{1,2,0:T(8,128)S(1)}, s32[]{:T(128)}, f32[8,2,128,128]{3,2,1,0:T(8,128)}, f32[8,2,256,128]{3,2,1,0:T(8,128)}, /*index=5*/s32[]{:T(128)}, s32[]{:T(128)}) while((s32[]{:T(128)}, f32[2,256,128]{1,2,0:T(8,128)S(1)}, s32[]{:T(128)}, f32[8,2,128,128]{3,2,1,0:T(8,128)}, ...), condition=%wide.region_19.21_spmd.clone, body=%wide.region_18.20_spmd.clone.sunk | while | flops 100925440 | bytes 2754667 | solution.py:134
  462.5 28.1 %all-reduce.38.cloned.1.call-done = f32[128,1024]{1,0:T(8,128)} async-done(((f32[128,1024]{1,0:T(8,128)}), f32[128,1024]{1,0:T(8,128)}) %all-reduce.38.cloned.1.call-update) | async-done | bytes 524304 | tf_op jit(solution)/shard_map/psum | solution.py:280
  492.4 23.1 %reduce-scatter.16.cloned.1.call-done = f32[128,256]{1,0:T(8,128)} async-done(((f32[128,1024]{1,0:T(8,128)}), f32[128,256]{1,0:T(8,128)}) %reduce-scatter.16.cloned.1.call-update) | async-done | bytes 131088 | tf_op jit(solution)/shard_map/reduce_scatter | solution.py:157
  535.7 39.1 %while.214 = (s32[]{:T(128)}, f32[2,256,128]{2,1,0:T(8,128)S(1)}, f32[2,2,64,64]{3,2,1,0:T(8,128)}, f32[2,64,2,1]{1,2,3,0:T(2,128)S(1)}, f32[2,64,2,1]{1,2,3,0:T...) while((s32[]{:T(128)}, f32[2,256,128]{2,1,0:T(8,128)S(1)}, ...), condition=%wide.region_31.34_spmd.clone.clone, body=%wide.region_29.33_spmd.clone.clone.sunk | while | flops 164024704 | bytes 3933053 | solution.py:103
  579.9 32.3 %while.218 = (s32[]{:T(128)}, f32[2,256,128]{1,2,0:T(8,128)}, s32[]{:T(128)}, f32[8,2,128,128]{3,2,1,0:T(8,128)}, f32[8,2,256,128]{3,2,1,0:T(8,128)}, /*index=5*/s32[]{:T(128)}, s32[]{:T(128)}, s32[]{:T(128)}, s32[]{:T(128)}) while((s32[]{:T(128)}, f32[2,256,128]{1,2,0:T(8,128)}, s32[]{:T(128)}, f32[8,2,128,128]{3,2,1,0:T(8,128)}, ...), condition=%wide.region_28.30_spmd.clone, body=%wide.region_27.29_spmd.clone.sunk | while | flops 100925448 | bytes 2754729 | solution.py:152
  615.2 43.8 %while.212 = (s32[]{:T(128)}, f32[2,256,128]{2,1,0:T(8,128)S(1)}, f32[2,64,2,128]{3,1,0,2:T(8,128)}, f32[2,64,2,128]{3,1,0,2:T(8,128)}, f32[2,64,2,256]{3,1,0,2:...) while((s32[]{:T(128)}, f32[2,256,128]{2,1,0:T(8,128)S(1)}, ...), condition=%wide.region_33.38_spmd.clone, body=%wide.region_32.37_spmd.clone.sunk | while | flops 485101568 | bytes 11272125 | solution.py:103
  690.9 33.6 %all-reduce.40.cloned.1.call-done = f32[128,1024]{1,0:T(8,128)} async-done(((f32[128,1024]{1,0:T(8,128)}), f32[128,1024]{1,0:T(8,128)}) %all-reduce.40.cloned.1.call-update) | async-done | bytes 524304 | tf_op jit(solution)/shard_map/psum | solution.py:312
  731.5 33.5 %all-reduce.42.cloned.1.call-done = f32[128,1024]{1,0:T(8,128)} async-done(((f32[128,1024]{1,0:T(8,128)}), f32[128,1024]{1,0:T(8,128)}) %all-reduce.42.cloned.1.call-update) | async-done | bytes 524304 | tf_op jit(solution)/shard_map/psum | solution.py:280
  775.5 33.5 %while.215 = (s32[]{:T(128)}, f32[2,256,128]{2,1,0:T(8,128)S(1)}, f32[2,2,64,64]{3,2,1,0:T(8,128)S(1)}, f32[2,64,2,1]{1,2,3,0:T(2,128)S(1)}, f32[2,64,2,1]{1,2,3...) while((s32[]{:T(128)}, f32[2,256,128]{2,1,0:T(8,128)S(1)}, ...), condition=%wide.region_45.50_spmd.clone.clone, body=%wide.region_43.49_spmd.clone.clone.sunk | while | flops 164024704 | bytes 3990809 | solution.py:103
  843.7 35.4 %while.213 = (s32[]{:T(128)}, f32[2,256,128]{2,1,0:T(8,128)S(1)}, f32[2,64,2,128]{3,1,0,2:T(8,128)S(1)}, f32[2,64,2,128]{3,1,0,2:T(8,128)S(1)}, f32[2,64,2,256]{...) while((s32[]{:T(128)}, f32[2,256,128]{2,1,0:T(8,128)S(1)}, ...), condition=%wide.region_47.52_spmd.clone, body=%wide.region_46.51_spmd.clone.sunk | while | flops 485101568 | bytes 8618345 | solution.py:103
  945.9 38.6 %all-reduce.31 = (f32[2,1024]{1,0:T(2,128)}, f32[2,4,1024]{2,1,0:T(4,128)}, f32[2,256]{1,0:T(2,128)}, f32[2,1024]{1,0:T(2,128)}) all-reduce(f32[2,1024]{1,0:T(2,128)S(1)} %pad_maximum_fusion.8, f32[2,4,1024]{2,1,0:T(4,128)S(1)} %pad_maximum_fusion.7, ...), channel_id=1, replica_groups=mesh['seq'=8,'head'=4] {'seq'}, use_global_device_ids=true, to_apply=%region_54.59 | all-reduce | flops 12800 | bytes 102400 | tf_op jit(solution)/shard_map/psum | solution.py:396
  986.5 46.7 %reduce-scatter.20.cloned.1.call-done = f32[2,512,128]{2,1,0:T(8,128)} async-done(((f32[2,512,1024]{2,1,0:T(8,128)}), f32[2,512,128]{2,1,0:T(8,128)}) %reduce-scatter.20.cloned.1.call-update) | async-done | bytes 524304 | tf_op jit(solution)/shard_map/reduce_scatter | solution.py:385
  1033.2 114.8 %reduce-scatter.26.cloned.1.call-done = f32[2,704,128]{2,1,0:T(8,128)} async-done(((f32[2,704,1024]{2,1,0:T(8,128)}), f32[2,704,128]{2,1,0:T(8,128)}) %reduce-scatter.26.cloned.1.call-update) | async-done | bytes 720912 | tf_op jit(solution)/shard_map/reduce_scatter | solution.py:388
  1148.0 114.5 %reduce-scatter.22.cloned.1.call-done = f32[2,128,704]{1,2,0:T(8,128)} async-done(((f32[2,1024,704]{1,2,0:T(8,128)}), f32[2,128,704]{1,2,0:T(8,128)}) %reduce-scatter.22.cloned.1.call-update) | async-done | bytes 720912 | tf_op jit(solution)/shard_map/reduce_scatter | solution.py:386
  1262.5 114.5 %reduce-scatter.24.cloned.1.call-done = f32[2,128,704]{1,2,0:T(8,128)} async-done(((f32[2,1024,704]{1,2,0:T(8,128)}), f32[2,128,704]{1,2,0:T(8,128)}) %reduce-scatter.24.cloned.1.call-update) | async-done | bytes 720912 | tf_op jit(solution)/shard_map/reduce_scatter | solution.py:387
  1377.0 211.0 %reduce-scatter.18.cloned.1.call-done = f32[2,128,1536]{2,1,0:T(8,128)} async-done(((f32[2,1024,1536]{2,1,0:T(8,128)}), f32[2,128,1536]{2,1,0:T(8,128)}) %reduce-scatter.18.cloned.1.call-update) | async-done | bytes 1572880 | tf_op jit(solution)/shard_map/reduce_scatter | solution.py:384
  (1079 shorter events, 632.4 us)
Async XLA Ops:
  7.2 105.8 %all-gather.7.cloned.1.call-start = ((), (), s32[]{:S(2)}) async-start(), calls=%async_computation.9 | async-start | bytes 1179648 | tf_op jit(solution)/shard_map/all_gather | solution.py:119
  20.6 16.1 %collective-permute-start = (f32[3,1024]{0,1:T(8,128)S(1)}, f32[3,1024]{0,1:T(8,128)S(1)}, u32[]{:S(2)}, u32[]{:S(2)}) collective-permute-start(f32[3,1024]{0,1:T(8,128)S(1)} %copy.512), channel_id=1, source_target_pairs={{0,4},{4,8},{8,12},{12,16},{16,20},{20,24},{24,28},{1,5},{5,9},{9,... | collective-permute-start | bytes 36872 | tf_op jit(solution)/shard_map/ppermute | solution.py:22
  70.4 93.2 %all-gather.9.cloned.1.call-start = ((), (), s32[]{:S(2)}) async-start(), calls=%async_computation.10 | async-start | bytes 2359296 | tf_op jit(solution)/shard_map/all_gather | solution.py:120
  71.1 136.0 %reduce-scatter.10.cloned.1.call-start = ((), (), s32[]{:S(2)}) async-start(), calls=%async_computation.11 | async-start | bytes 655360 | tf_op jit(solution)/shard_map/reduce_scatter | solution.py:157
  186.9 54.5 %reduce-scatter.12.cloned.1.call-start = ((), (), s32[]{:S(2)}) async-start(), calls=%async_computation.12 | async-start | bytes 655360 | tf_op jit(solution)/shard_map/reduce_scatter | solution.py:157
  219.1 129.8 %all-gather.11.cloned.1.call-start = ((), (), s32[]{:S(2)}) async-start(), calls=%async_computation.13 | async-start | bytes 1179648 | tf_op jit(solution)/shard_map/all_gather | solution.py:119
  248.6 477.8 %copy-start = (f32[128,1024]{1,0:T(8,128)}, f32[128,1024]{1,0:T(8,128)S(1)}, u32[]{:S(2)}) copy-start(f32[128,1024]{1,0:T(8,128)S(1)} %get-tuple-element.3414) | copy-start | bytes 1572868
  254.3 15.4 collective-permute-start.1
  306.9 92.4 %all-gather.13.cloned.1.call-start = ((), (), s32[]{:S(2)}) async-start(), calls=%async_computation.14 | async-start | bytes 2359296 | tf_op jit(solution)/shard_map/all_gather | solution.py:120
  307.7 136.2 %reduce-scatter.14.cloned.1.call-start = ((), (), s32[]{:S(2)}) async-start(), calls=%async_computation.15 | async-start | bytes 655360 | tf_op jit(solution)/shard_map/reduce_scatter | solution.py:157
  423.6 67.0 %all-reduce.38.cloned.1.call-start = ((), (), s32[]{:S(2)}) async-start(), calls=%async_computation.17 | async-start | bytes 1048576 | tf_op jit(solution)/shard_map/psum | solution.py:280
  456.5 58.9 %reduce-scatter.16.cloned.1.call-start = ((), (), s32[]{:S(2)}) async-start(), calls=%async_computation.16 | async-start | bytes 655360 | tf_op jit(solution)/shard_map/reduce_scatter | solution.py:157
  459.2 120.6 %all-gather.15.cloned.1.call-start = ((), (), s32[]{:S(2)}) async-start(), calls=%async_computation.18 | async-start | bytes 2359296 | tf_op jit(solution)/shard_map/all_gather | solution.py:139
  529.6 194.8 %all-reduce.40.cloned.1.call-start = ((), (), s32[]{:S(2)}) async-start(), calls=%async_computation.19 | async-start | bytes 1048576 | tf_op jit(solution)/shard_map/psum | solution.py:312
  671.4 14.3 collective-permute-start.2
  690.8 74.1 %all-reduce.42.cloned.1.call-start = ((), (), s32[]{:S(2)}) async-start(), calls=%async_computation.20 | async-start | bytes 1048576 | tf_op jit(solution)/shard_map/psum | solution.py:280
  731.3 91.8 %all-gather.17.cloned.1.call-start = ((), (), s32[]{:S(2)}) async-start(), calls=%async_computation.21 | async-start | bytes 2359296 | tf_op jit(solution)/shard_map/all_gather | solution.py:139
  773.3 171.3 %all-reduce.44.cloned.1.call-start = ((), (), s32[]{:S(2)}) async-start(), calls=%async_computation.22 | async-start | bytes 1048576 | tf_op jit(solution)/shard_map/psum | solution.py:312
  884.7 14.0 collective-permute-start.3
  904.8 128.5 %reduce-scatter.20.cloned.1.call-start = ((), (), s32[]{:S(2)}) async-start(), calls=%async_computation.24 | async-start | bytes 4718592 | tf_op jit(solution)/shard_map/reduce_scatter | solution.py:385
  907.6 240.4 %reduce-scatter.26.cloned.1.call-start = ((), (), s32[]{:S(2)}) async-start(), calls=%async_computation.27 | async-start | bytes 6488064 | tf_op jit(solution)/shard_map/reduce_scatter | solution.py:388
  912.7 349.8 %reduce-scatter.22.cloned.1.call-start = ((), (), s32[]{:S(2)}) async-start(), calls=%async_computation.25 | async-start | bytes 6488064 | tf_op jit(solution)/shard_map/reduce_scatter | solution.py:386
  917.8 459.2 %reduce-scatter.24.cloned.1.call-start = ((), (), s32[]{:S(2)}) async-start(), calls=%async_computation.26 | async-start | bytes 6488064 | tf_op jit(solution)/shard_map/reduce_scatter | solution.py:387
  922.8 665.1 %reduce-scatter.18.cloned.1.call-start = ((), (), s32[]{:S(2)}) async-start(), calls=%async_computation.23 | async-start | bytes 14155776 | tf_op jit(solution)/shard_map/reduce_scatter | solution.py:384
  (188 other events, 4190.7 us)
Sparse Core Ops, SparseCore 0:
  70.5 42.4 all-gather.6
  115.7 47.7 all-gather.8
  187.0 20.1 reduce-scatter.9
  219.2 22.1 reduce-scatter.11
  307.1 41.8 all-gather.10
  351.5 47.7 all-gather.12
  423.7 20.1 reduce-scatter.13
  456.6 33.9 all-reduce.37
  493.7 21.7 reduce-scatter.15
  529.8 50.0 all-gather.14
  690.9 33.4 all-reduce.39
  731.4 33.4 all-reduce.41
  773.4 49.6 all-gather.16
  904.9 34.1 all-reduce.43
  943.2 90.0 reduce-scatter.19
  1037.3 110.6 reduce-scatter.25
  1152.1 110.3 reduce-scatter.21
  1266.6 110.3 reduce-scatter.23
  1381.2 206.7 reduce-scatter.17
where the time goes:
time: 1610 us; the launch traced here: 1590 us
  waiting for transfers between devices  1020 us (63%)
  other arithmetic  197 us (12%)
  matrix products  162 us (10%)
  local copies, waits for them, and re-layouts  107 us (7%)
  blocking collectives  72.1 us (4%)
  between operations  16.9 us (1%)
    reduce_scatter x1, waiting for transfers between devices, body(): lax.psum_scatter(large_stack[0], 'seq', scatter_dimension=1, tiled=True)  211 us
    another operation x32, other arithmetic, span_step(): lax.linalg.triangular_solve(system, right_side, left_side=True, lower=True)  122 us
    reduce_scatter x1, waiting for transfers between devices, body(): lax.psum_scatter(large_stack[4], 'seq', scatter_dimension=2, tiled=True)  115 us
    reduce_scatter x1, waiting for transfers between devices, body(): lax.psum_scatter(large_stack[3], 'seq', scatter_dimension=1, tiled=True)  115 us
    reduce_scatter x1, waiting for transfers between devices, body(): lax.psum_scatter(large_stack[2], 'seq', scatter_dimension=1, tiled=True)  114 us
    all_gather x2, waiting for transfers between devices, state_prefix(): lax.all_gather(offset, 'seq', axis=0, tiled=True)  101 us
    all_gather x2, waiting for transfers between devices, state_prefix(): lax.all_gather(transfer, 'seq', axis=0, tiled=True)  82.9 us
    reduce_scatter x4, waiting for transfers between devices, head_total(): lax.psum_scatter(partial_sum, 'head', scatter_dimension=1, tiled=True)  78.4 us
  transfers between devices with their start and end apart: 23, of which 22 were waited for; matrix products, arithmetic and copies ran while one was open for 8% of the time, Pallas kernels for 0%

commit v1 on v0

v1 whole, which is shorter than its diff:
```python
import functools

import jax
import jax.numpy as jnp
from jax import lax
from jax.experimental import pallas as pl
from jax.experimental.pallas import tpu as pltpu
from jax.sharding import PartitionSpec as P

DK = 128
DV = 256
CONV = 4
STACK_LEVELS = 2
QKV = 2 * DK + DV
WIDE = 2 * DK + 2 * DV
HALF = DV // 2
PAD = 8

f32 = jnp.float32
bf16 = jnp.bfloat16
highest = lax.Precision.HIGHEST
norm_eps = 1e-06
gate_unit = 1.0 / 1048576.0
beta_unit = 1.0 / 1024.0


def shape_of(dims, dtype=f32):
    return jax.ShapeDtypeStruct(tuple(dims), dtype)


def call(body, outs, args, name, scratch=()):
    specs = []
    for arg in args:
        if arg.dtype == jnp.int32:
            specs.append(pl.BlockSpec(memory_space=pltpu.SMEM))
        else:
            specs.append(pl.BlockSpec(memory_space=pltpu.VMEM))
    return pl.pallas_call(
        body,
        out_shape=tuple(outs),
        in_specs=specs,
        out_specs=tuple(pl.BlockSpec(memory_space=pltpu.VMEM) for _ in outs),
        scratch_shapes=list(scratch),
        name=name,
    )(*args)


def mm(a, b, ca, cb, precision=highest):
    return lax.dot_general(
        a, b, (((ca,), (cb,)), ((), ())), precision=precision, preferred_element_type=f32
    )


def mmb(a, b, ca, cb):
    return lax.dot_general(
        a.astype(bf16), b.astype(bf16), (((ca,), (cb,)), ((), ())), preferred_element_type=f32
    )


def sigmoid(u):
    return 1.0 / (1.0 + jnp.exp(-u))


def norm_forward(x, gain):
    return x * lax.rsqrt(jnp.mean(x * x, axis=-1, keepdims=True) + norm_eps) * gain


def norm_backward(x, gain, grad):
    rate = lax.rsqrt(jnp.mean(x * x, axis=-1, keepdims=True) + norm_eps)
    unit = x * rate
    grad_gain = jnp.sum(grad * unit, axis=0, keepdims=True)
    scaled = grad * gain
    grad_x = rate * (scaled - unit * jnp.mean(scaled * unit, axis=-1, keepdims=True))
    return grad_x, grad_gain


def in_kernel(stream_ref, gain_ref, w_ref, normed_ref, proj_ref):
    normed = norm_forward(stream_ref[...], gain_ref[...]).astype(bf16)
    normed_ref[...] = normed
    proj_ref[...] = mmb(normed, w_ref[...], 1, 0)


def in_sum_kernel(mid_ref, total_ref, gain_ref, w_ref, stream_ref, normed_ref, proj_ref):
    stream = mid_ref[...] + total_ref[...]
    stream_ref[...] = stream
    normed = norm_forward(stream, gain_ref[...]).astype(bf16)
    normed_ref[...] = normed
    proj_ref[...] = mmb(normed, w_ref[...], 1, 0)


def conv_of(win_ref, taps, length):
    conv = taps[0:1] * win_ref[pl.ds(PAD, length), :]
    for tap in range(1, CONV):
        conv = conv + taps[tap : tap + 1] * win_ref[pl.ds(PAD - tap, length), :]
    return conv


def decay_of(col, row, length):
    rows = lax.broadcasted_iota(jnp.int32, (length, length), 0)
    cols = lax.broadcasted_iota(jnp.int32, (length, length), 1)
    keep = rows >= cols
    ratio = jnp.where(keep, jnp.exp(jnp.where(keep, col - row, 0.0)), 0.0)
    return rows, cols, ratio


def delta_kernel(
    y_ref, proj_ref, before_ref, taps_ref, col_ref, row_ref, beta_ref,
    ow_ref, uw_ref, solve_ref, mix_ref, send_ref, keep_ref, transfer_ref,
    win_ref, offset_ref,
):
    length = proj_ref.shape[0]
    for head in range(col_ref.shape[0]):
        base = head * WIDE
        win_ref[0:PAD, :] = before_ref[:, base : base + QKV]
        win_ref[pl.ds(PAD, length), :] = proj_ref[:, base : base + QKV]
        conv = conv_of(win_ref, taps_ref[:, head * QKV : (head + 1) * QKV].astype(f32), length)
        active = conv * sigmoid(conv)
        q_act = active[:, :DK]
        k_act = active[:, DK : 2 * DK]
        values = active[:, 2 * DK :]
        q = q_act * lax.rsqrt(jnp.sum(q_act * q_act, axis=-1, keepdims=True) + norm_eps)
        q = q * DK ** (-0.5)
        k = k_act * lax.rsqrt(jnp.sum(k_act * k_act, axis=-1, keepdims=True) + norm_eps)
        col = col_ref[head]
        row = row_ref[head]
        beta = beta_ref[head]
        rows, cols, ratio = decay_of(col, row, length)
        key_key = mm(k, k, 1, 1)
        query_key = mm(q, k, 1, 1)
        lower = jnp.where(rows > cols, beta * ratio * key_key, 0.0)
        solve = jnp.where(rows == cols, 1.0, 0.0)
        block = 1
        while block < length:
            here = (
                (rows // (2 * block) == cols // (2 * block))
                & (rows % (2 * block) >= block)
                & (cols % (2 * block) < block)
            )
            part = jnp.where(here, lower, 0.0)
            if block == 1:
                solve = solve - part
            else:
                solve = solve - mm(solve, mm(part, solve, 1, 0), 1, 0)
            block *= 2
        decay = jnp.exp(col)
        right = jnp.concatenate([beta * values, (beta * decay) * k], axis=1)
        uw = mm(solve, right, 1, 0)
        mix = ratio * query_key
        muw = mm(mix, uw, 1, 0)
        last = row[:, length - 1 :]
        ends = mm(uw, jnp.exp(last - col) * k, 0, 0)
        eye = jnp.where(
            lax.broadcasted_iota(jnp.int32, (DK, DK), 0)
            == lax.broadcasted_iota(jnp.int32, (DK, DK), 1),
            1.0,
            0.0,
        )
        transfer = jnp.exp(last) * eye - ends[DV:]
        offset_ref[...] = ends[:DV]
        ow_ref[head] = jnp.concatenate([muw[:, :DV], decay * q - muw[:, DV:]], axis=1)
        uw_ref[head] = uw
        solve_ref[head] = solve
        mix_ref[head] = mix
        transfer_ref[head] = transfer
        y = y_ref[0]
        send_ref[head, 0:DK, :] = transfer
        send_ref[head, DK : DK + HALF, :] = offset_ref[
            pl.ds(pl.multiple_of((1 - y) * HALF, HALF), HALF), :
        ]
        keep_ref[head] = offset_ref[pl.ds(pl.multiple_of(y * HALF, HALF), HALF), :]


def pair_kernel(
    y_ref, own_ref, keep_ref, other_ref,
    first_t_ref, second_t_ref, pair_t_ref, first_o_ref, pair_o_ref,
):
    lead = y_ref[0] == 0
    for head in range(own_ref.shape[0]):
        own, other = own_ref[head], other_ref[head, 0:DK, :]
        keep, far = keep_ref[head], other_ref[head, DK : DK + HALF, :]
        first_t, second_t = jnp.where(lead, own, other), jnp.where(lead, other, own)
        first_o, second_o = jnp.where(lead, keep, far), jnp.where(lead, far, keep)
        first_t_ref[head] = first_t
        second_t_ref[head] = second_t
        first_o_ref[head] = first_o
        both = mm(jnp.concatenate([first_t, first_o], axis=0), second_t, 1, 0)
        pair_t_ref[head] = both[:DK]
        pair_o_ref[head] = both[DK:] + second_o


def step_kernel(state_ref, transfer_ref, offset_ref, out_ref):
    for head in range(state_ref.shape[0]):
        out_ref[head] = mm(state_ref[head], transfer_ref[head], 1, 0) + offset_ref[head]


def step_back_kernel(state_ref, transfer_ref, offset_ref, out_ref):
    for head in range(state_ref.shape[0]):
        out_ref[head] = mm(state_ref[head], transfer_ref[head], 1, 1) + offset_ref[head]


def last_kernel(y_ref, state_ref, transfer_ref, offset_ref, mine_ref, other_ref):
    lead = y_ref[0] == 0
    for head in range(state_ref.shape[0]):
        state = state_ref[head]
        moved = mm(state, transfer_ref[head], 1, 0) + offset_ref[head]
        mine_ref[head] = jnp.where(lead, state, moved)
        other_ref[head] = jnp.where(lead, moved, state)


def pair_back_kernel(y_ref, keep_ref, other_ref, first_t_ref, second_ref, pair_ref):
    lead = y_ref[0] == 0
    for head in range(keep_ref.shape[0]):
        keep, far = keep_ref[head], other_ref[head]
        first, second = jnp.where(lead, keep, far), jnp.where(lead, far, keep)
        second_ref[head] = second
        pair_ref[head] = first + mm(second, first_t_ref[head], 1, 1)


def last_back_kernel(y_ref, state_ref, transfer_ref, offset_ref, mine_ref, other_ref):
    lead = y_ref[0] == 0
    for head in range(state_ref.shape[0]):
        state = state_ref[head]
        moved = mm(state, transfer_ref[head], 1, 1) + offset_ref[head]
        mine_ref[head] = jnp.where(lead, moved, state)
        other_ref[head] = jnp.where(lead, state, moved)


def halves(y, mine, other):
    lead = y == 0
    return jnp.concatenate(
        [jnp.where(lead, mine, other), jnp.where(lead, other, mine)], axis=0
    )


def out_kernel(
    y_ref, mine_ref, other_ref, ow_ref, proj_ref, gain_ref, w_ref,
    state_ref, outputs_ref, gated_ref, part_ref,
):
    pieces = []
    for head in range(ow_ref.shape[0]):
        state = halves(y_ref[0], mine_ref[head], other_ref[head])
        state_ref[head] = state
        ow = ow_ref[head]
        outputs = ow[:, :DV] + mm(ow[:, DV:], state, 1, 1)
        outputs_ref[:, head * DV : (head + 1) * DV] = outputs
        z = proj_ref[:, head * WIDE + QKV : (head + 1) * WIDE]
        pieces.append((norm_forward(outputs, gain_ref[...]) * (z * sigmoid(z))).astype(bf16))
    gated = jnp.concatenate(pieces, axis=1)
    gated_ref[...] = gated
    part_ref[...] = mmb(gated, w_ref[...], 1, 0)


def ffn_kernel(
    stream_ref, total_ref, gain_ref, wg_ref, wu_ref, wd_ref,
    mid_ref, normed_ref, gate_ref, up_ref, hidden_ref, part_ref,
):
    mid = stream_ref[...] + total_ref[...]
    mid_ref[...] = mid
    normed = norm_forward(mid, gain_ref[...]).astype(bf16)
    normed_ref[...] = normed
    gate = mmb(normed, wg_ref[...], 1, 0)
    up = mmb(normed, wu_ref[...], 1, 0)
    gate_ref[...] = gate
    up_ref[...] = up
    hidden = (gate * sigmoid(gate) * up).astype(bf16)
    hidden_ref[...] = hidden
    part_ref[...] = mmb(hidden, wd_ref[...], 1, 0)


def sum_kernel(mid_ref, total_ref, out_ref):
    out_ref[...] = (mid_ref[...] + total_ref[...]).astype(bf16)


def ffn_back_kernel(
    grad_ref, gate_ref, up_ref, wg_ref, wu_ref, wd_ref,
    back_ref, gg_ref, gu_ref, part_ref,
):
    back = grad_ref[...].astype(bf16)
    back_ref[...] = back.astype(f32)
    hidden = mmb(back, wd_ref[...], 1, 1)
    gate, up = gate_ref[...], up_ref[...]
    rate = sigmoid(gate)
    gu = (hidden * (gate * rate)).astype(bf16)
    gg = (hidden * up * (rate * (1.0 + gate * (1.0 - rate)))).astype(bf16)
    gg_ref[...] = gg.astype(f32)
    gu_ref[...] = gu.astype(f32)
    part_ref[...] = mmb(gg, wg_ref[...], 1, 1) + mmb(gu, wu_ref[...], 1, 1)


def out_back_kernel(
    y_ref, grad_ref, total_ref, mid_ref, gain_ref, w_ref, outputs_ref, proj_ref, out_gain_ref,
    ow_ref,
    next_ref, back_ref, do_ref, dz_ref, dgain_ref, dout_gain_ref, send_ref, keep_ref,
    local_ref,
):
    grad_mid, grad_gain = norm_backward(mid_ref[...], gain_ref[...], total_ref[...])
    dgain_ref[...] = grad_gain
    grad = grad_ref[...] + grad_mid
    next_ref[...] = grad
    back = grad.astype(bf16)
    back_ref[...] = back.astype(f32)
    gated = mmb(back, w_ref[...], 1, 1)
    gain = out_gain_ref[...]
    total_gain = jnp.zeros_like(gain)
    y = y_ref[0]
    for head in range(ow_ref.shape[0]):
        span = slice(head * DV, (head + 1) * DV)
        outputs = outputs_ref[:, span]
        z = proj_ref[:, head * WIDE + QKV : (head + 1) * WIDE]
        rate = sigmoid(z)
        grad_h = gated[:, span]
        grad_n = grad_h * (z * rate)
        dz_ref[:, span] = (
            grad_h * norm_forward(outputs, gain) * (rate * (1.0 + z * (1.0 - rate)))
        )
        grad_o, gain_part = norm_backward(outputs, gain, grad_n)
        total_gain = total_gain + gain_part
        do_ref[:, span] = grad_o
        local_ref[...] = mm(grad_o, ow_ref[head][:, DV:], 0, 0)
        send_ref[head] = local_ref[pl.ds(pl.multiple_of((1 - y) * HALF, HALF), HALF), :]
        keep_ref[head] = local_ref[pl.ds(pl.multiple_of(y * HALF, HALF), HALF), :]
    dout_gain_ref[...] = total_gain


def delta_back_kernel(
    y_ref, mine_ref, other_ref, state_ref, uw_ref, solve_ref, mix_ref, do_ref,
    proj_ref, before_ref, taps_ref, col_ref, row_ref, beta_ref,
    dconv_ref, dtaps_ref, edge_ref,
    win_ref,
):
    length = proj_ref.shape[0]
    for head in range(col_ref.shape[0]):
        base = head * WIDE
        win_ref[0:PAD, :] = before_ref[:, base : base + QKV]
        win_ref[pl.ds(PAD, length), :] = proj_ref[:, base : base + QKV]
        taps = taps_ref[:, head * QKV : (head + 1) * QKV].astype(f32)
        conv = conv_of(win_ref, taps, length)
        rate = sigmoid(conv)
        active = conv * rate
        q_act = active[:, :DK]
        k_act = active[:, DK : 2 * DK]
        q_rate = lax.rsqrt(jnp.sum(q_act * q_act, axis=-1, keepdims=True) + norm_eps)
        k_rate = lax.rsqrt(jnp.sum(k_act * k_act, axis=-1, keepdims=True) + norm_eps)
        q_unit = q_act * q_rate
        k = k_act * k_rate
        q = q_unit * DK ** (-0.5)
        col = col_ref[head]
        row = row_ref[head]
        beta = beta_ref[head]
        rows, cols, ratio = decay_of(col, row, length)
        decay = jnp.exp(col)
        to_end = jnp.exp(row[:, length - 1 :] - col)
        state = state_ref[head]
        grad_end = halves(y_ref[0], mine_ref[head], other_ref[head])
        uw = uw_ref[head]
        grad_o = do_ref[:, head * DV : (head + 1) * DV]
        values_new = uw[:, :DV] - mm(uw[:, DV:], state, 1, 1)
        grad_new = mm(mix_ref[head], grad_o, 0, 0) + mm(to_end * k, grad_end, 1, 1)
        grad_right = mm(solve_ref[head], grad_new, 0, 0)
        grad_mix = jnp.where(rows >= cols, ratio * mm(grad_o, values_new, 1, 1), 0.0)
        grad_low = jnp.where(
            rows > cols, -(beta * ratio) * mm(grad_right, values_new, 1, 1), 0.0
        )
        grad_q = decay * mm(grad_o, state, 1, 0) + mm(grad_mix, k, 1, 0)
        grad_k = to_end * mm(values_new, grad_end, 1, 0)
        grad_k = grad_k - (beta * decay) * mm(grad_right, state, 1, 0)
        grad_k = grad_k + mm(grad_low, k, 1, 0) + mm(grad_low, k, 0, 0)
        grad_k = grad_k + mm(grad_mix, q, 0, 0)
        grad_v = beta * grad_right
        grad_qa = (DK ** (-0.5)) * q_rate * (
            grad_q - q_unit * jnp.sum(grad_q * q_unit, axis=-1, keepdims=True)
        )
        grad_ka = k_rate * (grad_k - k * jnp.sum(grad_k * k, axis=-1, keepdims=True))
        grad_conv = jnp.concatenate([grad_qa, grad_ka, grad_v], axis=1) * (
            rate * (1.0 + conv * (1.0 - rate))
        )
        span = slice(head * QKV, (head + 1) * QKV)
        dconv_ref[:, span] = grad_conv
        edge_ref[:, span] = grad_conv[0:PAD]
        for tap in range(CONV):
            dtaps_ref[tap : tap + 1, span] = jnp.sum(
                grad_conv * win_ref[pl.ds(PAD - tap, length), :], axis=0, keepdims=True
            )


def in_back_kernel(
    dconv_ref, after_ref, taps_ref, dz_ref, w_ref, gp_ref, part_ref, ext_ref
):
    length = dconv_ref.shape[0]
    ext_ref[pl.ds(0, length), :] = dconv_ref[...]
    ext_ref[pl.ds(length, PAD), :] = after_ref[...]
    taps = taps_ref[...].astype(f32)
    total = taps[0:1] * ext_ref[pl.ds(0, length), :]
    for tap in range(1, CONV):
        total = total + taps[tap : tap + 1] * ext_ref[pl.ds(tap, length), :]
    pieces = []
    for head in range(total.shape[1] // QKV):
        pieces.append(total[:, head * QKV : (head + 1) * QKV])
        pieces.append(dz_ref[:, head * DV : (head + 1) * DV])
    grad_proj = jnp.concatenate(pieces, axis=1).astype(bf16)
    gp_ref[...] = grad_proj.astype(f32)
    part_ref[...] = mmb(grad_proj, w_ref[...], 1, 1)


def norm_back_kernel(grad_ref, total_ref, stream_ref, gain_ref, out_ref, dgain_ref):
    grad_x, grad_gain = norm_backward(stream_ref[...], gain_ref[...], total_ref[...])
    out_ref[...] = grad_ref[...] + grad_x
    dgain_ref[...] = grad_gain


def weight_kernel(*refs, widths):
    out_ref = refs[-1]
    start = 0
    for index, width in enumerate(widths):
        a, b, a_far, b_far = refs[4 * index : 4 * index + 4]
        out_ref[:, start : start + width] = mmb(a[...], b[...], 0, 0) + mmb(
            a_far[...], b_far[...], 0, 0
        )
        start += width


def shift(array, axis, by):
    length = lax.axis_size(axis)
    pairs = [(i, i + by) for i in range(length) if 0 <= i + by < length]
    return lax.ppermute(array, axis, pairs)


def swap(array, axis, bit):
    length = lax.axis_size(axis)
    return lax.ppermute(array, axis, [(i, i ^ bit) for i in range(length)])


def head_total(part):
    size = lax.axis_size("head")
    rows = part.shape[0] // 2
    bit = lax.axis_index("head") % 2
    mine = lax.dynamic_slice_in_dim(part, bit * rows, rows, 0)
    other = lax.dynamic_slice_in_dim(part, (1 - bit) * rows, rows, 0)
    total = mine + swap(other, "head", 1)
    step = 2
    while step < size:
        total = total + swap(total, "head", step)
        step *= 2
    far = swap(total, "head", 1)
    return jnp.where(
        bit == 0, jnp.concatenate([total, far], 0), jnp.concatenate([far, total], 0)
    )


def full_sum(array, axis):
    step = 1
    while step < lax.axis_size(axis):
        array = array + swap(array, axis, step)
        step *= 2
    return array


def blocks_of(array, parity):
    size = lax.axis_size("seq")
    length, width = array.shape
    parts = array.reshape(length, size // 2, 2, width // size)
    return lax.dynamic_index_in_dim(parts, parity, 2, keepdims=False).reshape(length, width // 2)


def outer_scatter(array):
    size = lax.axis_size("seq")
    groups = [[2 * o + p for o in range(size // 2)] for p in range(2)]
    return lax.psum_scatter(
        array, "seq", scatter_dimension=0, tiled=True, axis_index_groups=groups
    )


def layer_forward(start, col, row, beta, weights, y):
    gain_one, w_in, taps, out_gain, w_out, gain_two, w_gate, w_up, w_down = weights
    length, width = start[0].shape
    heads = col.shape[0]
    proj_width = w_in.shape[1]
    if len(start) == 1:
        stream = start[0]
        normed, proj = call(
            in_kernel,
            [shape_of((length, width), bf16), shape_of((length, proj_width))],
            [stream, gain_one, w_in],
            "in_proj",
        )
    else:
        stream, normed, proj = call(
            in_sum_kernel,
            [
                shape_of((length, width)),
                shape_of((length, width), bf16),
                shape_of((length, proj_width)),
            ],
            [start[0], start[1], gain_one, w_in],
            "in_proj_sum",
        )
    before = shift(proj[length - PAD :], "seq", 1)
    square = shape_of((heads, DK, DK))
    wide = shape_of((heads, length, DV + DK))
    inner = shape_of((heads, length, length))
    half = shape_of((heads, HALF, DK))
    ow, uw, solve, mix, send, keep, transfer = call(
        delta_kernel,
        [wide, wide, inner, inner, shape_of((heads, DK + HALF, DK)), half, square],
        [y, proj, before, taps, col, row, beta],
        "delta",
        [pltpu.VMEM((length + PAD, QKV), f32), pltpu.VMEM((DV, DK), f32)],
    )
    far = swap(send, "seq", 1)
    first_t, second_t, pair_t, first_o, pair_o = call(
        pair_kernel, [square, square, square, half, half], [y, transfer, keep, far], "pair"
    )
    outer = lax.axis_size("seq") // 2
    state = shift(pair_o, "seq", 2)
    for _ in range(outer - 2):
        (moved,) = call(step_kernel, [half], [state, pair_t, pair_o], "step")
        state = shift(moved, "seq", 2)
    mine, other = call(last_kernel, [half, half], [y, state, first_t, first_o], "last")
    other = swap(other, "seq", 1)
    incoming, outputs, gated, part = call(
        out_kernel,
        [
            shape_of((heads, DV, DK)),
            shape_of((length, heads * DV)),
            shape_of((length, heads * DV), bf16),
            shape_of((length, width)),
        ],
        [y, mine, other, ow, proj, out_gain, w_out],
        "out_proj",
    )
    total = head_total(part)
    hidden_width = w_gate.shape[1]
    mid, normed_two, gate, up, hidden, part = call(
        ffn_kernel,
        [
            shape_of((length, width)),
            shape_of((length, width), bf16),
            shape_of((length, hidden_width)),
            shape_of((length, hidden_width)),
            shape_of((length, hidden_width), bf16),
            shape_of((length, width)),
        ],
        [stream, total, gain_two, w_gate, w_up, w_down],
        "ffn",
    )
    total = head_total(part)
    parity = lax.axis_index("seq") % 2
    sent = jnp.concatenate(
        [
            blocks_of(normed, 1 - parity).astype(f32),
            gated.astype(f32),
            blocks_of(normed_two, 1 - parity).astype(f32),
            hidden.astype(f32),
        ],
        axis=1,
    )
    far_forward = swap(sent, "seq", 1)
    stored = dict(
        stream=stream, normed=normed, proj=proj, before=before, ow=ow, uw=uw, solve=solve,
        mix=mix, first_t=first_t, second_t=second_t, pair_t=pair_t, incoming=incoming,
        outputs=outputs, gated=gated, mid=mid, normed_two=normed_two, gate=gate, up=up,
        hidden=hidden, far_forward=far_forward,
    )
    return (mid, total), stored


def layer_backward(grad, col, row, beta, weights, kept, y):
    gain_one, w_in, taps, out_gain, w_out, gain_two, w_gate, w_up, w_down = weights
    length, width = grad.shape
    heads = col.shape[0]
    hidden_width = w_gate.shape[1]
    proj_width = w_in.shape[1]
    parity = lax.axis_index("seq") % 2
    half_width = width // 2
    back, gg, gu, part = call(
        ffn_back_kernel,
        [
            shape_of((length, width)),
            shape_of((length, hidden_width)),
            shape_of((length, hidden_width)),
            shape_of((length, width)),
        ],
        [grad, kept["gate"], kept["up"], w_gate, w_up, w_down],
        "ffn_back",
    )
    total = head_total(part)
    far_forward = kept["far_forward"]
    value_width = heads * DV
    normed_far = far_forward[:, :half_width]
    gated_far = far_forward[:, half_width : half_width + value_width]
    normed_two_far = far_forward[
        :, half_width + value_width : 2 * half_width + value_width
    ]
    hidden_far = far_forward[:, 2 * half_width + value_width :]
    far_ffn = swap(
        jnp.concatenate([gg, gu, blocks_of(back, 1 - parity)], axis=1), "seq", 1
    )
    both = 2 * hidden_width
    (ffn_weights,) = call(
        functools.partial(weight_kernel, widths=(both, hidden_width)),
        [shape_of((half_width, both + hidden_width))],
        [
            blocks_of(kept["normed_two"], parity),
            jnp.concatenate([gg, gu], axis=1),
            normed_two_far,
            far_ffn[:, :both],
            blocks_of(back, parity),
            kept["hidden"],
            far_ffn[:, both:],
            hidden_far,
        ],
        "weights_ffn",
    )
    ffn_weights = outer_scatter(ffn_weights)
    half = shape_of((heads, HALF, DK))
    grad, back, grad_o, grad_z, dgain_two, dout_gain, send, keep = call(
        out_back_kernel,
        [
            shape_of((length, width)),
            shape_of((length, width)),
            shape_of((length, value_width)),
            shape_of((length, value_width)),
            shape_of((1, width)),
            shape_of((1, DV)),
            half,
            half,
        ],
        [
            y, grad, total, kept["mid"], gain_two, w_out, kept["outputs"], kept["proj"], out_gain,
            kept["ow"],
        ],
        "out_back",
        [pltpu.VMEM((DV, DK), f32)],
    )
    far = swap(send, "seq", 1)
    second_o, pair_o = call(
        pair_back_kernel, [half, half], [y, keep, far, kept["first_t"]], "pair_back"
    )
    outer = lax.axis_size("seq") // 2
    state = shift(pair_o, "seq", -2)
    for _ in range(outer - 2):
        (moved,) = call(step_back_kernel, [half], [state, kept["pair_t"], pair_o], "step_back")
        state = shift(moved, "seq", -2)
    mine, other = call(
        last_back_kernel, [half, half], [y, state, kept["second_t"], second_o], "last_back"
    )
    other = swap(other, "seq", 1)
    qkv_width = heads * QKV
    dconv, dtaps, edge = call(
        delta_back_kernel,
        [
            shape_of((length, qkv_width)),
            shape_of((CONV, qkv_width)),
            shape_of((PAD, qkv_width)),
        ],
        [
            y, mine, other, kept["incoming"], kept["uw"], kept["solve"], kept["mix"], grad_o,
            kept["proj"], kept["before"], taps, col, row, beta,
        ],
        "delta_back",
        [pltpu.VMEM((length + PAD, QKV), f32)],
    )
    after = shift(edge, "seq", -1)
    grad_proj, part = call(
        in_back_kernel,
        [shape_of((length, proj_width)), shape_of((length, width))],
        [dconv, after, taps, grad_z, w_in],
        "in_back",
        [pltpu.VMEM((length + PAD, qkv_width), f32)],
    )
    far_mix = swap(
        jnp.concatenate([grad_proj, blocks_of(back, 1 - parity)], axis=1), "seq", 1
    )
    (mix_weights,) = call(
        functools.partial(weight_kernel, widths=(proj_width, value_width)),
        [shape_of((half_width, proj_width + value_width))],
        [
            blocks_of(kept["normed"], parity),
            grad_proj,
            normed_far,
            far_mix[:, :proj_width],
            blocks_of(back, parity),
            kept["gated"],
            far_mix[:, proj_width:],
            gated_far,
        ],
        "weights_mix",
    )
    mix_weights = outer_scatter(mix_weights)
    total = head_total(part)
    grad, dgain_one = call(
        norm_back_kernel,
        [shape_of((length, width)), shape_of((1, width))],
        [grad, total, kept["stream"], gain_one],
        "norm_back",
    )
    return grad, (ffn_weights, mix_weights, dtaps, dgain_one, dout_gain, dgain_two)


def body(
    tokens,
    cotangent,
    gate_code,
    beta_code,
    norm1_gain,
    weight_in,
    conv_weight,
    out_gain,
    weight_out,
    norm2_gain,
    weight_gate,
    weight_up,
    weight_down,
):
    y = (lax.axis_index("seq") % 2).astype(jnp.int32).reshape(1)
    logdecay = -gate_code.astype(f32) * gate_unit
    beta_rate = beta_code.astype(f32) * beta_unit
    cumulated = jnp.transpose(jnp.cumsum(logdecay, axis=1), (0, 2, 1))
    beta_rate = jnp.transpose(beta_rate, (0, 2, 1))
    layers = []
    for level in range(STACK_LEVELS):
        layers.append(
            (
                cumulated[level][:, :, None],
                cumulated[level][:, None, :],
                beta_rate[level][:, :, None],
                (
                    norm1_gain[level][None],
                    weight_in[level],
                    conv_weight[level],
                    out_gain[level][None],
                    weight_out[level],
                    norm2_gain[level][None],
                    weight_gate[level],
                    weight_up[level],
                    weight_down[level],
                ),
            )
        )
    start = (tokens.astype(f32),)
    kept = []
    for level in range(STACK_LEVELS):
        start, stored = layer_forward(start, *layers[level], y)
        kept.append(stored)
    (activations,) = call(sum_kernel, [shape_of(tokens.shape, bf16)], list(start), "finish")
    grad = cotangent.astype(f32)
    parts = [None] * STACK_LEVELS
    for level in reversed(range(STACK_LEVELS)):
        grad, parts[level] = layer_backward(grad, *layers[level], kept[level], y)
    hidden_width = weight_gate.shape[2]
    proj_width = weight_in.shape[2]
    ffn = jnp.stack([part[0] for part in parts])
    mixer = jnp.stack([part[1] for part in parts])
    grad_gate = ffn[:, :, :hidden_width]
    grad_up = ffn[:, :, hidden_width : 2 * hidden_width]
    grad_down = jnp.transpose(ffn[:, :, 2 * hidden_width :], (0, 2, 1))
    grad_in = mixer[:, :, :proj_width]
    grad_out = jnp.transpose(mixer[:, :, proj_width:], (0, 2, 1))
    qkv_width = conv_weight.shape[2]
    width = tokens.shape[1]
    out_gain_part = full_sum(jnp.concatenate([part[4] for part in parts], axis=0), "head")
    small = jnp.concatenate(
        [part[2].reshape(1, -1) for part in parts]
        + [part[3] for part in parts]
        + [part[5] for part in parts]
        + [out_gain_part.reshape(1, -1)],
        axis=1,
    )
    small = full_sum(small, "seq")[0]
    sizes = [STACK_LEVELS * CONV * qkv_width, STACK_LEVELS * width, STACK_LEVELS * width]
    conv_grad = small[: sizes[0]].reshape(STACK_LEVELS, CONV, qkv_width)
    gain_one_grad = small[sizes[0] : sizes[0] + sizes[1]].reshape(STACK_LEVELS, width)
    gain_two_grad = small[sizes[0] + sizes[1] : sum(sizes)].reshape(STACK_LEVELS, width)
    out_gain_grad = small[sum(sizes) :].reshape(STACK_LEVELS, DV)
    return (
        activations,
        grad,
        gain_one_grad,
        grad_in,
        conv_grad,
        out_gain_grad,
        grad_out,
        gain_two_grad,
        grad_gate,
        grad_up,
        grad_down,
    )


def solution(mesh):
    in_specs = (
        P("seq", None),
        P("seq", None),
        P(None, "seq", "head"),
        P(None, "seq", "head"),
        P(),
        P(None, None, "head"),
        P(None, None, "head"),
        P(),
        P(None, "head", None),
        P(),
        P(None, None, "head"),
        P(None, None, "head"),
        P(None, "head", None),
    )
    out_specs = (
        P("seq", None),
        P("seq", None),
        P(),
        P(None, "seq", "head"),
        P(None, None, "head"),
        P(),
        P(None, "head", "seq"),
        P(),
        P(None, "seq", "head"),
        P(None, "seq", "head"),
        P(None, "head", "seq"),
    )
    return jax.shard_map(body, mesh=mesh, in_specs=in_specs, out_specs=out_specs, check_vma=False)
```

time: 1610 us -> 731 us (0.45)
  waiting for transfers between devices: 1020 us -> 348 us
  other arithmetic: 197 us -> 22.4 us
  matrix products: 162 us -> 0 us
  Pallas kernels: 0 us -> 142 us
  starting transfers between devices: 13.3 us -> 88.3 us
  blocking collectives: 72.1 us -> 0 us
    reduce_scatter x9 -> x4, waiting for transfers between devices: 680 us -> 54.8 us  [outer_scatter(): lax.psum_scatter(array, 'seq', scatter_dimension=0, tiled=True, axis_inde...]
    ppermute x4 -> x59, waiting for transfers between devices: 44.8 us -> 293 us  [the longest x43 195 us: swap(): return lax.ppermute(array, axis, [(i, i ^ bit) for i in range(length)])]
    all_gather x6 -> x0, waiting for transfers between devices: 203 us -> none  [the longest x2 101 us: state_prefix(): lax.all_gather(offset, 'seq', axis=0, tiled=True)]
    dot_general x158 -> x0, matrix products: 153 us -> none  [the longest x16 26.1 us: retreat(): jnp.einsum('hvj,hkj->hvk', carry_state, transfer_kept[index_now], precisi...]
    pallas_call x0 -> x39, Pallas kernels: none -> 142 us  [call(): pl.pallas_call(body, out_shape=tuple(outs), in_specs=specs, out_specs=tup...]
    another operation x51 -> x2, other arithmetic: 143 us -> 2.96 us  [the longest x1 2.77 us: body(): mixer = jnp.stack([part[1] for part in parts])]
    psum x4 -> x0, waiting for transfers between devices: 95.1 us -> none  [the longest x2 61.6 us: layer_backward(): grad_normed_two = lax.psum(ffn_partial, 'head')]
    ppermute x4 -> x59, starting transfers between devices: 12.1 us -> 88.1 us  [the longest x16 44.2 us: shift(): return lax.ppermute(array, axis, pairs)]
  transfers between devices with their start and end apart: 23 -> 63, of which waited for: 22 -> 51; matrix products, arithmetic and copies ran while one was open for 8% -> 12% of each run, Pallas kernels for 0% -> 10%
where the time goes in v1:
time: 731 us; the launch traced here: 723 us
  waiting for transfers between devices  348 us (48%)
  Pallas kernels  142 us (19%)
  local copies, waits for them, and re-layouts  107 us (15%)
  starting transfers between devices  88.3 us (12%)
  other arithmetic  22.4 us (3%)
  between operations  15 us (2%)
    ppermute x43, waiting for transfers between devices, swap(): return lax.ppermute(array, axis, [(i, i ^ bit) for i in range(length)])  195 us
    pallas_call x39, Pallas kernels, call(): pl.pallas_call(body, out_shape=tuple(outs), in_specs=specs, out_specs=tup...  142 us
    ppermute x16, waiting for transfers between devices, shift(): return lax.ppermute(array, axis, pairs)  98 us
    reduce_scatter x4, waiting for transfers between devices, outer_scatter(): lax.psum_scatter(array, 'seq', scatter_dimension=0, tiled=True, axis_inde...  54.8 us
    unnamed x185, local copies, waits for them, and re-layouts  46 us
    ppermute x16, starting transfers between devices, shift(): return lax.ppermute(array, axis, pairs)  44.2 us
    ppermute x43, starting transfers between devices, swap(): return lax.ppermute(array, axis, [(i, i ^ bit) for i in range(length)])  44 us
  transfers between devices with their start and end apart: 63, of which 51 were waited for; matrix products, arithmetic and copies ran while one was open for 12% of the time, Pallas kernels for 10%

profile of v1, /device:TPU:0, one launch (start us, length us, event | category | flops | bytes accessed | tf_op | source)
XLA Modules:
  0.0 722.9 jit_solution(14211939061025628726)
XLA Ops:
  10.4 5.9 slice_bitcast_fusion
  29.5 9.7 %delta.2 = (f32[2,128,384]{2,1,0:T(8,128)}, f32[2,128,384]{2,1,0:T(8,128)}, f32[2,128,128]{2,1,0:T(8,128)}, f32[2,128,128]{2,1,0:T(8,128)}, f32[2,256,128]{2,1,0...) custom-call(s32[1]{0:T(128)} %bitcast.y_ref, f32[128,1536]{1,0:T(8,128)} %get-tuple-element.110.proj_ref, ...), custom_call_target="tpu_custom_call" | custom-call | tf_op jit(solution)/shard_map/delta/pallas_call | solution.py:38
  40.7 6.5 collective-permute-done.1.other_ref
  119.0 7.1 collective-permute-done.10
  138.9 9.7 %delta.3 = (f32[2,128,384]{2,1,0:T(8,128)}, f32[2,128,384]{2,1,0:T(8,128)}, f32[2,128,128]{2,1,0:T(8,128)}, f32[2,128,128]{2,1,0:T(8,128)}, f32[2,256,128]{2,1,0...) custom-call(s32[1]{0:T(128)} %bitcast.y_ref, f32[128,1536]{1,0:T(8,128)} %get-tuple-element.125.proj_ref, ...), custom_call_target="tpu_custom_call" | custom-call | tf_op jit(solution)/shard_map/delta/pallas_call | solution.py:38
  151.0 6.4 collective-permute-done.13.other_ref
  203.9 6.8 collective-permute-done.19
  253.7 14.1 %collective-permute-done.55 = f32[128,2240]{0,1:T(8,128)S(1)} collective-permute-done((f32[128,2240]{0,1:T(8,128)}, f32[128,2240]{0,1:T(8,128)S(1)}, u32[]{:S(2)}, u32[]{:S(2)}) %collective-permute-start.55) | collective-permute-done | bytes 1146912 | tf_op jit(solution)/shard_map/ppermute | solution.py:430
  269.8 18.6 %collective-permute-done.58 = f32[128,1920]{1,0:T(8,128)S(1)} collective-permute-done((f32[128,1920]{1,0:T(8,128)}, f32[128,1920]{1,0:T(8,128)S(1)}, u32[]{:S(2)}, u32[]{:S(2)}) %collective-permute-start.58) | collective-permute-done | bytes 983072 | tf_op jit(solution)/shard_map/ppermute | solution.py:430
  305.3 13.1 %collective-permute-done.28.state_ref = f32[2,128,128]{2,1,0:T(8,128)S(1)} collective-permute-done((f32[2,128,128]{2,1,0:T(8,128)}, f32[2,128,128]{2,1,0:T(8,128)S(1)}, u32[]{:S(2)}, u32[]{:S(2)}) %collective-permute-start.28) | collective-permute-done | bytes 131104 | tf_op jit(solution)/shard_map/ppermute | solution.py:425
  322.5 12.3 %collective-permute-done.29.state_ref = f32[2,128,128]{2,1,0:T(8,128)S(1)} collective-permute-done((f32[2,128,128]{2,1,0:T(8,128)}, f32[2,128,128]{2,1,0:T(8,128)S(1)}, u32[]{:S(2)}, u32[]{:S(2)}) %collective-permute-start.29) | collective-permute-done | bytes 131104 | tf_op jit(solution)/shard_map/ppermute | solution.py:425
  338.8 12.2 %collective-permute-done.30.state_ref = f32[2,128,128]{2,1,0:T(8,128)S(1)} collective-permute-done((f32[2,128,128]{2,1,0:T(8,128)}, f32[2,128,128]{2,1,0:T(8,128)S(1)}, u32[]{:S(2)}, u32[]{:S(2)}) %collective-permute-start.30) | collective-permute-done | bytes 131104 | tf_op jit(solution)/shard_map/ppermute | solution.py:425
  359.6 6.2 delta_back.2
  381.6 6.9 collective-permute-done.34
  425.9 9.0 %collective-permute-done.53 = f32[128,2240]{0,1:T(8,128)S(1)} collective-permute-done((f32[128,2240]{0,1:T(8,128)}, f32[128,2240]{0,1:T(8,128)S(1)}, u32[]{:S(2)}, u32[]{:S(2)}) %collective-permute-start.53) | collective-permute-done | bytes 1146912 | tf_op jit(solution)/shard_map/ppermute | solution.py:430
  438.5 17.0 %collective-permute-done.57 = f32[128,1920]{1,0:T(8,128)} collective-permute-done((f32[128,1920]{1,0:T(8,128)}, f32[128,1920]{1,0:T(8,128)}, u32[]{:S(2)}, u32[]{:S(2)}) %collective-permute-start.57) | collective-permute-done | bytes 983072 | tf_op jit(solution)/shard_map/ppermute | solution.py:430
  470.6 19.8 %collective-permute-done.56 = f32[128,2048]{1,0:T(8,128)S(1)} collective-permute-done((f32[128,2048]{1,0:T(8,128)S(1)}, f32[128,2048]{1,0:T(8,128)S(1)}, u32[]{:S(2)}, u32[]{:S(2)}) %collective-permute-start.56) | collective-permute-done | bytes 1048608 | tf_op jit(solution)/shard_map/ppermute | solution.py:430
  507.2 14.3 %collective-permute-done.40.state_ref = f32[2,128,128]{2,1,0:T(8,128)S(1)} collective-permute-done((f32[2,128,128]{2,1,0:T(8,128)}, f32[2,128,128]{2,1,0:T(8,128)S(1)}, u32[]{:S(2)}, u32[]{:S(2)}) %collective-permute-start.40) | collective-permute-done | bytes 131104 | tf_op jit(solution)/shard_map/ppermute | solution.py:425
  525.5 12.0 %collective-permute-done.41.state_ref = f32[2,128,128]{2,1,0:T(8,128)S(1)} collective-permute-done((f32[2,128,128]{2,1,0:T(8,128)}, f32[2,128,128]{2,1,0:T(8,128)S(1)}, u32[]{:S(2)}, u32[]{:S(2)}) %collective-permute-start.41) | collective-permute-done | bytes 131104 | tf_op jit(solution)/shard_map/ppermute | solution.py:425
  541.6 9.4 %collective-permute-done.42.state_ref = f32[2,128,128]{2,1,0:T(8,128)S(1)} collective-permute-done((f32[2,128,128]{2,1,0:T(8,128)}, f32[2,128,128]{2,1,0:T(8,128)S(1)}, u32[]{:S(2)}, u32[]{:S(2)}) %collective-permute-start.42) | collective-permute-done | bytes 131104 | tf_op jit(solution)/shard_map/ppermute | solution.py:425
  559.7 6.6 delta_back.3
  585.5 14.4 %collective-permute-done.54 = f32[128,2048]{1,0:T(8,128)S(1)} collective-permute-done((f32[128,2048]{1,0:T(8,128)S(1)}, f32[128,2048]{1,0:T(8,128)S(1)}, u32[]{:S(2)}, u32[]{:S(2)}) %collective-permute-start.54) | collective-permute-done | bytes 1048608 | tf_op jit(solution)/shard_map/ppermute | solution.py:430
  619.4 7.4 %collective-permute-done.46 = f32[64,1024]{1,0:T(8,128)S(1)} collective-permute-done((f32[64,1024]{1,0:T(8,128)S(1)}, f32[64,1024]{1,0:T(8,128)S(1)}, u32[]{:S(2)}, u32[]{:S(2)}) %collective-permute-start.46) | collective-permute-done | bytes 262176 | tf_op jit(solution)/shard_map/ppermute | solution.py:430
  657.6 54.8 %reduce-scatter.5.cloned.1.call-done = f32[128,2048]{1,0:T(8,128)} async-done(((f32[512,2048]{1,0:T(8,128)}), f32[128,2048]{1,0:T(8,128)}) %reduce-scatter.5.cloned.1.call-update) | async-done | bytes 1048592 | tf_op jit(solution)/shard_map/reduce_scatter | solution.py:468
  (438 shorter events, 407.9 us)
Async XLA Ops:
  7.2 645.0 %reduce-scatter.11.cloned.1.call-start = ((), (), s32[]{:S(2)}) async-start(), calls=%async_computation.7 | async-start | bytes 5570560 | tf_op jit(solution)/shard_map/reduce_scatter | solution.py:468
  92.1 8.8 %collective-permute-start.7 = (f32[64,1024]{1,0:T(8,128)S(1)}, f32[64,1024]{1,0:T(8,128)S(1)}, u32[]{:S(2)}, u32[]{:S(2)}) collective-permute-start(f32[64,1024]{1,0:T(8,128)S(1)} %dynamic-slice_add_fusion.7), channel_id=1, source_target_pairs={{0,2},{1,3},{2,0},{3,1},{4,6},{5,7},{6,4},{7,5},{8,10},{9,11},{10,... | collective-permute-start | bytes 786440 | tf_op jit(solution)/shard_map/ppermute | solution.py:430
  117.4 8.6 %collective-permute-start.10 = (f32[64,1024]{1,0:T(8,128)S(1)}, f32[64,1024]{1,0:T(8,128)S(1)}, u32[]{:S(2)}, u32[]{:S(2)}) collective-permute-start(f32[64,1024]{1,0:T(8,128)S(1)} %dynamic-slice_add_fusion.6), channel_id=1, source_target_pairs={{0,2},{1,3},{2,0},{3,1},{4,6},{5,7},{6,4},{7,5},{8,10},{9,11},{10,... | collective-permute-start | bytes 786440 | tf_op jit(solution)/shard_map/ppermute | solution.py:430
  148.6 8.7 %collective-permute-start.13 = (f32[2,256,128]{2,1,0:T(8,128)}, f32[2,256,128]{2,1,0:T(8,128)S(1)}, u32[]{:S(2)}, u32[]{:S(2)}) collective-permute-start(f32[2,256,128]{2,1,0:T(8,128)} %get-tuple-element.128), channel_id=1, source_target_pairs={{0,4},{4,0},{8,12},{12,8},{16,20},{20,16},{24,28},{28,24},{1,5},{5... | collective-permute-start | bytes 786440 | tf_op jit(solution)/shard_map/ppermute | solution.py:430
  229.2 8.7 %collective-permute-start.25 = (f32[64,1024]{1,0:T(8,128)S(1)}, f32[64,1024]{1,0:T(8,128)S(1)}, u32[]{:S(2)}, u32[]{:S(2)}) collective-permute-start(f32[64,1024]{1,0:T(8,128)S(1)} %dynamic-slice_add_fusion.3), channel_id=1, source_target_pairs={{0,2},{1,3},{2,0},{3,1},{4,6},{5,7},{6,4},{7,5},{8,10},{9,11},{10,... | collective-permute-start | bytes 786440 | tf_op jit(solution)/shard_map/ppermute | solution.py:430
  239.4 28.3 %collective-permute-start.55 = (f32[128,2240]{0,1:T(8,128)}, f32[128,2240]{0,1:T(8,128)S(1)}, u32[]{:S(2)}, u32[]{:S(2)}) collective-permute-start(f32[128,2240]{0,1:T(8,128)} %copy.201), channel_id=1, source_target_pairs={{0,4},{4,0},{8,12},{12,8},{16,20},{20,16},{24,28},{28,24},{1,5},{5... | collective-permute-start | bytes 3440648 | tf_op jit(solution)/shard_map/ppermute | solution.py:430
  249.9 38.4 %collective-permute-start.58 = (f32[128,1920]{1,0:T(8,128)}, f32[128,1920]{1,0:T(8,128)S(1)}, u32[]{:S(2)}, u32[]{:S(2)}) collective-permute-start(f32[128,1920]{1,0:T(8,128)} %concatenate.111), channel_id=1, source_target_pairs={{0,4},{4,0},{8,12},{12,8},{16,20},{20,16},{24,28},{28,24},{1,5},{5... | collective-permute-start | bytes 2949128 | tf_op jit(solution)/shard_map/ppermute | solution.py:430
  295.2 357.0 %reduce-scatter.9.cloned.1.call-start = ((), (), s32[]{:S(2)}) async-start(), calls=%async_computation.6 | async-start | bytes 5570560 | tf_op jit(solution)/shard_map/reduce_scatter | solution.py:468
  304.0 14.4 %collective-permute-start.28 = (f32[2,128,128]{2,1,0:T(8,128)}, f32[2,128,128]{2,1,0:T(8,128)S(1)}, u32[]{:S(2)}, u32[]{:S(2)}) collective-permute-start(f32[2,128,128]{2,1,0:T(8,128)} %get-tuple-element.146.offset_ref), channel_id=1, source_target_pairs={{8,0},{12,4},{16,8},{20,12},{24,16},{28,20},{9,1},{13,5},{17,9},{2... | collective-permute-start | bytes 393224 | tf_op jit(solution)/shard_map/ppermute | solution.py:425
  321.2 13.6 %collective-permute-start.29 = (f32[2,128,128]{2,1,0:T(8,128)}, f32[2,128,128]{2,1,0:T(8,128)S(1)}, u32[]{:S(2)}, u32[]{:S(2)}) collective-permute-start(f32[2,128,128]{2,1,0:T(8,128)} %step_back.4), channel_id=1, source_target_pairs={{8,0},{12,4},{16,8},{20,12},{24,16},{28,20},{9,1},{13,5},{17,9},{2... | collective-permute-start | bytes 393224 | tf_op jit(solution)/shard_map/ppermute | solution.py:425
  337.5 13.5 %collective-permute-start.30 = (f32[2,128,128]{2,1,0:T(8,128)}, f32[2,128,128]{2,1,0:T(8,128)S(1)}, u32[]{:S(2)}, u32[]{:S(2)}) collective-permute-start(f32[2,128,128]{2,1,0:T(8,128)} %step_back.5), channel_id=1, source_target_pairs={{8,0},{12,4},{16,8},{20,12},{24,16},{28,20},{9,1},{13,5},{17,9},{2... | collective-permute-start | bytes 393224 | tf_op jit(solution)/shard_map/ppermute | solution.py:425
  402.2 8.6 %collective-permute-start.37 = (f32[64,1024]{1,0:T(8,128)S(1)}, f32[64,1024]{1,0:T(8,128)S(1)}, u32[]{:S(2)}, u32[]{:S(2)}) collective-permute-start(f32[64,1024]{1,0:T(8,128)S(1)} %dynamic-slice_add_fusion.1), channel_id=1, source_target_pairs={{0,2},{1,3},{2,0},{3,1},{4,6},{5,7},{6,4},{7,5},{8,10},{9,11},{10,... | collective-permute-start | bytes 786440 | tf_op jit(solution)/shard_map/ppermute | solution.py:430
  405.2 29.7 %collective-permute-start.53 = (f32[128,2240]{0,1:T(8,128)}, f32[128,2240]{0,1:T(8,128)S(1)}, u32[]{:S(2)}, u32[]{:S(2)}) collective-permute-start(f32[128,2240]{0,1:T(8,128)} %copy.193), channel_id=1, source_target_pairs={{0,4},{4,0},{8,12},{12,8},{16,20},{20,16},{24,28},{28,24},{1,5},{5... | collective-permute-start | bytes 3440648 | tf_op jit(solution)/shard_map/ppermute | solution.py:430
  421.9 33.6 %collective-permute-start.57 = (f32[128,1920]{1,0:T(8,128)}, f32[128,1920]{1,0:T(8,128)}, u32[]{:S(2)}, u32[]{:S(2)}) collective-permute-start(f32[128,1920]{1,0:T(8,128)} %concatenate.109), channel_id=1, source_target_pairs={{0,4},{4,0},{8,12},{12,8},{16,20},{20,16},{24,28},{28,24},{1,5},{5... | collective-permute-start | bytes 2949128 | tf_op jit(solution)/shard_map/ppermute | solution.py:430
  464.5 193.1 %reduce-scatter.7.cloned.1.call-start = ((), (), s32[]{:S(2)}) async-start(), calls=%async_computation.5 | async-start | bytes 5242880 | tf_op jit(solution)/shard_map/reduce_scatter | solution.py:468
  465.7 24.6 %collective-permute-start.56 = (f32[128,2048]{1,0:T(8,128)S(1)}, f32[128,2048]{1,0:T(8,128)S(1)}, u32[]{:S(2)}, u32[]{:S(2)}) collective-permute-start(f32[128,2048]{1,0:T(8,128)S(1)} %pad_maximum_fusion.1), channel_id=1, source_target_pairs={{0,4},{4,0},{8,12},{12,8},{16,20},{20,16},{24,28},{28,24},{1,5},{5... | collective-permute-start | bytes 3145736 | tf_op jit(solution)/shard_map/ppermute | solution.py:430
  497.2 215.2 %reduce-scatter.5.cloned.1.call-start = ((), (), s32[]{:S(2)}) async-start(), calls=%async_computation.4 | async-start | bytes 5242880 | tf_op jit(solution)/shard_map/reduce_scatter | solution.py:468
  505.7 15.8 %collective-permute-start.40 = (f32[2,128,128]{2,1,0:T(8,128)}, f32[2,128,128]{2,1,0:T(8,128)S(1)}, u32[]{:S(2)}, u32[]{:S(2)}) collective-permute-start(f32[2,128,128]{2,1,0:T(8,128)} %get-tuple-element.168.offset_ref), channel_id=1, source_target_pairs={{8,0},{12,4},{16,8},{20,12},{24,16},{28,20},{9,1},{13,5},{17,9},{2... | collective-permute-start | bytes 393224 | tf_op jit(solution)/shard_map/ppermute | solution.py:425
  524.2 13.3 %collective-permute-start.41 = (f32[2,128,128]{2,1,0:T(8,128)}, f32[2,128,128]{2,1,0:T(8,128)S(1)}, u32[]{:S(2)}, u32[]{:S(2)}) collective-permute-start(f32[2,128,128]{2,1,0:T(8,128)} %step_back.6), channel_id=1, source_target_pairs={{8,0},{12,4},{16,8},{20,12},{24,16},{28,20},{9,1},{13,5},{17,9},{2... | collective-permute-start | bytes 393224 | tf_op jit(solution)/shard_map/ppermute | solution.py:425
  540.3 10.7 %collective-permute-start.42 = (f32[2,128,128]{2,1,0:T(8,128)}, f32[2,128,128]{2,1,0:T(8,128)S(1)}, u32[]{:S(2)}, u32[]{:S(2)}) collective-permute-start(f32[2,128,128]{2,1,0:T(8,128)} %step_back.7), channel_id=1, source_target_pairs={{8,0},{12,4},{16,8},{20,12},{24,16},{28,20},{9,1},{13,5},{17,9},{2... | collective-permute-start | bytes 393224 | tf_op jit(solution)/shard_map/ppermute | solution.py:425
  578.3 21.6 %collective-permute-start.54 = (f32[128,2048]{1,0:T(8,128)S(1)}, f32[128,2048]{1,0:T(8,128)S(1)}, u32[]{:S(2)}, u32[]{:S(2)}) collective-permute-start(f32[128,2048]{1,0:T(8,128)S(1)} %pad_maximum_fusion), channel_id=1, source_target_pairs={{0,4},{4,0},{8,12},{12,8},{16,20},{20,16},{24,28},{28,24},{1,5},{5... | collective-permute-start | bytes 3145736 | tf_op jit(solution)/shard_map/ppermute | solution.py:430
  617.8 23.4 %collective-permute-start.23 = (f32[64,1024]{1,0:T(8,128)S(1)}, f32[64,1024]{1,0:T(8,128)S(1)}, u32[]{:S(2)}, u32[]{:S(2)}) collective-permute-start(f32[64,1024]{1,0:T(8,128)S(1)} %add.143), channel_id=1, source_target_pairs={{0,1},{1,0},{2,3},{3,2},{4,5},{5,4},{6,7},{7,6},{8,9},{9,8},{10,11... | collective-permute-start | bytes 786440 | tf_op jit(solution)/shard_map/ppermute | solution.py:430
  618.1 8.8 %collective-permute-start.46 = (f32[64,1024]{1,0:T(8,128)S(1)}, f32[64,1024]{1,0:T(8,128)S(1)}, u32[]{:S(2)}, u32[]{:S(2)}) collective-permute-start(f32[64,1024]{1,0:T(8,128)S(1)} %dynamic-slice_add_fusion), channel_id=1, source_target_pairs={{0,2},{1,3},{2,0},{3,1},{4,6},{5,7},{6,4},{7,5},{8,10},{9,11},{10,... | collective-permute-start | bytes 786440 | tf_op jit(solution)/shard_map/ppermute | solution.py:430
  641.0 8.6 %collective-permute-start.52 = (f32[1,12800]{1,0:T(1,128)S(1)}, f32[1,12800]{1,0:T(1,128)S(1)}, u32[]{:S(2)}, u32[]{:S(2)}) collective-permute-start(f32[1,12800]{1,0:T(1,128)S(1)} %add.155), channel_id=1, source_target_pairs={{0,16},{4,20},{8,24},{12,28},{16,0},{20,4},{24,8},{28,12},{1,17},{... | collective-permute-start | bytes 153608 | tf_op jit(solution)/shard_map/ppermute | solution.py:430
  (111 other events, 476.0 us)
Sparse Core Ops, SparseCore 0:
  295.3 91.2 reduce-scatter.10
  464.6 87.3 reduce-scatter.8
  554.3 78.2 reduce-scatter.6
  634.7 77.5 reduce-scatter.4

commit v2 on v1

v2 whole, which is shorter than its diff:
```python
import functools

import jax
import jax.numpy as jnp
from jax import lax
from jax.experimental import pallas as pl
from jax.experimental.pallas import tpu as pltpu
from jax.sharding import PartitionSpec as P

DK = 128
DV = 256
CONV = 4
STACK_LEVELS = 2
QKV = 2 * DK + DV
WIDE = 2 * DK + 2 * DV
HALF = DV // 2
PAD = 8

f32 = jnp.float32
bf16 = jnp.bfloat16
norm_eps = 1e-06
gate_unit = 1.0 / 1048576.0
beta_unit = 1.0 / 1024.0


def shape_of(dims, dtype=f32):
    return jax.ShapeDtypeStruct(tuple(dims), dtype)


def call(body, outs, args, name, scratch=()):
    specs, arrays = [], []
    for arg in args:
        if isinstance(arg, tuple):
            array, level = arg
            rest = (0,) * (array.ndim - 1)
            specs.append(
                pl.BlockSpec((None,) + array.shape[1:], functools.partial(at_level, level, rest))
            )
        elif arg.dtype == jnp.int32:
            array = arg
            specs.append(pl.BlockSpec(memory_space=pltpu.SMEM))
        else:
            array = arg
            specs.append(pl.BlockSpec(memory_space=pltpu.VMEM))
        arrays.append(array)
    with jax.named_scope("k_" + name):
        return pl.pallas_call(
            body,
            grid=(1,),
            out_shape=tuple(outs),
            in_specs=specs,
            out_specs=tuple(pl.BlockSpec(memory_space=pltpu.VMEM) for _ in outs),
            scratch_shapes=list(scratch),
            name=name,
        )(*arrays)


def at_level(level, rest, _):
    return (level,) + rest


def mm(a, b, ca, cb):
    a_high, b_high = a.astype(bf16), b.astype(bf16)
    a_low = (a - a_high.astype(f32)).astype(bf16)
    b_low = (b - b_high.astype(f32)).astype(bf16)
    return mmb(a_high, b_high, ca, cb) + (mmb(a_high, b_low, ca, cb) + mmb(a_low, b_high, ca, cb))


def mmb(a, b, ca, cb):
    return lax.dot_general(
        a.astype(bf16), b.astype(bf16), (((ca,), (cb,)), ((), ())), preferred_element_type=f32
    )


def sigmoid(u):
    return 1.0 / (1.0 + jnp.exp(-u))


def norm_forward(x, gain):
    return x * lax.rsqrt(jnp.mean(x * x, axis=-1, keepdims=True) + norm_eps) * gain


def norm_backward(x, gain, grad):
    rate = lax.rsqrt(jnp.mean(x * x, axis=-1, keepdims=True) + norm_eps)
    unit = x * rate
    grad_gain = jnp.sum(grad * unit, axis=0, keepdims=True)
    scaled = grad * gain
    grad_x = rate * (scaled - unit * jnp.mean(scaled * unit, axis=-1, keepdims=True))
    return grad_x, grad_gain


def blocks_of(array, parity, size):
    block = array.shape[1] // size
    return jnp.concatenate(
        [array[:, i * block : (i + 1) * block] for i in range(parity, size, 2)], axis=1
    )


def keep_send(array, y, size):
    even, odd = blocks_of(array, 0, size), blocks_of(array, 1, size)
    lead = y == 0
    return jnp.where(lead, even, odd), jnp.where(lead, odd, even)


def put_halves(part, index_ref, part_ref, mine_ref, other_ref):
    rows = part.shape[0] // 2
    bit = index_ref[1]
    part_ref[...] = part
    mine_ref[...] = part_ref[pl.ds(pl.multiple_of(bit * rows, rows), rows), :]
    other_ref[...] = part_ref[pl.ds(pl.multiple_of((1 - bit) * rows, rows), rows), :]


def get_total(index_ref, near_ref, far_ref):
    lead = index_ref[1] == 0
    near, far = near_ref[...], far_ref[...]
    return jnp.concatenate([jnp.where(lead, near, far), jnp.where(lead, far, near)], axis=0)


def in_kernel(
    index_ref, stream_ref, gain_ref, w_ref, keep_ref, send_ref, proj_ref, *, level, size
):
    normed = norm_forward(stream_ref[...].astype(f32), gain_ref[level : level + 1, :])
    keep, send = keep_send(normed, index_ref[0], size)
    keep_ref[...] = keep.astype(bf16)
    send_ref[...] = send.astype(bf16).astype(f32)
    proj_ref[...] = mmb(normed, w_ref[...], 1, 0)


def in_sum_kernel(
    index_ref, mid_ref, near_ref, far_ref, gain_ref, w_ref,
    stream_ref, keep_ref, send_ref, proj_ref, *, level, size
):
    stream_ref[...] = mid_ref[...] + get_total(index_ref, near_ref, far_ref)
    in_kernel(
        index_ref, stream_ref, gain_ref, w_ref, keep_ref, send_ref, proj_ref,
        level=level, size=size,
    )


def conv_of(win_ref, taps, length):
    conv = taps[0:1] * win_ref[pl.ds(PAD, length), :]
    for tap in range(1, CONV):
        conv = conv + taps[tap : tap + 1] * win_ref[pl.ds(PAD - tap, length), :]
    return conv


def decay_of(col, row, length):
    rows = lax.broadcasted_iota(jnp.int32, (length, length), 0)
    cols = lax.broadcasted_iota(jnp.int32, (length, length), 1)
    keep = rows >= cols
    ratio = jnp.where(keep, jnp.exp(jnp.where(keep, col - row, 0.0)), 0.0)
    return rows, cols, ratio


def delta_kernel(
    y_ref, proj_ref, before_ref, taps_ref, col_ref, row_ref, beta_ref,
    ow_ref, uw_ref, solve_ref, mix_ref, send_ref, keep_ref, transfer_ref,
    win_ref, offset_ref,
):
    length = proj_ref.shape[0]
    for head in range(col_ref.shape[0]):
        base = head * WIDE
        win_ref[0:PAD, :] = before_ref[:, base : base + QKV]
        win_ref[pl.ds(PAD, length), :] = proj_ref[:, base : base + QKV]
        conv = conv_of(win_ref, taps_ref[:, head * QKV : (head + 1) * QKV].astype(f32), length)
        active = conv * sigmoid(conv)
        q_act = active[:, :DK]
        k_act = active[:, DK : 2 * DK]
        values = active[:, 2 * DK :]
        q = q_act * lax.rsqrt(jnp.sum(q_act * q_act, axis=-1, keepdims=True) + norm_eps)
        q = q * DK ** (-0.5)
        k = k_act * lax.rsqrt(jnp.sum(k_act * k_act, axis=-1, keepdims=True) + norm_eps)
        col = col_ref[head]
        row = row_ref[head]
        beta = beta_ref[head]
        rows, cols, ratio = decay_of(col, row, length)
        key_key = mm(k, k, 1, 1)
        query_key = mm(q, k, 1, 1)
        lower = jnp.where(rows > cols, beta * ratio * key_key, 0.0)
        solve = jnp.where(rows == cols, 1.0, 0.0)
        block = 1
        while block < length:
            here = (
                (rows // (2 * block) == cols // (2 * block))
                & (rows % (2 * block) >= block)
                & (cols % (2 * block) < block)
            )
            part = jnp.where(here, lower, 0.0)
            if block == 1:
                solve = solve - part
            else:
                solve = solve - mm(solve, mm(part, solve, 1, 0), 1, 0)
            block *= 2
        decay = jnp.exp(col)
        right = jnp.concatenate([beta * values, (beta * decay) * k], axis=1)
        uw = mm(solve, right, 1, 0)
        mix = ratio * query_key
        muw = mm(mix, uw, 1, 0)
        last = row[:, length - 1 :]
        ends = mm(uw, jnp.exp(last - col) * k, 0, 0)
        eye = jnp.where(
            lax.broadcasted_iota(jnp.int32, (DK, DK), 0)
            == lax.broadcasted_iota(jnp.int32, (DK, DK), 1),
            1.0,
            0.0,
        )
        transfer = jnp.exp(last) * eye - ends[DV:]
        offset_ref[...] = ends[:DV]
        ow_ref[head] = jnp.concatenate([muw[:, :DV], decay * q - muw[:, DV:]], axis=1)
        uw_ref[head] = uw
        solve_ref[head] = solve
        mix_ref[head] = mix
        transfer_ref[head] = transfer
        y = y_ref[0]
        send_ref[head, 0:DK, :] = transfer
        send_ref[head, DK : DK + HALF, :] = offset_ref[
            pl.ds(pl.multiple_of((1 - y) * HALF, HALF), HALF), :
        ]
        keep_ref[head] = offset_ref[pl.ds(pl.multiple_of(y * HALF, HALF), HALF), :]


def pair_kernel(
    y_ref, own_ref, keep_ref, other_ref, first_t_ref, second_t_ref, first_o_ref, pair_ref
):
    lead = y_ref[0] == 0
    for head in range(own_ref.shape[0]):
        own, other = own_ref[head], other_ref[head, 0:DK, :]
        keep, far = keep_ref[head], other_ref[head, DK : DK + HALF, :]
        first_t, second_t = jnp.where(lead, own, other), jnp.where(lead, other, own)
        first_o, second_o = jnp.where(lead, keep, far), jnp.where(lead, far, keep)
        first_t_ref[head] = first_t
        second_t_ref[head] = second_t
        first_o_ref[head] = first_o
        both = mm(jnp.concatenate([first_t, first_o], axis=0), second_t, 1, 0)
        pair_ref[head, 0:DK, :] = both[:DK]
        pair_ref[head, DK : DK + HALF, :] = both[DK:] + second_o


def window_kernel(near_ref, pair_ref, out_ref):
    for head in range(pair_ref.shape[0]):
        pair = pair_ref[head]
        out_ref[head] = mm(near_ref[head, DK : DK + HALF, :], pair[:DK], 1, 0) + pair[DK:]


def step_kernel(state_ref, pair_ref, out_ref):
    for head in range(state_ref.shape[0]):
        pair = pair_ref[head]
        out_ref[head] = mm(state_ref[head], pair[:DK], 1, 0) + pair[DK:]


def step_back_kernel(state_ref, pair_ref, offset_ref, out_ref):
    for head in range(state_ref.shape[0]):
        transfer = pair_ref[head, 0:DK, :]
        out_ref[head] = mm(state_ref[head], transfer, 1, 1) + offset_ref[head]


def last_kernel(
    y_ref, state_ref, near_ref, transfer_ref, offset_ref, mine_ref, other_ref, *, window
):
    lead = y_ref[0] == 0
    for head in range(state_ref.shape[0]):
        state = state_ref[head]
        if window:
            near = near_ref[head]
            state = mm(state, near[:DK], 1, 0) + near[DK:]
        moved = mm(state, transfer_ref[head], 1, 0) + offset_ref[head]
        mine_ref[head] = jnp.where(lead, state, moved)
        other_ref[head] = jnp.where(lead, moved, state)


def pair_back_kernel(y_ref, keep_ref, other_ref, first_t_ref, second_ref, pair_ref):
    lead = y_ref[0] == 0
    for head in range(keep_ref.shape[0]):
        keep, far = keep_ref[head], other_ref[head]
        first, second = jnp.where(lead, keep, far), jnp.where(lead, far, keep)
        second_ref[head] = second
        pair_ref[head] = first + mm(second, first_t_ref[head], 1, 1)


def last_back_kernel(y_ref, state_ref, transfer_ref, offset_ref, mine_ref, other_ref):
    lead = y_ref[0] == 0
    for head in range(state_ref.shape[0]):
        state = state_ref[head]
        moved = mm(state, transfer_ref[head], 1, 1) + offset_ref[head]
        mine_ref[head] = jnp.where(lead, moved, state)
        other_ref[head] = jnp.where(lead, state, moved)


def halves(y, mine, other):
    lead = y == 0
    return jnp.concatenate(
        [jnp.where(lead, mine, other), jnp.where(lead, other, mine)], axis=0
    )


def out_kernel(
    y_ref, mine_ref, other_ref, ow_ref, proj_ref, gain_ref, w_ref,
    state_ref, outputs_ref, gated_ref, near_ref, far_ref, part_ref, *, level,
):
    pieces = []
    for head in range(ow_ref.shape[0]):
        state = halves(y_ref[0], mine_ref[head], other_ref[head])
        state_ref[head] = state
        ow = ow_ref[head]
        outputs = ow[:, :DV] + mm(ow[:, DV:], state, 1, 1)
        outputs_ref[:, head * DV : (head + 1) * DV] = outputs
        z = proj_ref[:, head * WIDE + QKV : (head + 1) * WIDE]
        pieces.append((norm_forward(outputs, gain_ref[level : level + 1, :]) * (z * sigmoid(z))).astype(bf16))
    gated = jnp.concatenate(pieces, axis=1)
    gated_ref[...] = gated.astype(f32)
    put_halves(mmb(gated, w_ref[...], 1, 0), y_ref, part_ref, near_ref, far_ref)


def ffn_kernel(
    index_ref, stream_ref, near_ref, far_ref, gain_ref, wg_ref, wu_ref, wd_ref,
    mid_ref, keep_ref, send_ref, gate_ref, up_ref, mine_ref, other_ref, part_ref,
    *, level, size,
):
    mid = stream_ref[...].astype(f32) + get_total(index_ref, near_ref, far_ref)
    mid_ref[...] = mid
    normed = norm_forward(mid, gain_ref[level : level + 1, :])
    keep, send = keep_send(normed, index_ref[0], size)
    keep_ref[...] = keep.astype(bf16)
    half = mid.shape[1] // 2
    send_ref[:, :half] = send.astype(bf16).astype(f32)
    normed = normed.astype(bf16)
    gate = mmb(normed, wg_ref[...], 1, 0)
    up = mmb(normed, wu_ref[...], 1, 0)
    gate_ref[...] = gate
    up_ref[...] = up
    hidden = (gate * sigmoid(gate) * up).astype(bf16)
    send_ref[:, half:] = hidden.astype(f32)
    put_halves(mmb(hidden, wd_ref[...], 1, 0), index_ref, part_ref, mine_ref, other_ref)


def sum_kernel(index_ref, mid_ref, near_ref, far_ref, out_ref):
    out_ref[...] = (mid_ref[...] + get_total(index_ref, near_ref, far_ref)).astype(bf16)


def ffn_back_kernel(
    index_ref, grad_ref, gate_ref, up_ref, wg_ref, wu_ref, wd_ref,
    keep_ref, send_ref, mine_ref, other_ref, part_ref, *, size,
):
    back = grad_ref[...].astype(bf16)
    keep, send = keep_send(back.astype(f32), index_ref[0], size)
    keep_ref[...] = keep.astype(bf16)
    hidden = mmb(back, wd_ref[...], 1, 1)
    gate, up = gate_ref[...], up_ref[...]
    rate = sigmoid(gate)
    gu = (hidden * (gate * rate)).astype(bf16)
    gg = (hidden * up * (rate * (1.0 + gate * (1.0 - rate)))).astype(bf16)
    width = gate.shape[1]
    send_ref[:, : 2 * width] = jnp.concatenate([gg.astype(f32), gu.astype(f32)], axis=1)
    send_ref[:, 2 * width :] = send
    part = mmb(gg, wg_ref[...], 1, 1) + mmb(gu, wu_ref[...], 1, 1)
    put_halves(part, index_ref, part_ref, mine_ref, other_ref)


def out_back_kernel(
    y_ref, grad_ref, near_ref, far_ref, mid_ref, gain_ref, w_ref, outputs_ref, proj_ref,
    out_gain_ref, ow_ref,
    next_ref, back_keep_ref, back_send_ref, do_ref, dz_ref, dgain_ref, dout_gain_ref,
    send_ref, keep_ref,
    local_ref, *, level, size,
):
    grad_mid, grad_gain = norm_backward(
        mid_ref[...], gain_ref[level : level + 1, :], get_total(y_ref, near_ref, far_ref)
    )
    dgain_ref[...] = grad_gain
    grad = grad_ref[...].astype(f32) + grad_mid
    next_ref[...] = grad
    back = grad.astype(bf16)
    back_keep, back_send = keep_send(back.astype(f32), y_ref[0], size)
    back_keep_ref[...] = back_keep.astype(bf16)
    back_send_ref[...] = back_send
    gated = mmb(back, w_ref[...], 1, 1)
    gain = out_gain_ref[level : level + 1, :]
    total_gain = jnp.zeros_like(gain)
    y = y_ref[0]
    for head in range(ow_ref.shape[0]):
        span = slice(head * DV, (head + 1) * DV)
        outputs = outputs_ref[:, span]
        z = proj_ref[:, head * WIDE + QKV : (head + 1) * WIDE]
        rate = sigmoid(z)
        grad_h = gated[:, span]
        grad_n = grad_h * (z * rate)
        dz_ref[:, span] = (
            grad_h * norm_forward(outputs, gain) * (rate * (1.0 + z * (1.0 - rate)))
        )
        grad_o, gain_part = norm_backward(outputs, gain, grad_n)
        total_gain = total_gain + gain_part
        do_ref[:, span] = grad_o
        local_ref[...] = mm(grad_o, ow_ref[head][:, DV:], 0, 0)
        send_ref[head] = local_ref[pl.ds(pl.multiple_of((1 - y) * HALF, HALF), HALF), :]
        keep_ref[head] = local_ref[pl.ds(pl.multiple_of(y * HALF, HALF), HALF), :]
    dout_gain_ref[...] = total_gain


def delta_back_kernel(
    y_ref, mine_ref, other_ref, state_ref, uw_ref, solve_ref, mix_ref, do_ref,
    proj_ref, before_ref, taps_ref, col_ref, row_ref, beta_ref,
    dconv_ref, dtaps_ref, edge_ref,
    win_ref,
):
    length = proj_ref.shape[0]
    for head in range(col_ref.shape[0]):
        base = head * WIDE
        win_ref[0:PAD, :] = before_ref[:, base : base + QKV]
        win_ref[pl.ds(PAD, length), :] = proj_ref[:, base : base + QKV]
        taps = taps_ref[:, head * QKV : (head + 1) * QKV].astype(f32)
        conv = conv_of(win_ref, taps, length)
        rate = sigmoid(conv)
        active = conv * rate
        q_act = active[:, :DK]
        k_act = active[:, DK : 2 * DK]
        q_rate = lax.rsqrt(jnp.sum(q_act * q_act, axis=-1, keepdims=True) + norm_eps)
        k_rate = lax.rsqrt(jnp.sum(k_act * k_act, axis=-1, keepdims=True) + norm_eps)
        q_unit = q_act * q_rate
        k = k_act * k_rate
        q = q_unit * DK ** (-0.5)
        col = col_ref[head]
        row = row_ref[head]
        beta = beta_ref[head]
        rows, cols, ratio = decay_of(col, row, length)
        decay = jnp.exp(col)
        to_end = jnp.exp(row[:, length - 1 :] - col)
        state = state_ref[head]
        grad_end = halves(y_ref[0], mine_ref[head], other_ref[head])
        uw = uw_ref[head]
        grad_o = do_ref[:, head * DV : (head + 1) * DV]
        values_new = uw[:, :DV] - mmb(uw[:, DV:], state, 1, 1)
        grad_new = mmb(mix_ref[head], grad_o, 0, 0) + mmb(to_end * k, grad_end, 1, 1)
        grad_right = mmb(solve_ref[head], grad_new, 0, 0)
        grad_mix = jnp.where(rows >= cols, ratio * mmb(grad_o, values_new, 1, 1), 0.0)
        grad_low = jnp.where(
            rows > cols, -(beta * ratio) * mmb(grad_right, values_new, 1, 1), 0.0
        )
        grad_q = decay * mmb(grad_o, state, 1, 0) + mmb(grad_mix, k, 1, 0)
        grad_k = to_end * mmb(values_new, grad_end, 1, 0)
        grad_k = grad_k - (beta * decay) * mmb(grad_right, state, 1, 0)
        grad_k = grad_k + mmb(grad_low, k, 1, 0) + mmb(grad_low, k, 0, 0)
        grad_k = grad_k + mmb(grad_mix, q, 0, 0)
        grad_v = beta * grad_right
        grad_qa = (DK ** (-0.5)) * q_rate * (
            grad_q - q_unit * jnp.sum(grad_q * q_unit, axis=-1, keepdims=True)
        )
        grad_ka = k_rate * (grad_k - k * jnp.sum(grad_k * k, axis=-1, keepdims=True))
        grad_conv = jnp.concatenate([grad_qa, grad_ka, grad_v], axis=1) * (
            rate * (1.0 + conv * (1.0 - rate))
        )
        span = slice(head * QKV, (head + 1) * QKV)
        dconv_ref[:, span] = grad_conv
        edge_ref[:, span] = grad_conv[0:PAD]
        for tap in range(CONV):
            dtaps_ref[tap : tap + 1, span] = jnp.sum(
                grad_conv * win_ref[pl.ds(PAD - tap, length), :], axis=0, keepdims=True
            )


def in_back_kernel(
    index_ref, dconv_ref, after_ref, taps_ref, dz_ref, w_ref,
    gp_ref, mine_ref, other_ref, ext_ref, part_ref,
):
    length = dconv_ref.shape[0]
    ext_ref[pl.ds(0, length), :] = dconv_ref[...]
    ext_ref[pl.ds(length, PAD), :] = after_ref[...]
    taps = taps_ref[...].astype(f32)
    total = taps[0:1] * ext_ref[pl.ds(0, length), :]
    for tap in range(1, CONV):
        total = total + taps[tap : tap + 1] * ext_ref[pl.ds(tap, length), :]
    pieces = []
    for head in range(total.shape[1] // QKV):
        pieces.append(total[:, head * QKV : (head + 1) * QKV])
        pieces.append(dz_ref[:, head * DV : (head + 1) * DV])
    grad_proj = jnp.concatenate(pieces, axis=1).astype(bf16)
    gp_ref[...] = grad_proj.astype(f32)
    put_halves(mmb(grad_proj, w_ref[...], 1, 1), index_ref, part_ref, mine_ref, other_ref)


def norm_back_kernel(
    index_ref, grad_ref, near_ref, far_ref, stream_ref, gain_ref, out_ref, dgain_ref, *, level
):
    grad_x, grad_gain = norm_backward(
        stream_ref[...].astype(f32),
        gain_ref[level : level + 1, :],
        get_total(index_ref, near_ref, far_ref),
    )
    out_ref[...] = grad_ref[...] + grad_x
    dgain_ref[...] = grad_gain


def weight_block_kernel(
    n2_ref, own_ref, own_far_ref, ffn_ref, ffn_far_ref, back_ref, mid_ref, mid_far_ref,
    gated_ref, gated_far_ref, out_ref,
):
    half = back_ref.shape[1]
    width = own_ref.shape[1] - half
    both = 2 * width
    out_ref[:, :both] = mmb(n2_ref[...], ffn_ref[:, :both], 0, 0) + mmb(
        own_far_ref[:, :half], ffn_far_ref[:, :both], 0, 0
    )
    out_ref[:, both : both + width] = mmb(back_ref[...], own_ref[:, half:], 0, 0) + mmb(
        ffn_far_ref[:, both:], own_far_ref[:, half:], 0, 0
    )
    out_ref[:, both + width :] = mmb(mid_ref[...], gated_ref[...], 0, 0) + mmb(
        mid_far_ref[...], gated_far_ref[...], 0, 0
    )


def weight_in_kernel(a_ref, b_ref, a_far_ref, b_far_ref, out_ref):
    out_ref[...] = mmb(a_ref[...], b_ref[...], 0, 0) + mmb(a_far_ref[...], b_far_ref[...], 0, 0)


def shift(array, axis, by):
    length = lax.axis_size(axis)
    pairs = [(i, i + by) for i in range(length) if 0 <= i + by < length]
    return lax.ppermute(array, axis, pairs)


def swap(array, axis, bit):
    length = lax.axis_size(axis)
    return lax.ppermute(array, axis, [(i, i ^ bit) for i in range(length)])


def head_total(mine, other, name):
    with jax.named_scope("x_" + name):
        total = mine + swap(other, "head", 1)
        step = 2
        while step < lax.axis_size("head"):
            total = total + swap(total, "head", step)
            step *= 2
        return total, swap(total, "head", 1)


def after(array, mark):
    return lax.optimization_barrier((array, mark))[0]


def full_sum(array, axis):
    step = 1
    while step < lax.axis_size(axis):
        array = array + swap(array, axis, step)
        step *= 2
    return array


def outer_scatter(array):
    size = lax.axis_size("seq")
    groups = [[2 * o + p for o in range(size // 2)] for p in range(2)]
    return lax.psum_scatter(
        array, "seq", scatter_dimension=0, tiled=True, axis_index_groups=groups
    )


def prefix(local, transfer, y, level):
    send, keep = local
    heads = keep.shape[0]
    square = shape_of((heads, DK, DK))
    half = shape_of((heads, HALF, DK))
    outer = lax.axis_size("seq") // 2
    far = swap(send, "seq", 1)
    first_t, second_t, first_o, pair = call(
        pair_kernel,
        [square, square, half, shape_of((heads, DK + HALF, DK))],
        [y, transfer, keep, far],
        f"pair_{level}",
    )
    if outer == 4:
        near = shift(pair, "seq", 2)
        (moved,) = call(window_kernel, [half], [near, pair], f"window_{level}")
        state = shift(moved, "seq", 4)
    else:
        near = pair
        state = shift(pair[:, DK:], "seq", 2)
        for hop in range(outer - 2):
            (moved,) = call(step_kernel, [half], [state, pair], f"step_{level}_{hop}")
            state = shift(moved, "seq", 2)
    mine, other = call(
        functools.partial(last_kernel, window=outer == 4),
        [half, half],
        [y, state, near, first_t, first_o],
        f"last_{level}",
    )
    return mine, swap(other, "seq", 1), first_t, second_t, pair, near


def suffix(send, keep, kept, y, level):
    heads = keep.shape[0]
    half = shape_of((heads, HALF, DK))
    outer = lax.axis_size("seq") // 2
    far = swap(send, "seq", 1)
    second_o, pair_o = call(
        pair_back_kernel, [half, half], [y, keep, far, kept["first_t"]], f"pair_back_{level}"
    )
    state = shift(pair_o, "seq", -2)
    mark = state
    for hop in range(outer - 2):
        (moved,) = call(
            step_back_kernel, [half], [state, kept["pair"], pair_o], f"step_back_{level}_{hop}"
        )
        state = shift(moved, "seq", -2)
    mine, other = call(
        last_back_kernel,
        [half, half],
        [y, state, kept["second_t"], second_o],
        f"last_back_{level}",
    )
    return mine, swap(other, "seq", 1), mark


def layer_forward(start, shared, level, y):
    col, row, beta, gain_one, w_in, taps, out_gain, w_out, gain_two, w_gate, w_up, w_down = shared
    length, width = start[0].shape
    heads = col.shape[1]
    proj_width = w_in.shape[2]
    hidden_width = w_gate.shape[2]
    value_width = heads * DV
    size = lax.axis_size("seq")
    half_width = width // 2
    rows = shape_of((length // 2, width))
    whole = pltpu.VMEM((length, width), f32)
    kept_half = [shape_of((length, half_width), bf16), shape_of((length, half_width))]
    if len(start) == 1:
        stream = start[0]
        normed, normed_send, proj = call(
            functools.partial(in_kernel, level=level, size=size),
            kept_half + [shape_of((length, proj_width))],
            [y, stream, gain_one, (w_in, level)],
            f"in_{level}",
        )
    else:
        stream, normed, normed_send, proj = call(
            functools.partial(in_sum_kernel, level=level, size=size),
            [shape_of((length, width))] + kept_half + [shape_of((length, proj_width))],
            [y, *start, gain_one, (w_in, level)],
            f"in_{level}",
        )
    before = shift(proj[length - PAD :], "seq", 1)
    square = shape_of((heads, DK, DK))
    wide = shape_of((heads, length, DV + DK))
    inner = shape_of((heads, length, length))
    half = shape_of((heads, HALF, DK))
    ow, uw, solve, mix, send, keep, transfer = call(
        delta_kernel,
        [wide, wide, inner, inner, shape_of((heads, DK + HALF, DK)), half, square],
        [y, proj, before, (taps, level), (col, level), (row, level), (beta, level)],
        f"delta_{level}",
        [pltpu.VMEM((length + PAD, QKV), f32), pltpu.VMEM((DV, DK), f32)],
    )
    mine, other, first_t, second_t, pair, _ = prefix((send, keep), transfer, y, level)
    incoming, outputs, gated, near, far = call(
        functools.partial(out_kernel, level=level),
        [
            shape_of((heads, DV, DK)),
            shape_of((length, value_width)),
            shape_of((length, value_width)),
            rows,
            rows,
        ],
        [y, mine, other, ow, proj, out_gain, (w_out, level)],
        f"out_{level}",
        [whole],
    )
    total = head_total(near, far, f"out_{level}")
    mid, normed_two, ffn_send, gate, up, near, far = call(
        functools.partial(ffn_kernel, level=level, size=size),
        [
            shape_of((length, width)),
            shape_of((length, half_width), bf16),
            shape_of((length, half_width + hidden_width)),
            shape_of((length, hidden_width)),
            shape_of((length, hidden_width)),
            rows,
            rows,
        ],
        [y, stream, *total, gain_two, (w_gate, level), (w_up, level), (w_down, level)],
        f"ffn_{level}",
        [whole],
    )
    total = head_total(near, far, f"ffn_{level}")
    stored = dict(
        stream=stream, normed=normed, proj=proj, before=before, ow=ow, uw=uw, solve=solve,
        mix=mix, first_t=first_t, second_t=second_t, pair=pair, incoming=incoming,
        outputs=outputs, gated=gated, mid=mid, normed_two=normed_two, gate=gate, up=up,
        ffn_send=ffn_send, normed_far=swap(normed_send, "seq", 1),
        gated_far=swap(gated, "seq", 1), ffn_far=swap(ffn_send, "seq", 1),
    )
    return (mid, *total), stored


def layer_backward(grad, shared, level, kept, y, pending):
    col, row, beta, gain_one, w_in, taps, out_gain, w_out, gain_two, w_gate, w_up, w_down = shared
    length, width = grad.shape
    heads = col.shape[1]
    proj_width = w_in.shape[2]
    hidden_width = w_gate.shape[2]
    value_width = heads * DV
    qkv_width = heads * QKV
    size = lax.axis_size("seq")
    half_width = width // 2
    rows = shape_of((length // 2, width))
    whole = pltpu.VMEM((length, width), f32)
    back, back_send, near, far = call(
        functools.partial(ffn_back_kernel, size=size),
        [
            shape_of((length, half_width), bf16),
            shape_of((length, 2 * hidden_width + half_width)),
            rows,
            rows,
        ],
        [y, grad, kept["gate"], kept["up"], (w_gate, level), (w_up, level), (w_down, level)],
        f"ffn_back_{level}",
        [whole],
    )
    with jax.named_scope(f"x_ffn_far_{level}"):
        back_far = swap(back_send, "seq", 1)
    total = head_total(near, far, f"ffn_back_{level}")
    if pending is not None:
        pending = pending(near)
    half = shape_of((heads, HALF, DK))
    grad, mid_back, mid_send, grad_o, grad_z, dgain_two, dout_gain, send, keep = call(
        functools.partial(out_back_kernel, level=level, size=size),
        [
            shape_of((length, width)),
            shape_of((length, half_width), bf16),
            shape_of((length, half_width)),
            shape_of((length, value_width)),
            shape_of((length, value_width)),
            shape_of((1, width)),
            shape_of((1, DV)),
            half,
            half,
        ],
        [
            y, grad, *total, kept["mid"], gain_two, (w_out, level), kept["outputs"],
            kept["proj"], out_gain, kept["ow"],
        ],
        f"out_back_{level}",
        [pltpu.VMEM((DV, DK), f32)],
    )
    with jax.named_scope(f"x_mid_far_{level}"):
        mid_far = swap(mid_send, "seq", 1)
    mine, other, mark = suffix(send, keep, kept, y, level)
    (block_weights,) = call(
        weight_block_kernel,
        [shape_of((half_width, 3 * hidden_width + value_width))],
        [
            kept["normed_two"], kept["ffn_send"], kept["ffn_far"], back_send,
            after(back_far, mark), back, mid_back, mid_far, kept["gated"], kept["gated_far"],
        ],
        f"weights_block_{level}",
    )
    block_weights = outer_scatter(block_weights)
    dconv, dtaps, edge = call(
        delta_back_kernel,
        [
            shape_of((length, qkv_width)),
            shape_of((CONV, qkv_width)),
            shape_of((PAD, qkv_width)),
        ],
        [
            y, mine, other, kept["incoming"], kept["uw"], kept["solve"], kept["mix"], grad_o,
            kept["proj"], kept["before"], (taps, level), (col, level), (row, level),
            (beta, level),
        ],
        f"delta_back_{level}",
        [pltpu.VMEM((length + PAD, QKV), f32)],
    )
    grad_proj, near, far = call(
        in_back_kernel,
        [shape_of((length, proj_width)), rows, rows],
        [y, dconv, shift(edge, "seq", -1), (taps, level), grad_z, (w_in, level)],
        f"in_back_{level}",
        [pltpu.VMEM((length + PAD, qkv_width), f32), whole],
    )
    with jax.named_scope(f"x_in_far_{level}"):
        proj_far = swap(grad_proj, "seq", 1)

    def finish(mark):
        held = proj_far if mark is None else after(proj_far, mark)
        (in_weights,) = call(
            weight_in_kernel,
            [shape_of((half_width, proj_width))],
            [kept["normed"], grad_proj, kept["normed_far"], held],
            f"weights_in_{level}",
        )
        return outer_scatter(in_weights)

    total = head_total(near, far, f"in_back_{level}")
    grad, dgain_one = call(
        functools.partial(norm_back_kernel, level=level),
        [shape_of((length, width)), shape_of((1, width))],
        [y, grad, *total, kept["stream"], gain_one],
        f"norm_back_{level}",
    )
    return grad, (block_weights, dtaps, dgain_one, dout_gain, dgain_two), finish, pending


def body(
    tokens,
    cotangent,
    gate_code,
    beta_code,
    norm1_gain,
    weight_in,
    conv_weight,
    out_gain,
    weight_out,
    norm2_gain,
    weight_gate,
    weight_up,
    weight_down,
):
    y = jnp.stack([lax.axis_index("seq") % 2, lax.axis_index("head") % 2]).astype(jnp.int32)
    logdecay = -gate_code.astype(f32) * gate_unit
    beta_rate = jnp.transpose(beta_code.astype(f32) * beta_unit, (0, 2, 1))
    cumulated = jnp.transpose(jnp.cumsum(logdecay, axis=1), (0, 2, 1))
    shared = (
        cumulated[:, :, :, None],
        cumulated[:, :, None, :],
        beta_rate[:, :, :, None],
        norm1_gain,
        weight_in,
        conv_weight,
        out_gain,
        weight_out,
        norm2_gain,
        weight_gate,
        weight_up,
        weight_down,
    )
    start = (tokens,)
    kept = []
    for level in range(STACK_LEVELS):
        start, stored = layer_forward(start, shared, level, y)
        kept.append(stored)
    grad = cotangent
    parts = [None] * STACK_LEVELS
    in_weights = [None] * STACK_LEVELS
    finish = None
    for level in reversed(range(STACK_LEVELS)):
        grad, parts[level], finish, done = layer_backward(
            grad, shared, level, kept[level], y, finish
        )
        if done is not None:
            in_weights[level + 1] = done
    in_weights[0] = finish(None)
    (activations,) = call(sum_kernel, [shape_of(tokens.shape, bf16)], [y, *start], "finish")
    hidden_width = weight_gate.shape[2]
    block = [part[0] for part in parts]

    def join(pick):
        return jnp.stack([pick(piece) for piece in block])

    grad_gate = join(lambda piece: piece[:, :hidden_width])
    grad_up = join(lambda piece: piece[:, hidden_width : 2 * hidden_width])
    grad_down = join(lambda piece: piece[:, 2 * hidden_width : 3 * hidden_width].T)
    grad_out = join(lambda piece: piece[:, 3 * hidden_width :].T)
    grad_in = jnp.stack(in_weights)
    qkv_width = conv_weight.shape[2]
    width = tokens.shape[1]
    out_gain_part = full_sum(jnp.concatenate([part[3] for part in parts], axis=0), "head")
    small = jnp.concatenate(
        [part[1].reshape(1, -1) for part in parts]
        + [part[2] for part in parts]
        + [part[4] for part in parts]
        + [out_gain_part.reshape(1, -1)],
        axis=1,
    )
    small = full_sum(small, "seq")[0]
    sizes = [STACK_LEVELS * CONV * qkv_width, STACK_LEVELS * width, STACK_LEVELS * width]
    conv_grad = small[: sizes[0]].reshape(STACK_LEVELS, CONV, qkv_width)
    gain_one_grad = small[sizes[0] : sizes[0] + sizes[1]].reshape(STACK_LEVELS, width)
    gain_two_grad = small[sizes[0] + sizes[1] : sum(sizes)].reshape(STACK_LEVELS, width)
    out_gain_grad = small[sum(sizes) :].reshape(STACK_LEVELS, DV)
    return (
        activations,
        grad,
        gain_one_grad,
        grad_in,
        conv_grad,
        out_gain_grad,
        grad_out,
        gain_two_grad,
        grad_gate,
        grad_up,
        grad_down,
    )


def solution(mesh):
    in_specs = (
        P("seq", None),
        P("seq", None),
        P(None, "seq", "head"),
        P(None, "seq", "head"),
        P(),
        P(None, None, "head"),
        P(None, None, "head"),
        P(),
        P(None, "head", None),
        P(),
        P(None, None, "head"),
        P(None, None, "head"),
        P(None, "head", None),
    )
    out_specs = (
        P("seq", None),
        P("seq", None),
        P(),
        P(None, "seq", "head"),
        P(None, None, "head"),
        P(),
        P(None, "head", "seq"),
        P(),
        P(None, "seq", "head"),
        P(None, "seq", "head"),
        P(None, "head", "seq"),
    )
    return jax.shard_map(body, mesh=mesh, in_specs=in_specs, out_specs=out_specs, check_vma=False)
```

time: 731 us -> 698 us (0.955)
  waiting for transfers between devices: 348 us -> 405 us
  local copies, waits for them, and re-layouts: 107 us -> 51.1 us
  other arithmetic: 22.4 us -> 9.21 us
  Pallas kernels: 142 us -> 129 us
    reduce_scatter x4, waiting for transfers between devices: 54.8 us -> 108 us  [outer_scatter(): lax.psum_scatter(array, 'seq', scatter_dimension=0, tiled=True, axis_inde...]
    ppermute x43 -> x49, waiting for transfers between devices: 195 us -> 220 us  [swap(): return lax.ppermute(array, axis, [(i, i ^ bit) for i in range(length)])]
    ppermute x16 -> x14, waiting for transfers between devices: 98 us -> 75.9 us  [shift(): return lax.ppermute(array, axis, pairs)]
    dynamic_slice x13 -> x0, local copies, waits for them, and re-layouts: 17.2 us -> none  [the longest x5 11.2 us: blocks_of(): lax.dynamic_index_in_dim(parts, parity, 2, keepdims=False)]
    slice x18 -> x0, local copies, waits for them, and re-layouts: 16.9 us -> none  [the longest x1 3.4 us: body(): weight_gate[level]]
    pallas_call x39 -> x37, Pallas kernels: 142 us -> 129 us  [call(): pl.pallas_call(body, grid=(1,), out_shape=tuple(outs), in_specs=specs, ou...]
    squeeze x4 -> x0, local copies, waits for them, and re-layouts: 9.87 us -> none  [the longest x1 5.89 us: body(): weight_in[level]]
    unnamed x185 -> x155, local copies, waits for them, and re-layouts: 46 us -> 38.5 us
  transfers between devices with their start and end apart: 63 -> 67, of which waited for: 51 -> 54; matrix products, arithmetic and copies ran while one was open for 12% -> 3% of each run, Pallas kernels for 10% -> 7%
where the time goes in v2:
time: 698 us; the launch traced here: 696 us
  waiting for transfers between devices  405 us (58%)
  Pallas kernels  129 us (18%)
  starting transfers between devices  87.8 us (13%)
  local copies, waits for them, and re-layouts  51.1 us (7%)
  between operations  14.5 us (2%)
  other arithmetic  9.21 us (1%)
    ppermute x49, waiting for transfers between devices, swap(): return lax.ppermute(array, axis, [(i, i ^ bit) for i in range(length)])  220 us
    pallas_call x37, Pallas kernels, call(): pl.pallas_call(body, grid=(1,), out_shape=tuple(outs), in_specs=specs, ou...  129 us
    reduce_scatter x4, waiting for transfers between devices, outer_scatter(): lax.psum_scatter(array, 'seq', scatter_dimension=0, tiled=True, axis_inde...  108 us
    ppermute x14, waiting for transfers between devices, shift(): return lax.ppermute(array, axis, pairs)  75.9 us
    ppermute x49, starting transfers between devices, swap(): return lax.ppermute(array, axis, [(i, i ^ bit) for i in range(length)])  49.4 us
    unnamed x155, local copies, waits for them, and re-layouts  38.5 us
    ppermute x14, starting transfers between devices, shift(): return lax.ppermute(array, axis, pairs)  38.2 us
  transfers between devices with their start and end apart: 67, of which 54 were waited for; matrix products, arithmetic and copies ran while one was open for 3% of the time, Pallas kernels for 7%

profile of v2, /device:TPU:0, one launch (start us, length us, event | category | flops | bytes accessed | tf_op | source)
XLA Modules:
  0.0 696.1 jit_solution(15120951387181778951)
XLA Ops:
  20.0 7.8 %delta_0.1 = (f32[2,128,384]{2,1,0:T(8,128)}, f32[2,128,384]{2,1,0:T(8,128)}, f32[2,128,128]{2,1,0:T(8,128)}, f32[2,128,128]{2,1,0:T(8,128)}, f32[2,256,128]{2,1...) custom-call(s32[2]{0:T(128)} %pad_add_fusion.index_ref.y_ref, f32[128,1536]{1,0:T(8,128)} %get-tuple-element.121.proj_ref, ...), custom_call_target="tpu_custom_call" | custom-call | tf_op jit(solution)/shard_map/k_delta_0/delta_0/pallas_call | solution.py:47
  29.7 6.1 collective-permute-done.1.other_ref
  73.6 6.8 collective-permute-done.6
  97.6 7.1 %collective-permute-done.9 = f32[64,1024]{1,0:T(8,128)S(1)} collective-permute-done((f32[64,1024]{1,0:T(8,128)S(1)}, f32[64,1024]{1,0:T(8,128)S(1)}, u32[]{:S(2)}, u32[]{:S(2)}) %collective-permute-start.9) | collective-permute-done | bytes 262176 | tf_op jit(solution)/shard_map/x_ffn_0/ppermute | solution.py:522
  117.4 7.8 %delta_1.1 = (f32[2,128,384]{2,1,0:T(8,128)}, f32[2,128,384]{2,1,0:T(8,128)}, f32[2,128,128]{2,1,0:T(8,128)}, f32[2,128,128]{2,1,0:T(8,128)}, f32[2,256,128]{2,1...) custom-call(s32[2]{0:T(128)} %pad_add_fusion.index_ref.y_ref, f32[128,1536]{1,0:T(8,128)} %get-tuple-element.137.proj_ref, ...), custom_call_target="tpu_custom_call" | custom-call | tf_op jit(solution)/shard_map/k_delta_1/delta_1/pallas_call | solution.py:47
  128.1 6.0 collective-permute-done.12.other_ref
  173.0 6.8 collective-permute-done.17
  195.9 6.8 collective-permute-done.23
  218.7 6.6 collective-permute-done.26.state_ref
  229.2 5.8 collective-permute-done.27.state_ref
  238.9 5.8 collective-permute-done.28.state_ref
  272.7 6.9 collective-permute-done.32
  303.1 6.8 collective-permute-done.35
  326.3 11.7 %collective-permute-done.38.state_ref = f32[2,128,128]{2,1,0:T(8,128)S(1)} collective-permute-done((f32[2,128,128]{2,1,0:T(8,128)}, f32[2,128,128]{2,1,0:T(8,128)S(1)}, u32[]{:S(2)}, u32[]{:S(2)}) %collective-permute-start.38) | collective-permute-done | bytes 131104 | tf_op jit(solution)/shard_map/ppermute | solution.py:517
  341.8 14.4 %collective-permute-done.39.state_ref = f32[2,128,128]{2,1,0:T(8,128)S(1)} collective-permute-done((f32[2,128,128]{2,1,0:T(8,128)}, f32[2,128,128]{2,1,0:T(8,128)S(1)}, u32[]{:S(2)}, u32[]{:S(2)}) %collective-permute-start.39) | collective-permute-done | bytes 131104 | tf_op jit(solution)/shard_map/ppermute | solution.py:517
  360.1 6.8 collective-permute-done.40.state_ref
  392.7 20.2 %collective-permute-done.51.a_far_ref = f32[128,512]{1,0:T(8,128)S(1)} collective-permute-done((f32[128,512]{1,0:T(8,128)S(1)}, f32[128,512]{1,0:T(8,128)S(1)}, u32[]{:S(2)}, u32[]{:S(2)}) %collective-permute-start.51) | collective-permute-done | bytes 262176 | tf_op jit(solution)/shard_map/ppermute | solution.py:522
  423.6 33.6 %collective-permute-done.59 = f32[128,1216]{0,1:T(8,128)S(1)} collective-permute-done((f32[128,1216]{0,1:T(8,128)S(1)}, f32[128,1216]{0,1:T(8,128)S(1)}, u32[]{:S(2)}, u32[]{:S(2)}) %collective-permute-start.59) | collective-permute-done | bytes 622624 | tf_op jit(solution)/shard_map/ppermute | solution.py:522
  463.7 6.3 weights_block_1.1
  475.5 33.6 %collective-permute-done.55 = f32[128,1216]{0,1:T(8,128)S(1)} collective-permute-done((f32[128,1216]{0,1:T(8,128)S(1)}, f32[128,1216]{0,1:T(8,128)S(1)}, u32[]{:S(2)}, u32[]{:S(2)}) %collective-permute-start.55) | collective-permute-done | bytes 622624 | tf_op jit(solution)/shard_map/ppermute | solution.py:522
  514.9 6.3 weights_block_0.1
  534.0 7.3 %collective-permute-done.44 = f32[64,1024]{1,0:T(8,128)S(1)} collective-permute-done((f32[64,1024]{1,0:T(8,128)S(1)}, f32[64,1024]{1,0:T(8,128)S(1)}, u32[]{:S(2)}, u32[]{:S(2)}) %collective-permute-start.44) | collective-permute-done | bytes 262176 | tf_op jit(solution)/shard_map/x_in_back_0/ppermute | solution.py:522
  572.6 10.2 %reduce-scatter.11.cloned.1.call-done = f32[128,2624]{1,0:T(8,128)} async-done(((f32[512,2624]{1,0:T(8,128)}), f32[128,2624]{1,0:T(8,128)}) %reduce-scatter.11.cloned.1.call-update) | async-done | bytes 1343504 | tf_op jit(solution)/shard_map/reduce_scatter | solution.py:550
  585.4 98.1 %reduce-scatter.9.cloned.1.call-done = f32[128,2624]{1,0:T(8,128)} async-done(((f32[512,2624]{1,0:T(8,128)}), f32[128,2624]{1,0:T(8,128)}) %reduce-scatter.9.cloned.1.call-update) | async-done | bytes 1343504 | tf_op jit(solution)/shard_map/reduce_scatter | solution.py:550
  (358 shorter events, 345.8 us)
Async XLA Ops:
  7.2 562.8 %reduce-scatter.7.cloned.1.call-start = ((), (), s32[]{:S(2)}) async-start(), calls=%async_computation.5 | async-start | bytes 3932160 | tf_op jit(solution)/shard_map/reduce_scatter | solution.py:550
  96.1 8.6 %collective-permute-start.9 = (f32[64,1024]{1,0:T(8,128)S(1)}, f32[64,1024]{1,0:T(8,128)S(1)}, u32[]{:S(2)}, u32[]{:S(2)}) collective-permute-start(f32[64,1024]{1,0:T(8,128)S(1)} %add.82), channel_id=1, source_target_pairs={{0,2},{1,3},{2,0},{3,1},{4,6},{5,7},{6,4},{7,5},{8,10},{9,11},{10,... | collective-permute-start | bytes 786440 | tf_op jit(solution)/shard_map/x_ffn_0/ppermute | solution.py:522
  125.2 8.9 %collective-permute-start.12 = (f32[2,256,128]{2,1,0:T(8,128)}, f32[2,256,128]{2,1,0:T(8,128)S(1)}, u32[]{:S(2)}, u32[]{:S(2)}) collective-permute-start(f32[2,256,128]{2,1,0:T(8,128)} %get-tuple-element.140), channel_id=1, source_target_pairs={{0,4},{4,0},{8,12},{12,8},{16,20},{20,16},{24,28},{28,24},{1,5},{5... | collective-permute-start | bytes 786440 | tf_op jit(solution)/shard_map/ppermute | solution.py:522
  136.9 9.3 %collective-permute-start.13 = (f32[2,256,128]{2,1,0:T(8,128)}, f32[2,256,128]{2,1,0:T(8,128)S(1)}, u32[]{:S(2)}, u32[]{:S(2)}) collective-permute-start(f32[2,256,128]{2,1,0:T(8,128)} %get-tuple-element.141.pair_ref), channel_id=1, source_target_pairs={{0,8},{4,12},{8,16},{12,20},{16,24},{20,28},{1,9},{5,13},{9,17},{1... | collective-permute-start | bytes 786440 | tf_op jit(solution)/shard_map/ppermute | solution.py:517
  268.1 21.5 %collective-permute-start.54 = (f32[128,1536]{1,0:T(8,128)}, f32[128,1536]{1,0:T(8,128)S(1)}, u32[]{:S(2)}, u32[]{:S(2)}) collective-permute-start(f32[128,1536]{1,0:T(8,128)} %get-tuple-element.212.b_ref), channel_id=1, source_target_pairs={{0,4},{4,0},{8,12},{12,8},{16,20},{20,16},{24,28},{28,24},{1,5},{5... | collective-permute-start | bytes 2359304 | tf_op jit(solution)/shard_map/x_in_far_1/ppermute | solution.py:522
  279.8 14.4 %collective-permute-start.53 = (f32[128,512]{1,0:T(8,128)S(1)}, f32[128,512]{1,0:T(8,128)S(1)}, u32[]{:S(2)}, u32[]{:S(2)}) collective-permute-start(f32[128,512]{1,0:T(8,128)S(1)} %copy-done.67), channel_id=1, source_target_pairs={{0,4},{4,0},{8,12},{12,8},{16,20},{20,16},{24,28},{28,24},{1,5},{5... | collective-permute-start | bytes 786440 | tf_op jit(solution)/shard_map/ppermute | solution.py:522
  299.0 271.0 %reduce-scatter.5.cloned.1.call-start = ((), (), s32[]{:S(2)}) async-start(), calls=%async_computation.4 | async-start | bytes 3932160 | tf_op jit(solution)/shard_map/reduce_scatter | solution.py:550
  324.7 13.2 %collective-permute-start.38 = (f32[2,128,128]{2,1,0:T(8,128)}, f32[2,128,128]{2,1,0:T(8,128)S(1)}, u32[]{:S(2)}, u32[]{:S(2)}) collective-permute-start(f32[2,128,128]{2,1,0:T(8,128)} %get-tuple-element.184.offset_ref), channel_id=1, source_target_pairs={{8,0},{12,4},{16,8},{20,12},{24,16},{28,20},{9,1},{13,5},{17,9},{2... | collective-permute-start | bytes 393224 | tf_op jit(solution)/shard_map/ppermute | solution.py:517
  340.5 15.7 %collective-permute-start.39 = (f32[2,128,128]{2,1,0:T(8,128)}, f32[2,128,128]{2,1,0:T(8,128)S(1)}, u32[]{:S(2)}, u32[]{:S(2)}) collective-permute-start(f32[2,128,128]{2,1,0:T(8,128)} %step_back_0_0.1), channel_id=1, source_target_pairs={{8,0},{12,4},{16,8},{20,12},{24,16},{28,20},{9,1},{13,5},{17,9},{2... | collective-permute-start | bytes 393224 | tf_op jit(solution)/shard_map/ppermute | solution.py:517
  390.3 22.6 %collective-permute-start.52 = (f32[128,1536]{1,0:T(8,128)}, f32[128,1536]{1,0:T(8,128)S(1)}, u32[]{:S(2)}, u32[]{:S(2)}) collective-permute-start(f32[128,1536]{1,0:T(8,128)} %get-tuple-element.209.b_ref), channel_id=1, source_target_pairs={{0,4},{4,0},{8,12},{12,8},{16,20},{20,16},{24,28},{28,24},{1,5},{5... | collective-permute-start | bytes 2359304 | tf_op jit(solution)/shard_map/x_in_far_0/ppermute | solution.py:522
  392.7 20.3 %collective-permute-start.51 = (f32[128,512]{1,0:T(8,128)S(1)}, f32[128,512]{1,0:T(8,128)S(1)}, u32[]{:S(2)}, u32[]{:S(2)}) collective-permute-start(f32[128,512]{1,0:T(8,128)S(1)} %copy-done.65), channel_id=1, source_target_pairs={{0,4},{4,0},{8,12},{12,8},{16,20},{20,16},{24,28},{28,24},{1,5},{5... | collective-permute-start | bytes 786440 | tf_op jit(solution)/shard_map/ppermute | solution.py:522
  418.1 164.8 %reduce-scatter.11.cloned.1.call-start = ((), (), s32[]{:S(2)}) async-start(), calls=%async_computation.7 | async-start | bytes 6881280 | tf_op jit(solution)/shard_map/reduce_scatter | solution.py:550
  419.2 39.0 %collective-permute-start.60 = (f32[128,1920]{1,0:T(8,128)S(1)}, f32[128,1920]{1,0:T(8,128)S(1)}, u32[]{:S(2)}, u32[]{:S(2)}) collective-permute-start(f32[128,1920]{1,0:T(8,128)S(1)} %copy-done.14), channel_id=1, source_target_pairs={{0,4},{4,0},{8,12},{12,8},{16,20},{20,16},{24,28},{28,24},{1,5},{5... | collective-permute-start | bytes 2949128 | tf_op jit(solution)/shard_map/x_ffn_far_1/ppermute | solution.py:522
  421.2 36.0 %collective-permute-start.59 = (f32[128,1216]{0,1:T(8,128)S(1)}, f32[128,1216]{0,1:T(8,128)S(1)}, u32[]{:S(2)}, u32[]{:S(2)}) collective-permute-start(f32[128,1216]{0,1:T(8,128)S(1)} %copy.84), channel_id=1, source_target_pairs={{0,4},{4,0},{8,12},{12,8},{16,20},{20,16},{24,28},{28,24},{1,5},{5... | collective-permute-start | bytes 1867784 | tf_op jit(solution)/shard_map/ppermute | solution.py:522
  421.6 39.3 %collective-permute-start.62 = (f32[128,512]{1,0:T(8,128)S(1)}, f32[128,512]{1,0:T(8,128)}, u32[]{:S(2)}, u32[]{:S(2)}) collective-permute-start(f32[128,512]{1,0:T(8,128)S(1)} %copy-done.22), channel_id=1, source_target_pairs={{0,4},{4,0},{8,12},{12,8},{16,20},{20,16},{24,28},{28,24},{1,5},{5... | collective-permute-start | bytes 786440 | tf_op jit(solution)/shard_map/ppermute | solution.py:522
  423.3 40.4 %collective-permute-start.61 = (f32[128,512]{1,0:T(8,128)}, f32[128,512]{1,0:T(8,128)}, u32[]{:S(2)}, u32[]{:S(2)}) collective-permute-start(f32[128,512]{1,0:T(8,128)} %get-tuple-element.229), channel_id=1, source_target_pairs={{0,4},{4,0},{8,12},{12,8},{16,20},{20,16},{24,28},{28,24},{1,5},{5... | collective-permute-start | bytes 786440 | tf_op jit(solution)/shard_map/x_mid_far_1/ppermute | solution.py:522
  470.0 213.5 %reduce-scatter.9.cloned.1.call-start = ((), (), s32[]{:S(2)}) async-start(), calls=%async_computation.6 | async-start | bytes 6881280 | tf_op jit(solution)/shard_map/reduce_scatter | solution.py:550
  471.2 39.0 %collective-permute-start.56 = (f32[128,1920]{1,0:T(8,128)S(1)}, f32[128,1920]{1,0:T(8,128)S(1)}, u32[]{:S(2)}, u32[]{:S(2)}) collective-permute-start(f32[128,1920]{1,0:T(8,128)S(1)} %copy-done.15), channel_id=1, source_target_pairs={{0,4},{4,0},{8,12},{12,8},{16,20},{20,16},{24,28},{28,24},{1,5},{5... | collective-permute-start | bytes 2949128 | tf_op jit(solution)/shard_map/x_ffn_far_0/ppermute | solution.py:522
  472.9 36.3 %collective-permute-start.55 = (f32[128,1216]{0,1:T(8,128)S(1)}, f32[128,1216]{0,1:T(8,128)S(1)}, u32[]{:S(2)}, u32[]{:S(2)}) collective-permute-start(f32[128,1216]{0,1:T(8,128)S(1)} %copy.82), channel_id=1, source_target_pairs={{0,4},{4,0},{8,12},{12,8},{16,20},{20,16},{24,28},{28,24},{1,5},{5... | collective-permute-start | bytes 1867784 | tf_op jit(solution)/shard_map/ppermute | solution.py:522
  473.5 38.5 %collective-permute-start.58 = (f32[128,512]{1,0:T(8,128)S(1)}, f32[128,512]{1,0:T(8,128)}, u32[]{:S(2)}, u32[]{:S(2)}) collective-permute-start(f32[128,512]{1,0:T(8,128)S(1)} %copy-done.20), channel_id=1, source_target_pairs={{0,4},{4,0},{8,12},{12,8},{16,20},{20,16},{24,28},{28,24},{1,5},{5... | collective-permute-start | bytes 786440 | tf_op jit(solution)/shard_map/ppermute | solution.py:522
  475.0 39.9 %collective-permute-start.57 = (f32[128,512]{1,0:T(8,128)}, f32[128,512]{1,0:T(8,128)}, u32[]{:S(2)}, u32[]{:S(2)}) collective-permute-start(f32[128,512]{1,0:T(8,128)} %get-tuple-element.221), channel_id=1, source_target_pairs={{0,4},{4,0},{8,12},{12,8},{16,20},{20,16},{24,28},{28,24},{1,5},{5... | collective-permute-start | bytes 786440 | tf_op jit(solution)/shard_map/x_mid_far_0/ppermute | solution.py:522
  532.3 30.0 %collective-permute-start.21 = (f32[64,1024]{1,0:T(8,128)S(1)}, f32[64,1024]{1,0:T(8,128)S(1)}, u32[]{:S(2)}, u32[]{:S(2)}) collective-permute-start(f32[64,1024]{1,0:T(8,128)S(1)} %add.87.near_ref), channel_id=1, source_target_pairs={{0,1},{1,0},{2,3},{3,2},{4,5},{5,4},{6,7},{7,6},{8,9},{9,8},{10,11... | collective-permute-start | bytes 786440 | tf_op jit(solution)/shard_map/x_ffn_1/ppermute | solution.py:522
  532.5 8.8 %collective-permute-start.44 = (f32[64,1024]{1,0:T(8,128)S(1)}, f32[64,1024]{1,0:T(8,128)S(1)}, u32[]{:S(2)}, u32[]{:S(2)}) collective-permute-start(f32[64,1024]{1,0:T(8,128)S(1)} %add.94), channel_id=1, source_target_pairs={{0,2},{1,3},{2,0},{3,1},{4,6},{5,7},{6,4},{7,5},{8,10},{9,11},{10,... | collective-permute-start | bytes 786440 | tf_op jit(solution)/shard_map/x_in_back_0/ppermute | solution.py:522
  557.9 9.5 %collective-permute-start.50 = (f32[1,12800]{1,0:T(1,128)S(1)}, f32[1,12800]{1,0:T(1,128)S(1)}, u32[]{:S(2)}, u32[]{:S(2)}) collective-permute-start(f32[1,12800]{1,0:T(1,128)S(1)} %add.99), channel_id=1, source_target_pairs={{0,16},{4,20},{8,24},{12,28},{16,0},{20,4},{24,8},{28,12},{1,17},{... | collective-permute-start | bytes 153608 | tf_op jit(solution)/shard_map/ppermute | solution.py:522
  (113 other events, 500.0 us)
Sparse Core Ops, SparseCore 0:
  299.2 68.4 reduce-scatter.6
  418.2 62.1 reduce-scatter.4
  482.7 100.1 reduce-scatter.10
  585.0 98.4 reduce-scatter.8

commit v3 on v2

--- a/solution.py
+++ b/solution.py
@@ -6,6 +6,7 @@
 from jax.experimental import pallas as pl
 from jax.experimental.pallas import tpu as pltpu
 from jax.sharding import PartitionSpec as P
+
 
 DK = 128
 DV = 256
@@ -27,7 +28,7 @@
     return jax.ShapeDtypeStruct(tuple(dims), dtype)
 
 
-def call(body, outs, args, name, scratch=()):
+def call(body, outs, args, scratch=()):
     specs, arrays = [], []
     for arg in args:
         if isinstance(arg, tuple):
@@ -43,16 +44,14 @@
             array = arg
             specs.append(pl.BlockSpec(memory_space=pltpu.VMEM))
         arrays.append(array)
-    with jax.named_scope("k_" + name):
-        return pl.pallas_call(
-            body,
-            grid=(1,),
-            out_shape=tuple(outs),
-            in_specs=specs,
-            out_specs=tuple(pl.BlockSpec(memory_space=pltpu.VMEM) for _ in outs),
-            scratch_shapes=list(scratch),
-            name=name,
-        )(*arrays)
+    return pl.pallas_call(
+        body,
+        grid=(1,),
+        out_shape=tuple(outs),
+        in_specs=specs,
+        out_specs=tuple(pl.BlockSpec(memory_space=pltpu.VMEM) for _ in outs),
+        scratch_shapes=list(scratch),
+    )(*arrays)
 
 
 def at_level(level, rest, _):
@@ -522,14 +521,17 @@
     return lax.ppermute(array, axis, [(i, i ^ bit) for i in range(length)])
 
 
-def head_total(mine, other, name):
-    with jax.named_scope("x_" + name):
-        total = mine + swap(other, "head", 1)
-        step = 2
-        while step < lax.axis_size("head"):
-            total = total + swap(total, "head", step)
-            step *= 2
-        return total, swap(total, "head", 1)
+def head_total(mine, other):
+    total = mine + swap(other, "head", 1)
+    step = 2
+    while step < lax.axis_size("head"):
+        total = total + swap(total, "head", step)
+        step *= 2
+    return total, swap(total, "head", 1)
+
+
+def far_swap(array):
+    return swap(array, "seq", 1)
 
 
 def after(array, mark):
@@ -547,12 +549,10 @@
 def outer_scatter(array):
     size = lax.axis_size("seq")
     groups = [[2 * o + p for o in range(size // 2)] for p in range(2)]
-    return lax.psum_scatter(
-        array, "seq", scatter_dimension=0, tiled=True, axis_index_groups=groups
-    )
-
-
-def prefix(local, transfer, y, level):
+    return lax.psum_scatter(array, "seq", scatter_dimension=0, tiled=True, axis_index_groups=groups)
+
+
+def prefix(local, transfer, y):
     send, keep = local
     heads = keep.shape[0]
     square = shape_of((heads, DK, DK))
@@ -563,48 +563,39 @@
         pair_kernel,
         [square, square, half, shape_of((heads, DK + HALF, DK))],
         [y, transfer, keep, far],
-        f"pair_{level}",
     )
     if outer == 4:
         near = shift(pair, "seq", 2)
-        (moved,) = call(window_kernel, [half], [near, pair], f"window_{level}")
+        (moved,) = call(window_kernel, [half], [near, pair])
         state = shift(moved, "seq", 4)
     else:
         near = pair
         state = shift(pair[:, DK:], "seq", 2)
-        for hop in range(outer - 2):
-            (moved,) = call(step_kernel, [half], [state, pair], f"step_{level}_{hop}")
+        for _ in range(outer - 2):
+            (moved,) = call(step_kernel, [half], [state, pair])
             state = shift(moved, "seq", 2)
     mine, other = call(
         functools.partial(last_kernel, window=outer == 4),
         [half, half],
         [y, state, near, first_t, first_o],
-        f"last_{level}",
     )
     return mine, swap(other, "seq", 1), first_t, second_t, pair, near
 
 
-def suffix(send, keep, kept, y, level):
+def suffix(send, keep, kept, y):
     heads = keep.shape[0]
     half = shape_of((heads, HALF, DK))
     outer = lax.axis_size("seq") // 2
     far = swap(send, "seq", 1)
-    second_o, pair_o = call(
-        pair_back_kernel, [half, half], [y, keep, far, kept["first_t"]], f"pair_back_{level}"
-    )
+    second_o, pair_o = call(pair_back_kernel, [half, half], [y, keep, far, kept["first_t"]])
     state = shift(pair_o, "seq", -2)
     mark = state
     for hop in range(outer - 2):
-        (moved,) = call(
-            step_back_kernel, [half], [state, kept["pair"], pair_o], f"step_back_{level}_{hop}"
-        )
+        (moved,) = call(step_back_kernel, [half], [state, kept["pair"], pair_o])
+        if hop == 0:
+            mark = moved
         state = shift(moved, "seq", -2)
-    mine, other = call(
-        last_back_kernel,
-        [half, half],
-        [y, state, kept["second_t"], second_o],
-        f"last_back_{level}",
-    )
+    mine, other = call(last_back_kernel, [half, half], [y, state, kept["second_t"], second_o])
     return mine, swap(other, "seq", 1), mark
 
 
@@ -626,14 +617,12 @@
             functools.partial(in_kernel, level=level, size=size),
             kept_half + [shape_of((length, proj_width))],
             [y, stream, gain_one, (w_in, level)],
-            f"in_{level}",
         )
     else:
         stream, normed, normed_send, proj = call(
             functools.partial(in_sum_kernel, level=level, size=size),
             [shape_of((length, width))] + kept_half + [shape_of((length, proj_width))],
             [y, *start, gain_one, (w_in, level)],
-            f"in_{level}",
         )
     before = shift(proj[length - PAD :], "seq", 1)
     square = shape_of((heads, DK, DK))
@@ -644,10 +633,9 @@
         delta_kernel,
         [wide, wide, inner, inner, shape_of((heads, DK + HALF, DK)), half, square],
         [y, proj, before, (taps, level), (col, level), (row, level), (beta, level)],
-        f"delta_{level}",
         [pltpu.VMEM((length + PAD, QKV), f32), pltpu.VMEM((DV, DK), f32)],
     )
-    mine, other, first_t, second_t, pair, _ = prefix((send, keep), transfer, y, level)
+    mine, other, first_t, second_t, pair, _ = prefix((send, keep), transfer, y)
     incoming, outputs, gated, near, far = call(
         functools.partial(out_kernel, level=level),
         [
@@ -658,10 +646,9 @@
             rows,
         ],
         [y, mine, other, ow, proj, out_gain, (w_out, level)],
-        f"out_{level}",
         [whole],
     )
-    total = head_total(near, far, f"out_{level}")
+    total = head_total(near, far)
     mid, normed_two, ffn_send, gate, up, near, far = call(
         functools.partial(ffn_kernel, level=level, size=size),
         [
@@ -674,16 +661,15 @@
             rows,
         ],
         [y, stream, *total, gain_two, (w_gate, level), (w_up, level), (w_down, level)],
-        f"ffn_{level}",
         [whole],
     )
-    total = head_total(near, far, f"ffn_{level}")
+    total = head_total(near, far)
     stored = dict(
         stream=stream, normed=normed, proj=proj, before=before, ow=ow, uw=uw, solve=solve,
         mix=mix, first_t=first_t, second_t=second_t, pair=pair, incoming=incoming,
         outputs=outputs, gated=gated, mid=mid, normed_two=normed_two, gate=gate, up=up,
-        ffn_send=ffn_send, normed_far=swap(normed_send, "seq", 1),
-        gated_far=swap(gated, "seq", 1), ffn_far=swap(ffn_send, "seq", 1),
+        ffn_send=ffn_send, normed_far=far_swap(after(normed_send, gated)),
+        gated_far=far_swap(gated), ffn_far=far_swap(ffn_send),
     )
     return (mid, *total), stored
 
@@ -709,12 +695,10 @@
             rows,
         ],
         [y, grad, kept["gate"], kept["up"], (w_gate, level), (w_up, level), (w_down, level)],
-        f"ffn_back_{level}",
         [whole],
     )
-    with jax.named_scope(f"x_ffn_far_{level}"):
-        back_far = swap(back_send, "seq", 1)
-    total = head_total(near, far, f"ffn_back_{level}")
+    back_far = far_swap(back_send)
+    total = head_total(near, far)
     if pending is not None:
         pending = pending(near)
     half = shape_of((heads, HALF, DK))
@@ -735,12 +719,10 @@
             y, grad, *total, kept["mid"], gain_two, (w_out, level), kept["outputs"],
             kept["proj"], out_gain, kept["ow"],
         ],
-        f"out_back_{level}",
         [pltpu.VMEM((DV, DK), f32)],
     )
-    with jax.named_scope(f"x_mid_far_{level}"):
-        mid_far = swap(mid_send, "seq", 1)
-    mine, other, mark = suffix(send, keep, kept, y, level)
+    mid_far = far_swap(mid_send)
+    mine, other, mark = suffix(send, keep, kept, y)
     (block_weights,) = call(
         weight_block_kernel,
         [shape_of((half_width, 3 * hidden_width + value_width))],
@@ -748,7 +730,6 @@
             kept["normed_two"], kept["ffn_send"], kept["ffn_far"], back_send,
             after(back_far, mark), back, mid_back, mid_far, kept["gated"], kept["gated_far"],
         ],
-        f"weights_block_{level}",
     )
     block_weights = outer_scatter(block_weights)
     dconv, dtaps, edge = call(
@@ -763,18 +744,15 @@
             kept["proj"], kept["before"], (taps, level), (col, level), (row, level),
             (beta, level),
         ],
-        f"delta_back_{level}",
         [pltpu.VMEM((length + PAD, QKV), f32)],
     )
     grad_proj, near, far = call(
         in_back_kernel,
         [shape_of((length, proj_width)), rows, rows],
         [y, dconv, shift(edge, "seq", -1), (taps, level), grad_z, (w_in, level)],
-        f"in_back_{level}",
         [pltpu.VMEM((length + PAD, qkv_width), f32), whole],
     )
-    with jax.named_scope(f"x_in_far_{level}"):
-        proj_far = swap(grad_proj, "seq", 1)
+    proj_far = far_swap(grad_proj)
 
     def finish(mark):
         held = proj_far if mark is None else after(proj_far, mark)
@@ -782,16 +760,14 @@
             weight_in_kernel,
             [shape_of((half_width, proj_width))],
             [kept["normed"], grad_proj, kept["normed_far"], held],
-            f"weights_in_{level}",
         )
         return outer_scatter(in_weights)
 
-    total = head_total(near, far, f"in_back_{level}")
+    total = head_total(near, far)
     grad, dgain_one = call(
         functools.partial(norm_back_kernel, level=level),
         [shape_of((length, width)), shape_of((1, width))],
         [y, grad, *total, kept["stream"], gain_one],
-        f"norm_back_{level}",
     )
     return grad, (block_weights, dtaps, dgain_one, dout_gain, dgain_two), finish, pending
 
@@ -845,7 +821,7 @@
         if done is not None:
             in_weights[level + 1] = done
     in_weights[0] = finish(None)
-    (activations,) = call(sum_kernel, [shape_of(tokens.shape, bf16)], [y, *start], "finish")
+    (activations,) = call(sum_kernel, [shape_of(tokens.shape, bf16)], [y, *start])
     hidden_width = weight_gate.shape[2]
     block = [part[0] for part in parts]
 
@@ -917,4 +893,5 @@
         P(None, "seq", "head"),
         P(None, "head", "seq"),
     )
+
     return jax.shard_map(body, mesh=mesh, in_specs=in_specs, out_specs=out_specs, check_vma=False)

time: 698 us -> 698 us (level)
  no operation moved by 1% of the time
where the time goes in v3:
time: 698 us; the launch traced here: 696 us
  waiting for transfers between devices  405 us (58%)
  Pallas kernels  129 us (18%)
  starting transfers between devices  87.8 us (13%)
  local copies, waits for them, and re-layouts  51.1 us (7%)
  between operations  14.5 us (2%)
  other arithmetic  9.21 us (1%)
    ppermute x49, waiting for transfers between devices, swap(): return lax.ppermute(array, axis, [(i, i ^ bit) for i in range(length)])  220 us
    pallas_call x37, Pallas kernels, call(): pl.pallas_call(body, grid=(1,), out_shape=tuple(outs), in_specs=specs, ou...  129 us
    reduce_scatter x4, waiting for transfers between devices, outer_scatter(): lax.psum_scatter(array, 'seq', scatter_dimension=0, tiled=True, axis_inde...  108 us
    ppermute x14, waiting for transfers between devices, shift(): return lax.ppermute(array, axis, pairs)  75.9 us
    ppermute x49, starting transfers between devices, swap(): return lax.ppermute(array, axis, [(i, i ^ bit) for i in range(length)])  49.4 us
    unnamed x155, local copies, waits for them, and re-layouts  38.5 us
    ppermute x14, starting transfers between devices, shift(): return lax.ppermute(array, axis, pairs)  38.2 us
  transfers between devices with their start and end apart: 67, of which 54 were waited for; matrix products, arithmetic and copies ran while one was open for 3% of the time, Pallas kernels for 7%

profile of v3, /device:TPU:0, one launch (start us, length us, event | category | flops | bytes accessed | tf_op | source)
XLA Modules:
  0.0 696.1 jit_solution(15120951387181778951)
XLA Ops:
  20.0 7.8 %shard_map.213 = (f32[2,128,384]{2,1,0:T(8,128)}, f32[2,128,384]{2,1,0:T(8,128)}, f32[2,128,128]{2,1,0:T(8,128)}, f32[2,128,128]{2,1,0:T(8,128)}, f32[2,256,128]...) custom-call(s32[2]{0:T(128)} %pad_add_fusion.index_ref.y_ref, f32[128,1536]{1,0:T(8,128)} %get-tuple-element.123.proj_ref, ...), custom_call_target="tpu_custom_call" | custom-call | tf_op jit(solution)/shard_map/pallas_call | solution.py:47
  29.7 6.1 collective-permute-done.1.other_ref
  73.6 6.8 collective-permute-done.6
  97.6 7.1 %collective-permute-done.9 = f32[64,1024]{1,0:T(8,128)S(1)} collective-permute-done((f32[64,1024]{1,0:T(8,128)S(1)}, f32[64,1024]{1,0:T(8,128)S(1)}, u32[]{:S(2)}, u32[]{:S(2)}) %collective-permute-start.9) | collective-permute-done | bytes 262176 | tf_op jit(solution)/shard_map/ppermute | solution.py:521
  117.4 7.8 %shard_map.220 = (f32[2,128,384]{2,1,0:T(8,128)}, f32[2,128,384]{2,1,0:T(8,128)}, f32[2,128,128]{2,1,0:T(8,128)}, f32[2,128,128]{2,1,0:T(8,128)}, f32[2,256,128]...) custom-call(s32[2]{0:T(128)} %pad_add_fusion.index_ref.y_ref, f32[128,1536]{1,0:T(8,128)} %get-tuple-element.139.proj_ref, ...), custom_call_target="tpu_custom_call" | custom-call | tf_op jit(solution)/shard_map/pallas_call | solution.py:47
  128.1 6.0 collective-permute-done.12.other_ref
  173.0 6.8 collective-permute-done.17
  195.9 6.8 collective-permute-done.23
  218.7 6.6 collective-permute-done.26.state_ref
  229.2 5.8 collective-permute-done.27.state_ref
  238.9 5.8 collective-permute-done.28.state_ref
  272.7 6.9 collective-permute-done.32
  303.1 6.8 collective-permute-done.35
  326.3 11.7 %collective-permute-done.38.state_ref = f32[2,128,128]{2,1,0:T(8,128)S(1)} collective-permute-done((f32[2,128,128]{2,1,0:T(8,128)}, f32[2,128,128]{2,1,0:T(8,128)S(1)}, u32[]{:S(2)}, u32[]{:S(2)}) %collective-permute-start.38) | collective-permute-done | bytes 131104 | tf_op jit(solution)/shard_map/ppermute | solution.py:516
  341.8 14.4 %collective-permute-done.39.state_ref = f32[2,128,128]{2,1,0:T(8,128)S(1)} collective-permute-done((f32[2,128,128]{2,1,0:T(8,128)}, f32[2,128,128]{2,1,0:T(8,128)S(1)}, u32[]{:S(2)}, u32[]{:S(2)}) %collective-permute-start.39) | collective-permute-done | bytes 131104 | tf_op jit(solution)/shard_map/ppermute | solution.py:516
  360.1 6.8 collective-permute-done.40.state_ref
  392.7 20.2 %collective-permute-done.51.a_far_ref = f32[128,512]{1,0:T(8,128)S(1)} collective-permute-done((f32[128,512]{1,0:T(8,128)S(1)}, f32[128,512]{1,0:T(8,128)S(1)}, u32[]{:S(2)}, u32[]{:S(2)}) %collective-permute-start.51) | collective-permute-done | bytes 262176 | tf_op jit(solution)/shard_map/ppermute | solution.py:521
  423.6 33.6 %collective-permute-done.59 = f32[128,1216]{0,1:T(8,128)S(1)} collective-permute-done((f32[128,1216]{0,1:T(8,128)S(1)}, f32[128,1216]{0,1:T(8,128)S(1)}, u32[]{:S(2)}, u32[]{:S(2)}) %collective-permute-start.59) | collective-permute-done | bytes 622624 | tf_op jit(solution)/shard_map/ppermute | solution.py:521
  463.7 6.3 shard_map.248
  475.5 33.6 %collective-permute-done.55 = f32[128,1216]{0,1:T(8,128)S(1)} collective-permute-done((f32[128,1216]{0,1:T(8,128)S(1)}, f32[128,1216]{0,1:T(8,128)S(1)}, u32[]{:S(2)}, u32[]{:S(2)}) %collective-permute-start.55) | collective-permute-done | bytes 622624 | tf_op jit(solution)/shard_map/ppermute | solution.py:521
  514.9 6.3 shard_map.247
  534.0 7.3 %collective-permute-done.44 = f32[64,1024]{1,0:T(8,128)S(1)} collective-permute-done((f32[64,1024]{1,0:T(8,128)S(1)}, f32[64,1024]{1,0:T(8,128)S(1)}, u32[]{:S(2)}, u32[]{:S(2)}) %collective-permute-start.44) | collective-permute-done | bytes 262176 | tf_op jit(solution)/shard_map/ppermute | solution.py:521
  572.6 10.2 %reduce-scatter.11.cloned.1.call-done = f32[128,2624]{1,0:T(8,128)} async-done(((f32[512,2624]{1,0:T(8,128)}), f32[128,2624]{1,0:T(8,128)}) %reduce-scatter.11.cloned.1.call-update) | async-done | bytes 1343504 | tf_op jit(solution)/shard_map/reduce_scatter | solution.py:552
  585.4 98.1 %reduce-scatter.9.cloned.1.call-done = f32[128,2624]{1,0:T(8,128)} async-done(((f32[512,2624]{1,0:T(8,128)}), f32[128,2624]{1,0:T(8,128)}) %reduce-scatter.9.cloned.1.call-update) | async-done | bytes 1343504 | tf_op jit(solution)/shard_map/reduce_scatter | solution.py:552
  (358 shorter events, 345.8 us)
Async XLA Ops:
  7.2 562.8 %reduce-scatter.7.cloned.1.call-start = ((), (), s32[]{:S(2)}) async-start(), calls=%async_computation.5 | async-start | bytes 3932160 | tf_op jit(solution)/shard_map/reduce_scatter | solution.py:552
  96.1 8.6 %collective-permute-start.9 = (f32[64,1024]{1,0:T(8,128)S(1)}, f32[64,1024]{1,0:T(8,128)S(1)}, u32[]{:S(2)}, u32[]{:S(2)}) collective-permute-start(f32[64,1024]{1,0:T(8,128)S(1)} %add.82), channel_id=1, source_target_pairs={{0,2},{1,3},{2,0},{3,1},{4,6},{5,7},{6,4},{7,5},{8,10},{9,11},{10,... | collective-permute-start | bytes 786440 | tf_op jit(solution)/shard_map/ppermute | solution.py:521
  125.2 8.9 %collective-permute-start.12 = (f32[2,256,128]{2,1,0:T(8,128)}, f32[2,256,128]{2,1,0:T(8,128)S(1)}, u32[]{:S(2)}, u32[]{:S(2)}) collective-permute-start(f32[2,256,128]{2,1,0:T(8,128)} %get-tuple-element.142), channel_id=1, source_target_pairs={{0,4},{4,0},{8,12},{12,8},{16,20},{20,16},{24,28},{28,24},{1,5},{5... | collective-permute-start | bytes 786440 | tf_op jit(solution)/shard_map/ppermute | solution.py:521
  136.9 9.3 %collective-permute-start.13 = (f32[2,256,128]{2,1,0:T(8,128)}, f32[2,256,128]{2,1,0:T(8,128)S(1)}, u32[]{:S(2)}, u32[]{:S(2)}) collective-permute-start(f32[2,256,128]{2,1,0:T(8,128)} %get-tuple-element.143.pair_ref), channel_id=1, source_target_pairs={{0,8},{4,12},{8,16},{12,20},{16,24},{20,28},{1,9},{5,13},{9,17},{1... | collective-permute-start | bytes 786440 | tf_op jit(solution)/shard_map/ppermute | solution.py:516
  268.1 21.5 %collective-permute-start.54 = (f32[128,1536]{1,0:T(8,128)}, f32[128,1536]{1,0:T(8,128)S(1)}, u32[]{:S(2)}, u32[]{:S(2)}) collective-permute-start(f32[128,1536]{1,0:T(8,128)} %get-tuple-element.216.b_ref), channel_id=1, source_target_pairs={{0,4},{4,0},{8,12},{12,8},{16,20},{20,16},{24,28},{28,24},{1,5},{5... | collective-permute-start | bytes 2359304 | tf_op jit(solution)/shard_map/ppermute | solution.py:521
  279.8 14.4 %collective-permute-start.53 = (f32[128,512]{1,0:T(8,128)S(1)}, f32[128,512]{1,0:T(8,128)S(1)}, u32[]{:S(2)}, u32[]{:S(2)}) collective-permute-start(f32[128,512]{1,0:T(8,128)S(1)} %copy-done.67), channel_id=1, source_target_pairs={{0,4},{4,0},{8,12},{12,8},{16,20},{20,16},{24,28},{28,24},{1,5},{5... | collective-permute-start | bytes 786440 | tf_op jit(solution)/shard_map/ppermute | solution.py:521
  299.0 271.0 %reduce-scatter.5.cloned.1.call-start = ((), (), s32[]{:S(2)}) async-start(), calls=%async_computation.4 | async-start | bytes 3932160 | tf_op jit(solution)/shard_map/reduce_scatter | solution.py:552
  324.7 13.2 %collective-permute-start.38 = (f32[2,128,128]{2,1,0:T(8,128)}, f32[2,128,128]{2,1,0:T(8,128)S(1)}, u32[]{:S(2)}, u32[]{:S(2)}) collective-permute-start(f32[2,128,128]{2,1,0:T(8,128)} %get-tuple-element.186.offset_ref), channel_id=1, source_target_pairs={{8,0},{12,4},{16,8},{20,12},{24,16},{28,20},{9,1},{13,5},{17,9},{2... | collective-permute-start | bytes 393224 | tf_op jit(solution)/shard_map/ppermute | solution.py:516
  340.5 15.7 %collective-permute-start.39 = (f32[2,128,128]{2,1,0:T(8,128)}, f32[2,128,128]{2,1,0:T(8,128)S(1)}, u32[]{:S(2)}, u32[]{:S(2)}) collective-permute-start(f32[2,128,128]{2,1,0:T(8,128)} %shard_map.239), channel_id=1, source_target_pairs={{8,0},{12,4},{16,8},{20,12},{24,16},{28,20},{9,1},{13,5},{17,9},{2... | collective-permute-start | bytes 393224 | tf_op jit(solution)/shard_map/ppermute | solution.py:516
  390.3 22.6 %collective-permute-start.52 = (f32[128,1536]{1,0:T(8,128)}, f32[128,1536]{1,0:T(8,128)S(1)}, u32[]{:S(2)}, u32[]{:S(2)}) collective-permute-start(f32[128,1536]{1,0:T(8,128)} %get-tuple-element.211.b_ref), channel_id=1, source_target_pairs={{0,4},{4,0},{8,12},{12,8},{16,20},{20,16},{24,28},{28,24},{1,5},{5... | collective-permute-start | bytes 2359304 | tf_op jit(solution)/shard_map/ppermute | solution.py:521
  392.7 20.3 %collective-permute-start.51 = (f32[128,512]{1,0:T(8,128)S(1)}, f32[128,512]{1,0:T(8,128)S(1)}, u32[]{:S(2)}, u32[]{:S(2)}) collective-permute-start(f32[128,512]{1,0:T(8,128)S(1)} %copy-done.65), channel_id=1, source_target_pairs={{0,4},{4,0},{8,12},{12,8},{16,20},{20,16},{24,28},{28,24},{1,5},{5... | collective-permute-start | bytes 786440 | tf_op jit(solution)/shard_map/ppermute | solution.py:521
  418.1 164.8 %reduce-scatter.11.cloned.1.call-start = ((), (), s32[]{:S(2)}) async-start(), calls=%async_computation.7 | async-start | bytes 6881280 | tf_op jit(solution)/shard_map/reduce_scatter | solution.py:552
  419.2 39.0 %collective-permute-start.60 = (f32[128,1920]{1,0:T(8,128)S(1)}, f32[128,1920]{1,0:T(8,128)S(1)}, u32[]{:S(2)}, u32[]{:S(2)}) collective-permute-start(f32[128,1920]{1,0:T(8,128)S(1)} %copy-done.14), channel_id=1, source_target_pairs={{0,4},{4,0},{8,12},{12,8},{16,20},{20,16},{24,28},{28,24},{1,5},{5... | collective-permute-start | bytes 2949128 | tf_op jit(solution)/shard_map/ppermute | solution.py:521
  421.2 36.0 %collective-permute-start.59 = (f32[128,1216]{0,1:T(8,128)S(1)}, f32[128,1216]{0,1:T(8,128)S(1)}, u32[]{:S(2)}, u32[]{:S(2)}) collective-permute-start(f32[128,1216]{0,1:T(8,128)S(1)} %copy.84), channel_id=1, source_target_pairs={{0,4},{4,0},{8,12},{12,8},{16,20},{20,16},{24,28},{28,24},{1,5},{5... | collective-permute-start | bytes 1867784 | tf_op jit(solution)/shard_map/ppermute | solution.py:521
  421.6 39.3 %collective-permute-start.62 = (f32[128,512]{1,0:T(8,128)S(1)}, f32[128,512]{1,0:T(8,128)}, u32[]{:S(2)}, u32[]{:S(2)}) collective-permute-start(f32[128,512]{1,0:T(8,128)S(1)} %copy-done.22), channel_id=1, source_target_pairs={{0,4},{4,0},{8,12},{12,8},{16,20},{20,16},{24,28},{28,24},{1,5},{5... | collective-permute-start | bytes 786440 | tf_op jit(solution)/shard_map/ppermute | solution.py:521
  423.3 40.4 %collective-permute-start.61 = (f32[128,512]{1,0:T(8,128)}, f32[128,512]{1,0:T(8,128)}, u32[]{:S(2)}, u32[]{:S(2)}) collective-permute-start(f32[128,512]{1,0:T(8,128)} %get-tuple-element.234), channel_id=1, source_target_pairs={{0,4},{4,0},{8,12},{12,8},{16,20},{20,16},{24,28},{28,24},{1,5},{5... | collective-permute-start | bytes 786440 | tf_op jit(solution)/shard_map/ppermute | solution.py:521
  470.0 213.5 %reduce-scatter.9.cloned.1.call-start = ((), (), s32[]{:S(2)}) async-start(), calls=%async_computation.6 | async-start | bytes 6881280 | tf_op jit(solution)/shard_map/reduce_scatter | solution.py:552
  471.2 39.0 %collective-permute-start.56 = (f32[128,1920]{1,0:T(8,128)S(1)}, f32[128,1920]{1,0:T(8,128)S(1)}, u32[]{:S(2)}, u32[]{:S(2)}) collective-permute-start(f32[128,1920]{1,0:T(8,128)S(1)} %copy-done.15), channel_id=1, source_target_pairs={{0,4},{4,0},{8,12},{12,8},{16,20},{20,16},{24,28},{28,24},{1,5},{5... | collective-permute-start | bytes 2949128 | tf_op jit(solution)/shard_map/ppermute | solution.py:521
  472.9 36.3 %collective-permute-start.55 = (f32[128,1216]{0,1:T(8,128)S(1)}, f32[128,1216]{0,1:T(8,128)S(1)}, u32[]{:S(2)}, u32[]{:S(2)}) collective-permute-start(f32[128,1216]{0,1:T(8,128)S(1)} %copy.82), channel_id=1, source_target_pairs={{0,4},{4,0},{8,12},{12,8},{16,20},{20,16},{24,28},{28,24},{1,5},{5... | collective-permute-start | bytes 1867784 | tf_op jit(solution)/shard_map/ppermute | solution.py:521
  473.5 38.5 %collective-permute-start.58 = (f32[128,512]{1,0:T(8,128)S(1)}, f32[128,512]{1,0:T(8,128)}, u32[]{:S(2)}, u32[]{:S(2)}) collective-permute-start(f32[128,512]{1,0:T(8,128)S(1)} %copy-done.20), channel_id=1, source_target_pairs={{0,4},{4,0},{8,12},{12,8},{16,20},{20,16},{24,28},{28,24},{1,5},{5... | collective-permute-start | bytes 786440 | tf_op jit(solution)/shard_map/ppermute | solution.py:521
  475.0 39.9 %collective-permute-start.57 = (f32[128,512]{1,0:T(8,128)}, f32[128,512]{1,0:T(8,128)}, u32[]{:S(2)}, u32[]{:S(2)}) collective-permute-start(f32[128,512]{1,0:T(8,128)} %get-tuple-element.227), channel_id=1, source_target_pairs={{0,4},{4,0},{8,12},{12,8},{16,20},{20,16},{24,28},{28,24},{1,5},{5... | collective-permute-start | bytes 786440 | tf_op jit(solution)/shard_map/ppermute | solution.py:521
  532.3 30.0 %collective-permute-start.21 = (f32[64,1024]{1,0:T(8,128)S(1)}, f32[64,1024]{1,0:T(8,128)S(1)}, u32[]{:S(2)}, u32[]{:S(2)}) collective-permute-start(f32[64,1024]{1,0:T(8,128)S(1)} %add.87.near_ref), channel_id=1, source_target_pairs={{0,1},{1,0},{2,3},{3,2},{4,5},{5,4},{6,7},{7,6},{8,9},{9,8},{10,11... | collective-permute-start | bytes 786440 | tf_op jit(solution)/shard_map/ppermute | solution.py:521
  532.5 8.8 %collective-permute-start.44 = (f32[64,1024]{1,0:T(8,128)S(1)}, f32[64,1024]{1,0:T(8,128)S(1)}, u32[]{:S(2)}, u32[]{:S(2)}) collective-permute-start(f32[64,1024]{1,0:T(8,128)S(1)} %add.94), channel_id=1, source_target_pairs={{0,2},{1,3},{2,0},{3,1},{4,6},{5,7},{6,4},{7,5},{8,10},{9,11},{10,... | collective-permute-start | bytes 786440 | tf_op jit(solution)/shard_map/ppermute | solution.py:521
  557.9 9.5 %collective-permute-start.50 = (f32[1,12800]{1,0:T(1,128)S(1)}, f32[1,12800]{1,0:T(1,128)S(1)}, u32[]{:S(2)}, u32[]{:S(2)}) collective-permute-start(f32[1,12800]{1,0:T(1,128)S(1)} %add.99), channel_id=1, source_target_pairs={{0,16},{4,20},{8,24},{12,28},{16,0},{20,4},{24,8},{28,12},{1,17},{... | collective-permute-start | bytes 153608 | tf_op jit(solution)/shard_map/ppermute | solution.py:521
  (113 other events, 500.0 us)
Sparse Core Ops, SparseCore 0:
  299.2 68.4 reduce-scatter.6
  418.2 62.1 reduce-scatter.4
  482.7 100.1 reduce-scatter.10
  585.0 98.4 reduce-scatter.8

commit v4 on v3

--- a/solution.py
+++ b/solution.py
@@ -1,4 +1,5 @@
 import functools
+import types
 
 import jax
 import jax.numpy as jnp
@@ -8,6 +9,8 @@
 from jax.sharding import PartitionSpec as P
 
 
+SEQ = "seq"
+HEAD = "head"
 DK = 128
 DV = 256
 CONV = 4
@@ -522,16 +525,16 @@
 
 
 def head_total(mine, other):
-    total = mine + swap(other, "head", 1)
+    total = mine + swap(other, HEAD, 1)
     step = 2
-    while step < lax.axis_size("head"):
-        total = total + swap(total, "head", step)
+    while step < lax.axis_size(HEAD):
+        total = total + swap(total, HEAD, step)
         step *= 2
-    return total, swap(total, "head", 1)
+    return total, swap(total, HEAD, 1)
 
 
 def far_swap(array):
-    return swap(array, "seq", 1)
+    return swap(array, SEQ, 1)
 
 
 def after(array, mark):
@@ -547,9 +550,9 @@
 
 
 def outer_scatter(array):
-    size = lax.axis_size("seq")
+    size = lax.axis_size(SEQ)
     groups = [[2 * o + p for o in range(size // 2)] for p in range(2)]
-    return lax.psum_scatter(array, "seq", scatter_dimension=0, tiled=True, axis_index_groups=groups)
+    return lax.psum_scatter(array, SEQ, scatter_dimension=0, tiled=True, axis_index_groups=groups)
 
 
 def prefix(local, transfer, y):
@@ -557,46 +560,44 @@
     heads = keep.shape[0]
     square = shape_of((heads, DK, DK))
     half = shape_of((heads, HALF, DK))
-    outer = lax.axis_size("seq") // 2
-    far = swap(send, "seq", 1)
+    outer = lax.axis_size(SEQ) // 2
+    far = swap(send, SEQ, 1)
     first_t, second_t, first_o, pair = call(
         pair_kernel,
         [square, square, half, shape_of((heads, DK + HALF, DK))],
         [y, transfer, keep, far],
     )
     if outer == 4:
-        near = shift(pair, "seq", 2)
+        near = shift(pair, SEQ, 2)
         (moved,) = call(window_kernel, [half], [near, pair])
-        state = shift(moved, "seq", 4)
+        state = shift(moved, SEQ, 4)
     else:
         near = pair
-        state = shift(pair[:, DK:], "seq", 2)
+        state = shift(pair[:, DK:], SEQ, 2)
         for _ in range(outer - 2):
             (moved,) = call(step_kernel, [half], [state, pair])
-            state = shift(moved, "seq", 2)
+            state = shift(moved, SEQ, 2)
     mine, other = call(
         functools.partial(last_kernel, window=outer == 4),
         [half, half],
         [y, state, near, first_t, first_o],
     )
-    return mine, swap(other, "seq", 1), first_t, second_t, pair, near
+    return mine, swap(other, SEQ, 1), first_t, second_t, pair, near
 
 
 def suffix(send, keep, kept, y):
     heads = keep.shape[0]
     half = shape_of((heads, HALF, DK))
-    outer = lax.axis_size("seq") // 2
-    far = swap(send, "seq", 1)
-    second_o, pair_o = call(pair_back_kernel, [half, half], [y, keep, far, kept["first_t"]])
-    state = shift(pair_o, "seq", -2)
-    mark = state
-    for hop in range(outer - 2):
-        (moved,) = call(step_back_kernel, [half], [state, kept["pair"], pair_o])
-        if hop == 0:
-            mark = moved
-        state = shift(moved, "seq", -2)
-    mine, other = call(last_back_kernel, [half, half], [y, state, kept["second_t"], second_o])
-    return mine, swap(other, "seq", 1), mark
+    outer = lax.axis_size(SEQ) // 2
+    far = swap(send, SEQ, 1)
+    second_o, pair_o = call(pair_back_kernel, [half, half], [y, keep, far, kept.first_t])
+    state = shift(pair_o, SEQ, -2)
+    mark = pair_o
+    for _ in range(outer - 2):
+        (moved,) = call(step_back_kernel, [half], [state, kept.pair, pair_o])
+        state = shift(moved, SEQ, -2)
+    mine, other = call(last_back_kernel, [half, half], [y, state, kept.second_t, second_o])
+    return mine, swap(other, SEQ, 1), mark
 
 
 def layer_forward(start, shared, level, y):
@@ -606,7 +607,7 @@
     proj_width = w_in.shape[2]
     hidden_width = w_gate.shape[2]
     value_width = heads * DV
-    size = lax.axis_size("seq")
+    size = lax.axis_size(SEQ)
     half_width = width // 2
     rows = shape_of((length // 2, width))
     whole = pltpu.VMEM((length, width), f32)
@@ -624,7 +625,7 @@
             [shape_of((length, width))] + kept_half + [shape_of((length, proj_width))],
             [y, *start, gain_one, (w_in, level)],
         )
-    before = shift(proj[length - PAD :], "seq", 1)
+    before = shift(proj[length - PAD :], SEQ, 1)
     square = shape_of((heads, DK, DK))
     wide = shape_of((heads, length, DV + DK))
     inner = shape_of((heads, length, length))
@@ -664,7 +665,7 @@
         [whole],
     )
     total = head_total(near, far)
-    stored = dict(
+    stored = types.SimpleNamespace(
         stream=stream, normed=normed, proj=proj, before=before, ow=ow, uw=uw, solve=solve,
         mix=mix, first_t=first_t, second_t=second_t, pair=pair, incoming=incoming,
         outputs=outputs, gated=gated, mid=mid, normed_two=normed_two, gate=gate, up=up,
@@ -682,7 +683,7 @@
     hidden_width = w_gate.shape[2]
     value_width = heads * DV
     qkv_width = heads * QKV
-    size = lax.axis_size("seq")
+    size = lax.axis_size(SEQ)
     half_width = width // 2
     rows = shape_of((length // 2, width))
     whole = pltpu.VMEM((length, width), f32)
@@ -694,7 +695,7 @@
             rows,
             rows,
         ],
-        [y, grad, kept["gate"], kept["up"], (w_gate, level), (w_up, level), (w_down, level)],
+        [y, grad, kept.gate, kept.up, (w_gate, level), (w_up, level), (w_down, level)],
         [whole],
     )
     back_far = far_swap(back_send)
@@ -716,8 +717,8 @@
             half,
         ],
         [
-            y, grad, *total, kept["mid"], gain_two, (w_out, level), kept["outputs"],
-            kept["proj"], out_gain, kept["ow"],
+            y, grad, *total, kept.mid, gain_two, (w_out, level), kept.outputs,
+            kept.proj, out_gain, kept.ow,
         ],
         [pltpu.VMEM((DV, DK), f32)],
     )
@@ -727,8 +728,8 @@
         weight_block_kernel,
         [shape_of((half_width, 3 * hidden_width + value_width))],
         [
-            kept["normed_two"], kept["ffn_send"], kept["ffn_far"], back_send,
-            after(back_far, mark), back, mid_back, mid_far, kept["gated"], kept["gated_far"],
+            kept.normed_two, kept.ffn_send, kept.ffn_far, back_send,
+            after(back_far, mark), back, mid_back, mid_far, kept.gated, kept.gated_far,
         ],
     )
     block_weights = outer_scatter(block_weights)
@@ -740,8 +741,8 @@
             shape_of((PAD, qkv_width)),
         ],
         [
-            y, mine, other, kept["incoming"], kept["uw"], kept["solve"], kept["mix"], grad_o,
-            kept["proj"], kept["before"], (taps, level), (col, level), (row, level),
+            y, mine, other, kept.incoming, kept.uw, kept.solve, kept.mix, grad_o,
+            kept.proj, kept.before, (taps, level), (col, level), (row, level),
             (beta, level),
         ],
         [pltpu.VMEM((length + PAD, QKV), f32)],
@@ -749,7 +750,7 @@
     grad_proj, near, far = call(
         in_back_kernel,
         [shape_of((length, proj_width)), rows, rows],
-        [y, dconv, shift(edge, "seq", -1), (taps, level), grad_z, (w_in, level)],
+        [y, dconv, shift(edge, SEQ, -1), (taps, level), grad_z, (w_in, level)],
         [pltpu.VMEM((length + PAD, qkv_width), f32), whole],
     )
     proj_far = far_swap(grad_proj)
@@ -759,7 +760,7 @@
         (in_weights,) = call(
             weight_in_kernel,
             [shape_of((half_width, proj_width))],
-            [kept["normed"], grad_proj, kept["normed_far"], held],
+            [kept.normed, grad_proj, kept.normed_far, held],
         )
         return outer_scatter(in_weights)
 
@@ -767,7 +768,7 @@
     grad, dgain_one = call(
         functools.partial(norm_back_kernel, level=level),
         [shape_of((length, width)), shape_of((1, width))],
-        [y, grad, *total, kept["stream"], gain_one],
+        [y, grad, *total, kept.stream, gain_one],
     )
     return grad, (block_weights, dtaps, dgain_one, dout_gain, dgain_two), finish, pending
 
@@ -787,7 +788,7 @@
     weight_up,
     weight_down,
 ):
-    y = jnp.stack([lax.axis_index("seq") % 2, lax.axis_index("head") % 2]).astype(jnp.int32)
+    y = jnp.stack([lax.axis_index(SEQ) % 2, lax.axis_index(HEAD) % 2]).astype(jnp.int32)
     logdecay = -gate_code.astype(f32) * gate_unit
     beta_rate = jnp.transpose(beta_code.astype(f32) * beta_unit, (0, 2, 1))
     cumulated = jnp.transpose(jnp.cumsum(logdecay, axis=1), (0, 2, 1))
@@ -835,7 +836,7 @@
     grad_in = jnp.stack(in_weights)
     qkv_width = conv_weight.shape[2]
     width = tokens.shape[1]
-    out_gain_part = full_sum(jnp.concatenate([part[3] for part in parts], axis=0), "head")
+    out_gain_part = full_sum(jnp.concatenate([part[3] for part in parts], axis=0), HEAD)
     small = jnp.concatenate(
         [part[1].reshape(1, -1) for part in parts]
         + [part[2] for part in parts]
@@ -843,7 +844,7 @@
         + [out_gain_part.reshape(1, -1)],
         axis=1,
     )
-    small = full_sum(small, "seq")[0]
+    small = full_sum(small, SEQ)[0]
     sizes = [STACK_LEVELS * CONV * qkv_width, STACK_LEVELS * width, STACK_LEVELS * width]
     conv_grad = small[: sizes[0]].reshape(STACK_LEVELS, CONV, qkv_width)
     gain_one_grad = small[sizes[0] : sizes[0] + sizes[1]].reshape(STACK_LEVELS, width)
@@ -866,32 +867,32 @@
 
 def solution(mesh):
     in_specs = (
-        P("seq", None),
-        P("seq", None),
-        P(None, "seq", "head"),
-        P(None, "seq", "head"),
+        P(SEQ, None),
+        P(SEQ, None),
+        P(None, SEQ, HEAD),
+        P(None, SEQ, HEAD),
         P(),
-        P(None, None, "head"),
-        P(None, None, "head"),
+        P(None, None, HEAD),
+        P(None, None, HEAD),
         P(),
-        P(None, "head", None),
+        P(None, HEAD, None),
         P(),
-        P(None, None, "head"),
-        P(None, None, "head"),
-        P(None, "head", None),
+        P(None, None, HEAD),
+        P(None, None, HEAD),
+        P(None, HEAD, None),
     )
     out_specs = (
-        P("seq", None),
-        P("seq", None),
+        P(SEQ, None),
+        P(SEQ, None),
         P(),
-        P(None, "seq", "head"),
-        P(None, None, "head"),
+        P(None, SEQ, HEAD),
+        P(None, None, HEAD),
         P(),
-        P(None, "head", "seq"),
+        P(None, HEAD, SEQ),
         P(),
-        P(None, "seq", "head"),
-        P(None, "seq", "head"),
-        P(None, "head", "seq"),
+        P(None, SEQ, HEAD),
+        P(None, SEQ, HEAD),
+        P(None, HEAD, SEQ),
     )
 
     return jax.shard_map(body, mesh=mesh, in_specs=in_specs, out_specs=out_specs, check_vma=False)

time: 698 us -> 698 us (level)
  no operation moved by 1% of the time
where the time goes in v4:
time: 698 us; the launch traced here: 696 us
  waiting for transfers between devices  405 us (58%)
  Pallas kernels  129 us (18%)
  starting transfers between devices  87.8 us (13%)
  local copies, waits for them, and re-layouts  51.1 us (7%)
  between operations  14.5 us (2%)
  other arithmetic  9.21 us (1%)
    ppermute x49, waiting for transfers between devices, swap(): return lax.ppermute(array, axis, [(i, i ^ bit) for i in range(length)])  220 us
    pallas_call x37, Pallas kernels, call(): pl.pallas_call(body, grid=(1,), out_shape=tuple(outs), in_specs=specs, ou...  129 us
    reduce_scatter x4, waiting for transfers between devices, outer_scatter(): lax.psum_scatter(array, SEQ, scatter_dimension=0, tiled=True, axis_index_...  108 us
    ppermute x14, waiting for transfers between devices, shift(): return lax.ppermute(array, axis, pairs)  75.9 us
    ppermute x49, starting transfers between devices, swap(): return lax.ppermute(array, axis, [(i, i ^ bit) for i in range(length)])  49.4 us
    unnamed x155, local copies, waits for them, and re-layouts  38.5 us
    ppermute x14, starting transfers between devices, shift(): return lax.ppermute(array, axis, pairs)  38.2 us
  transfers between devices with their start and end apart: 67, of which 54 were waited for; matrix products, arithmetic and copies ran while one was open for 3% of the time, Pallas kernels for 7%

profile of v4, /device:TPU:0, one launch (start us, length us, event | category | flops | bytes accessed | tf_op | source)
XLA Modules:
  0.0 696.1 jit_solution(15120951387181778951)
XLA Ops:
  20.0 7.8 %shard_map.213 = (f32[2,128,384]{2,1,0:T(8,128)}, f32[2,128,384]{2,1,0:T(8,128)}, f32[2,128,128]{2,1,0:T(8,128)}, f32[2,128,128]{2,1,0:T(8,128)}, f32[2,256,128]...) custom-call(s32[2]{0:T(128)} %pad_add_fusion.index_ref.y_ref, f32[128,1536]{1,0:T(8,128)} %get-tuple-element.123.proj_ref, ...), custom_call_target="tpu_custom_call" | custom-call | tf_op jit(solution)/shard_map/pallas_call | solution.py:50
  29.7 6.1 collective-permute-done.1.other_ref
  73.6 6.8 collective-permute-done.6
  97.6 7.1 %collective-permute-done.9 = f32[64,1024]{1,0:T(8,128)S(1)} collective-permute-done((f32[64,1024]{1,0:T(8,128)S(1)}, f32[64,1024]{1,0:T(8,128)S(1)}, u32[]{:S(2)}, u32[]{:S(2)}) %collective-permute-start.9) | collective-permute-done | bytes 262176 | tf_op jit(solution)/shard_map/ppermute | solution.py:524
  117.4 7.8 %shard_map.220 = (f32[2,128,384]{2,1,0:T(8,128)}, f32[2,128,384]{2,1,0:T(8,128)}, f32[2,128,128]{2,1,0:T(8,128)}, f32[2,128,128]{2,1,0:T(8,128)}, f32[2,256,128]...) custom-call(s32[2]{0:T(128)} %pad_add_fusion.index_ref.y_ref, f32[128,1536]{1,0:T(8,128)} %get-tuple-element.139.proj_ref, ...), custom_call_target="tpu_custom_call" | custom-call | tf_op jit(solution)/shard_map/pallas_call | solution.py:50
  128.1 6.0 collective-permute-done.12.other_ref
  173.0 6.8 collective-permute-done.17
  195.9 6.8 collective-permute-done.23
  218.7 6.6 collective-permute-done.26.state_ref
  229.2 5.8 collective-permute-done.27.state_ref
  238.9 5.8 collective-permute-done.28.state_ref
  272.7 6.9 collective-permute-done.32
  303.1 6.8 collective-permute-done.35
  326.3 11.7 %collective-permute-done.38.state_ref = f32[2,128,128]{2,1,0:T(8,128)S(1)} collective-permute-done((f32[2,128,128]{2,1,0:T(8,128)}, f32[2,128,128]{2,1,0:T(8,128)S(1)}, u32[]{:S(2)}, u32[]{:S(2)}) %collective-permute-start.38) | collective-permute-done | bytes 131104 | tf_op jit(solution)/shard_map/ppermute | solution.py:519
  341.8 14.4 %collective-permute-done.39.state_ref = f32[2,128,128]{2,1,0:T(8,128)S(1)} collective-permute-done((f32[2,128,128]{2,1,0:T(8,128)}, f32[2,128,128]{2,1,0:T(8,128)S(1)}, u32[]{:S(2)}, u32[]{:S(2)}) %collective-permute-start.39) | collective-permute-done | bytes 131104 | tf_op jit(solution)/shard_map/ppermute | solution.py:519
  360.1 6.8 collective-permute-done.40.state_ref
  392.7 20.2 %collective-permute-done.51.a_far_ref = f32[128,512]{1,0:T(8,128)S(1)} collective-permute-done((f32[128,512]{1,0:T(8,128)S(1)}, f32[128,512]{1,0:T(8,128)S(1)}, u32[]{:S(2)}, u32[]{:S(2)}) %collective-permute-start.51) | collective-permute-done | bytes 262176 | tf_op jit(solution)/shard_map/ppermute | solution.py:524
  423.6 33.6 %collective-permute-done.59 = f32[128,1216]{0,1:T(8,128)S(1)} collective-permute-done((f32[128,1216]{0,1:T(8,128)S(1)}, f32[128,1216]{0,1:T(8,128)S(1)}, u32[]{:S(2)}, u32[]{:S(2)}) %collective-permute-start.59) | collective-permute-done | bytes 622624 | tf_op jit(solution)/shard_map/ppermute | solution.py:524
  463.7 6.3 shard_map.248
  475.5 33.6 %collective-permute-done.55 = f32[128,1216]{0,1:T(8,128)S(1)} collective-permute-done((f32[128,1216]{0,1:T(8,128)S(1)}, f32[128,1216]{0,1:T(8,128)S(1)}, u32[]{:S(2)}, u32[]{:S(2)}) %collective-permute-start.55) | collective-permute-done | bytes 622624 | tf_op jit(solution)/shard_map/ppermute | solution.py:524
  514.9 6.3 shard_map.247
  534.0 7.3 %collective-permute-done.44 = f32[64,1024]{1,0:T(8,128)S(1)} collective-permute-done((f32[64,1024]{1,0:T(8,128)S(1)}, f32[64,1024]{1,0:T(8,128)S(1)}, u32[]{:S(2)}, u32[]{:S(2)}) %collective-permute-start.44) | collective-permute-done | bytes 262176 | tf_op jit(solution)/shard_map/ppermute | solution.py:524
  572.6 10.2 %reduce-scatter.11.cloned.1.call-done = f32[128,2624]{1,0:T(8,128)} async-done(((f32[512,2624]{1,0:T(8,128)}), f32[128,2624]{1,0:T(8,128)}) %reduce-scatter.11.cloned.1.call-update) | async-done | bytes 1343504 | tf_op jit(solution)/shard_map/reduce_scatter | solution.py:555
  585.4 98.1 %reduce-scatter.9.cloned.1.call-done = f32[128,2624]{1,0:T(8,128)} async-done(((f32[512,2624]{1,0:T(8,128)}), f32[128,2624]{1,0:T(8,128)}) %reduce-scatter.9.cloned.1.call-update) | async-done | bytes 1343504 | tf_op jit(solution)/shard_map/reduce_scatter | solution.py:555
  (358 shorter events, 345.8 us)
Async XLA Ops:
  7.2 562.8 %reduce-scatter.7.cloned.1.call-start = ((), (), s32[]{:S(2)}) async-start(), calls=%async_computation.5 | async-start | bytes 3932160 | tf_op jit(solution)/shard_map/reduce_scatter | solution.py:555
  96.1 8.6 %collective-permute-start.9 = (f32[64,1024]{1,0:T(8,128)S(1)}, f32[64,1024]{1,0:T(8,128)S(1)}, u32[]{:S(2)}, u32[]{:S(2)}) collective-permute-start(f32[64,1024]{1,0:T(8,128)S(1)} %add.82), channel_id=1, source_target_pairs={{0,2},{1,3},{2,0},{3,1},{4,6},{5,7},{6,4},{7,5},{8,10},{9,11},{10,... | collective-permute-start | bytes 786440 | tf_op jit(solution)/shard_map/ppermute | solution.py:524
  125.2 8.9 %collective-permute-start.12 = (f32[2,256,128]{2,1,0:T(8,128)}, f32[2,256,128]{2,1,0:T(8,128)S(1)}, u32[]{:S(2)}, u32[]{:S(2)}) collective-permute-start(f32[2,256,128]{2,1,0:T(8,128)} %get-tuple-element.142), channel_id=1, source_target_pairs={{0,4},{4,0},{8,12},{12,8},{16,20},{20,16},{24,28},{28,24},{1,5},{5... | collective-permute-start | bytes 786440 | tf_op jit(solution)/shard_map/ppermute | solution.py:524
  136.9 9.3 %collective-permute-start.13 = (f32[2,256,128]{2,1,0:T(8,128)}, f32[2,256,128]{2,1,0:T(8,128)S(1)}, u32[]{:S(2)}, u32[]{:S(2)}) collective-permute-start(f32[2,256,128]{2,1,0:T(8,128)} %get-tuple-element.143.pair_ref), channel_id=1, source_target_pairs={{0,8},{4,12},{8,16},{12,20},{16,24},{20,28},{1,9},{5,13},{9,17},{1... | collective-permute-start | bytes 786440 | tf_op jit(solution)/shard_map/ppermute | solution.py:519
  268.1 21.5 %collective-permute-start.54 = (f32[128,1536]{1,0:T(8,128)}, f32[128,1536]{1,0:T(8,128)S(1)}, u32[]{:S(2)}, u32[]{:S(2)}) collective-permute-start(f32[128,1536]{1,0:T(8,128)} %get-tuple-element.216.b_ref), channel_id=1, source_target_pairs={{0,4},{4,0},{8,12},{12,8},{16,20},{20,16},{24,28},{28,24},{1,5},{5... | collective-permute-start | bytes 2359304 | tf_op jit(solution)/shard_map/ppermute | solution.py:524
  279.8 14.4 %collective-permute-start.53 = (f32[128,512]{1,0:T(8,128)S(1)}, f32[128,512]{1,0:T(8,128)S(1)}, u32[]{:S(2)}, u32[]{:S(2)}) collective-permute-start(f32[128,512]{1,0:T(8,128)S(1)} %copy-done.67), channel_id=1, source_target_pairs={{0,4},{4,0},{8,12},{12,8},{16,20},{20,16},{24,28},{28,24},{1,5},{5... | collective-permute-start | bytes 786440 | tf_op jit(solution)/shard_map/ppermute | solution.py:524
  299.0 271.0 %reduce-scatter.5.cloned.1.call-start = ((), (), s32[]{:S(2)}) async-start(), calls=%async_computation.4 | async-start | bytes 3932160 | tf_op jit(solution)/shard_map/reduce_scatter | solution.py:555
  324.7 13.2 %collective-permute-start.38 = (f32[2,128,128]{2,1,0:T(8,128)}, f32[2,128,128]{2,1,0:T(8,128)S(1)}, u32[]{:S(2)}, u32[]{:S(2)}) collective-permute-start(f32[2,128,128]{2,1,0:T(8,128)} %get-tuple-element.186.offset_ref), channel_id=1, source_target_pairs={{8,0},{12,4},{16,8},{20,12},{24,16},{28,20},{9,1},{13,5},{17,9},{2... | collective-permute-start | bytes 393224 | tf_op jit(solution)/shard_map/ppermute | solution.py:519
  340.5 15.7 %collective-permute-start.39 = (f32[2,128,128]{2,1,0:T(8,128)}, f32[2,128,128]{2,1,0:T(8,128)S(1)}, u32[]{:S(2)}, u32[]{:S(2)}) collective-permute-start(f32[2,128,128]{2,1,0:T(8,128)} %shard_map.239), channel_id=1, source_target_pairs={{8,0},{12,4},{16,8},{20,12},{24,16},{28,20},{9,1},{13,5},{17,9},{2... | collective-permute-start | bytes 393224 | tf_op jit(solution)/shard_map/ppermute | solution.py:519
  390.3 22.6 %collective-permute-start.52 = (f32[128,1536]{1,0:T(8,128)}, f32[128,1536]{1,0:T(8,128)S(1)}, u32[]{:S(2)}, u32[]{:S(2)}) collective-permute-start(f32[128,1536]{1,0:T(8,128)} %get-tuple-element.211.b_ref), channel_id=1, source_target_pairs={{0,4},{4,0},{8,12},{12,8},{16,20},{20,16},{24,28},{28,24},{1,5},{5... | collective-permute-start | bytes 2359304 | tf_op jit(solution)/shard_map/ppermute | solution.py:524
  392.7 20.3 %collective-permute-start.51 = (f32[128,512]{1,0:T(8,128)S(1)}, f32[128,512]{1,0:T(8,128)S(1)}, u32[]{:S(2)}, u32[]{:S(2)}) collective-permute-start(f32[128,512]{1,0:T(8,128)S(1)} %copy-done.65), channel_id=1, source_target_pairs={{0,4},{4,0},{8,12},{12,8},{16,20},{20,16},{24,28},{28,24},{1,5},{5... | collective-permute-start | bytes 786440 | tf_op jit(solution)/shard_map/ppermute | solution.py:524
  418.1 164.8 %reduce-scatter.11.cloned.1.call-start = ((), (), s32[]{:S(2)}) async-start(), calls=%async_computation.7 | async-start | bytes 6881280 | tf_op jit(solution)/shard_map/reduce_scatter | solution.py:555
  419.2 39.0 %collective-permute-start.60 = (f32[128,1920]{1,0:T(8,128)S(1)}, f32[128,1920]{1,0:T(8,128)S(1)}, u32[]{:S(2)}, u32[]{:S(2)}) collective-permute-start(f32[128,1920]{1,0:T(8,128)S(1)} %copy-done.14), channel_id=1, source_target_pairs={{0,4},{4,0},{8,12},{12,8},{16,20},{20,16},{24,28},{28,24},{1,5},{5... | collective-permute-start | bytes 2949128 | tf_op jit(solution)/shard_map/ppermute | solution.py:524
  421.2 36.0 %collective-permute-start.59 = (f32[128,1216]{0,1:T(8,128)S(1)}, f32[128,1216]{0,1:T(8,128)S(1)}, u32[]{:S(2)}, u32[]{:S(2)}) collective-permute-start(f32[128,1216]{0,1:T(8,128)S(1)} %copy.84), channel_id=1, source_target_pairs={{0,4},{4,0},{8,12},{12,8},{16,20},{20,16},{24,28},{28,24},{1,5},{5... | collective-permute-start | bytes 1867784 | tf_op jit(solution)/shard_map/ppermute | solution.py:524
  421.6 39.3 %collective-permute-start.62 = (f32[128,512]{1,0:T(8,128)S(1)}, f32[128,512]{1,0:T(8,128)}, u32[]{:S(2)}, u32[]{:S(2)}) collective-permute-start(f32[128,512]{1,0:T(8,128)S(1)} %copy-done.22), channel_id=1, source_target_pairs={{0,4},{4,0},{8,12},{12,8},{16,20},{20,16},{24,28},{28,24},{1,5},{5... | collective-permute-start | bytes 786440 | tf_op jit(solution)/shard_map/ppermute | solution.py:524
  423.3 40.4 %collective-permute-start.61 = (f32[128,512]{1,0:T(8,128)}, f32[128,512]{1,0:T(8,128)}, u32[]{:S(2)}, u32[]{:S(2)}) collective-permute-start(f32[128,512]{1,0:T(8,128)} %get-tuple-element.234), channel_id=1, source_target_pairs={{0,4},{4,0},{8,12},{12,8},{16,20},{20,16},{24,28},{28,24},{1,5},{5... | collective-permute-start | bytes 786440 | tf_op jit(solution)/shard_map/ppermute | solution.py:524
  470.0 213.5 %reduce-scatter.9.cloned.1.call-start = ((), (), s32[]{:S(2)}) async-start(), calls=%async_computation.6 | async-start | bytes 6881280 | tf_op jit(solution)/shard_map/reduce_scatter | solution.py:555
  471.2 39.0 %collective-permute-start.56 = (f32[128,1920]{1,0:T(8,128)S(1)}, f32[128,1920]{1,0:T(8,128)S(1)}, u32[]{:S(2)}, u32[]{:S(2)}) collective-permute-start(f32[128,1920]{1,0:T(8,128)S(1)} %copy-done.15), channel_id=1, source_target_pairs={{0,4},{4,0},{8,12},{12,8},{16,20},{20,16},{24,28},{28,24},{1,5},{5... | collective-permute-start | bytes 2949128 | tf_op jit(solution)/shard_map/ppermute | solution.py:524
  472.9 36.3 %collective-permute-start.55 = (f32[128,1216]{0,1:T(8,128)S(1)}, f32[128,1216]{0,1:T(8,128)S(1)}, u32[]{:S(2)}, u32[]{:S(2)}) collective-permute-start(f32[128,1216]{0,1:T(8,128)S(1)} %copy.82), channel_id=1, source_target_pairs={{0,4},{4,0},{8,12},{12,8},{16,20},{20,16},{24,28},{28,24},{1,5},{5... | collective-permute-start | bytes 1867784 | tf_op jit(solution)/shard_map/ppermute | solution.py:524
  473.5 38.5 %collective-permute-start.58 = (f32[128,512]{1,0:T(8,128)S(1)}, f32[128,512]{1,0:T(8,128)}, u32[]{:S(2)}, u32[]{:S(2)}) collective-permute-start(f32[128,512]{1,0:T(8,128)S(1)} %copy-done.20), channel_id=1, source_target_pairs={{0,4},{4,0},{8,12},{12,8},{16,20},{20,16},{24,28},{28,24},{1,5},{5... | collective-permute-start | bytes 786440 | tf_op jit(solution)/shard_map/ppermute | solution.py:524
  475.0 39.9 %collective-permute-start.57 = (f32[128,512]{1,0:T(8,128)}, f32[128,512]{1,0:T(8,128)}, u32[]{:S(2)}, u32[]{:S(2)}) collective-permute-start(f32[128,512]{1,0:T(8,128)} %get-tuple-element.227), channel_id=1, source_target_pairs={{0,4},{4,0},{8,12},{12,8},{16,20},{20,16},{24,28},{28,24},{1,5},{5... | collective-permute-start | bytes 786440 | tf_op jit(solution)/shard_map/ppermute | solution.py:524
  532.3 30.0 %collective-permute-start.21 = (f32[64,1024]{1,0:T(8,128)S(1)}, f32[64,1024]{1,0:T(8,128)S(1)}, u32[]{:S(2)}, u32[]{:S(2)}) collective-permute-start(f32[64,1024]{1,0:T(8,128)S(1)} %add.87.near_ref), channel_id=1, source_target_pairs={{0,1},{1,0},{2,3},{3,2},{4,5},{5,4},{6,7},{7,6},{8,9},{9,8},{10,11... | collective-permute-start | bytes 786440 | tf_op jit(solution)/shard_map/ppermute | solution.py:524
  532.5 8.8 %collective-permute-start.44 = (f32[64,1024]{1,0:T(8,128)S(1)}, f32[64,1024]{1,0:T(8,128)S(1)}, u32[]{:S(2)}, u32[]{:S(2)}) collective-permute-start(f32[64,1024]{1,0:T(8,128)S(1)} %add.94), channel_id=1, source_target_pairs={{0,2},{1,3},{2,0},{3,1},{4,6},{5,7},{6,4},{7,5},{8,10},{9,11},{10,... | collective-permute-start | bytes 786440 | tf_op jit(solution)/shard_map/ppermute | solution.py:524
  557.9 9.5 %collective-permute-start.50 = (f32[1,12800]{1,0:T(1,128)S(1)}, f32[1,12800]{1,0:T(1,128)S(1)}, u32[]{:S(2)}, u32[]{:S(2)}) collective-permute-start(f32[1,12800]{1,0:T(1,128)S(1)} %add.99), channel_id=1, source_target_pairs={{0,16},{4,20},{8,24},{12,28},{16,0},{20,4},{24,8},{28,12},{1,17},{... | collective-permute-start | bytes 153608 | tf_op jit(solution)/shard_map/ppermute | solution.py:524
  (113 other events, 500.0 us)
Sparse Core Ops, SparseCore 0:
  299.2 68.4 reduce-scatter.6
  418.2 62.1 reduce-scatter.4
  482.7 100.1 reduce-scatter.10
  585.0 98.4 reduce-scatter.8
